TPU v7x, 32 devices: a whole 2x2x4 slice. The times are simulated.
32 devices in a mesh: section: 16 (over z, y, x), replica: 2 (over core).
Axes of the slice: x: 2, y: 2, z: 4, core: 2. Of those that a mesh axis runs over, the one named last changes fastest.
Arguments:
- features: bfloat16 [16384, 256], P(('section', 'replica')), may hold values from -6 to 6
- adj_tiles: bfloat16 [4096, 128, 128], P(('section', 'replica')), may hold values from 0.0029907227 to 0.039794922
- tile_index: int32 [4096, 2], P(('section', 'replica')), may hold values from -1 to 7, as said below
- weight: bfloat16 [256, 256], replicated, may hold values from -0.375 to 0.375
- bias_vec: float32 [256], replicated, may hold values from -4 to 4
- grad_out: bfloat16 [16384, 256], P(('section', 'replica'))
Outputs:
- output: bfloat16 [16384, 256], P(('section', 'replica'))
- grad_weight: float32 [256, 256], replicated
- grad_bias: float32 [256], replicated
Inputs may be any that keep to these rules, and one draw needn't show every extreme that they name: `tile_index`: entry [k, 0] is a row block within the slab, or -1 for an empty slot; entry [k, 1] is a column block within the column section's slab, 0 in empty slots. Within each group of 16 slots the live slots come first and their (row, column) pairs are distinct; every group has a live slot, and some group is full.
All inputs are finite; a program needn't handle non-finite values.
Results may differ from a plain program's by a relative error of at most 0.0051.
Values may be sent and summed in bfloat16 or wider, within the bound.
No kernel may reach another device: no remote copies, remote signals or barrier semaphores. Data moves between devices by JAX's collectives and lax.ppermute only.
A program may use at most 64 MiB of HBM per device.

v0:
```python
import functools

import jax
import jax.numpy as jnp
from jax import lax
from jax.experimental import pallas as pl
from jax.experimental.pallas import tpu as pltpu
from jax.sharding import PartitionSpec as P

BOTH = ("section", "replica")
VMEM = pltpu.VMEM
SMEM = pltpu.SMEM


def spread(x, axis, root):
    mine = lax.axis_index(axis) == root
    return lax.psum(jnp.where(mine, x, jnp.zeros_like(x)), axis)


def add_tiles(summed, received, adj_tiles, row_ids, col_ids, first_slot, count, levels):
    tile_part = lax.dynamic_slice_in_dim(adj_tiles, first_slot, count, 0)
    row_pick = lax.dynamic_slice_in_dim(row_ids, first_slot, count, 0)
    col_pick = lax.dynamic_slice_in_dim(col_ids, first_slot, count, 0)
    picked = received[col_pick]
    products = jnp.einsum("kab,kbd->kad", tile_part, picked, preferred_element_type=jnp.float32)
    onehot = (row_pick[:, None] == levels[None, :]).astype(jnp.float32)
    return summed + jnp.einsum("kr,kad->rad", onehot, products, precision=lax.Precision.HIGHEST)


def general_shards(features, adj_tiles, tile_index, weight, bias_vec, grad_out):
    replicas = lax.axis_size("replica")
    replica_idx = lax.axis_index("replica")
    own_slab = lax.all_gather(features, "replica", axis=0, tiled=True)
    rows_slab, feat_width = own_slab.shape
    block_size = adj_tiles.shape[1]
    row_blocks = rows_slab // block_size
    turn_count = lax.axis_size("section") // replicas
    slot_count = adj_tiles.shape[0] // turn_count
    row_ids = tile_index[:, 0]
    col_ids = tile_index[:, 1]
    levels = jnp.arange(row_blocks, dtype=jnp.int32)

    def turn_step(step_idx, summed):
        received = spread(own_slab, "section", replica_idx * turn_count + step_idx)
        received = received.reshape(row_blocks, block_size, feat_width)
        first_slot = step_idx * slot_count
        return add_tiles(
            summed, received, adj_tiles, row_ids, col_ids, first_slot, slot_count, levels
        )

    start_sum = jnp.zeros((row_blocks, block_size, feat_width), jnp.float32)
    partial_sum = lax.fori_loop(0, turn_count, turn_step, start_sum).reshape(rows_slab, feat_width)
    share = rows_slab // replicas
    whole_sum = lax.psum(partial_sum, "replica")
    local_rows = lax.dynamic_slice_in_dim(whole_sum, replica_idx * share, share, 0)
    hidden = local_rows.astype(jnp.bfloat16)
    pre_act = jnp.dot(hidden, weight, preferred_element_type=jnp.float32) + bias_vec
    output = jax.nn.silu(pre_act).astype(jnp.bfloat16)
    sigma = jax.nn.sigmoid(pre_act)
    grad_pre = grad_out.astype(jnp.float32) * sigma * (1.0 + pre_act * (1.0 - sigma))
    grad_low = grad_pre.astype(jnp.bfloat16)
    weight_term = jnp.einsum("nd,ne->de", hidden, grad_low, preferred_element_type=jnp.float32)
    grad_weight, grad_bias = lax.psum((weight_term, jnp.sum(grad_pre, axis=0)), BOTH)
    return (output, grad_weight, grad_bias)


def send(x, target, name):
    perm = [(2 * p + c, 2 * target(p, c) + c) for p in range(16) for c in range(2)]
    with jax.named_scope(name):
        return lax.ppermute(x, BOTH, perm)


def swap(x, name):
    with jax.named_scope(name):
        return lax.ppermute(x, "replica", [(0, 1), (1, 0)])


def first_hop(x, name):
    return send(x, lambda p, c: p ^ (1 if c == 0 else 2), name)


def second_hop(x, name):
    return send(x, lambda p, c: p ^ (2 if c == 0 else 1), name)


def diagonal(x, name):
    return send(x, lambda p, c: p ^ 3, name)


def along_z(x, k, name):
    return send(x, lambda p, c: p ^ (4 * k), name)


def join(own, near):
    return jnp.concatenate([own, near], axis=0)


def after(*arrays):
    return lax.optimization_barrier(arrays)


def work_list(index, slots, row_blocks):
    chip = lax.axis_index("section")
    core = lax.axis_index("replica")
    half = row_blocks // 2
    count = index.shape[0] // 2
    tile = jnp.arange(2 * count, dtype=jnp.int32)
    source = tile // slots
    row, col = index[:, 0], index[:, 1]
    live = (row >= 0) & (col // half == core)
    apart = source ^ chip
    x_apart, y_apart, z_apart = apart & 1, (apart >> 1) & 1, apart >> 2
    near = jnp.where(core == 0, x_apart, y_apart)
    far = jnp.where(core == 0, y_apart, x_apart)
    groups = 8
    group = jnp.where(live, 2 * z_apart + far, groups)
    block = half * near + col % half
    mine = tile // count == core
    entry = (tile % count + jnp.where(mine, 0, count)) | (block << 8) | ((row ^ (half * core)) << 12)
    spare = row_blocks << 12
    sizes = jnp.sum((group[:, None] == jnp.arange(groups)[None, :]).astype(jnp.int32), axis=0)
    padded = (sizes + 1) // 2 * 2
    edge = jnp.arange(groups + 1)
    starts = jnp.sum(jnp.where(edge[None, :groups] < edge[:, None], padded[None, :], 0), axis=1)
    same = (group[:, None] == group[None, :]) & (tile[None, :] < tile[:, None])
    rank = jnp.sum(same.astype(jnp.int32), axis=1)
    base = jnp.sum(jnp.where(group[:, None] == edge[None, :groups], starts[None, :groups], 0), axis=1)
    place = jnp.where(live, base + rank, -1)
    length = 2 * count + 2 * groups
    hit = place[None, :] == jnp.arange(length, dtype=jnp.int32)[:, None]
    entries = spare + jnp.sum(jnp.where(hit, (entry - spare)[None, :], 0), axis=1)
    return entries, starts


def gather_kernel(count, entries, starts, own, other, out, sem):
    total = starts[8]

    def begin(m, carry):
        tile = entries[m] & 255

        @pl.when(tile < count)
        def _():
            pltpu.make_async_copy(own.at[tile], out.at[m], sem).start()

        @pl.when(tile >= count)
        def _():
            pltpu.make_async_copy(other.at[tile - count], out.at[m], sem).start()

        return carry

    def finish(m, carry):
        pltpu.make_async_copy(own.at[0], out.at[0], sem).wait()
        return carry

    lax.fori_loop(0, total, begin, 0)
    lax.fori_loop(0, total, finish, 0)


def gather_tiles(entries, starts, own, other):
    size = own.shape[1]
    return pl.pallas_call(
        functools.partial(gather_kernel, own.shape[0]),
        out_shape=VMEM((entries.shape[0], size, size), own.dtype),
        in_specs=[pl.BlockSpec(memory_space=SMEM)] * 2 + [pl.BlockSpec(memory_space=pltpu.HBM)] * 2,
        out_specs=pl.BlockSpec(memory_space=VMEM),
        scratch_shapes=[pltpu.SemaphoreType.DMA],
        name="gather_tiles",
        compiler_params=pltpu.CompilerParams(vmem_limit_bytes=1 << 20),
        cost_estimate=pl.CostEstimate(flops=4000000000, bytes_accessed=10000000, transcendentals=0),
    )(entries, starts, own, other)


def add_group(entries, lo, hi, tiles, blocks, acc):
    def step(j, carry):
        m = lo + 2 * j
        e0, e1 = entries[m], entries[m + 1]

        def product(e, m):
            at = pl.multiple_of(((e >> 8) & 15) * 128, 128)
            return jnp.dot(
                tiles[m], blocks[pl.ds(at, 128), :], preferred_element_type=jnp.float32
            )

        p0, p1 = product(e0, m), product(e1, m + 1)
        acc[e0 >> 12] += p0
        acc[e1 >> 12] += p1
        return carry

    lax.fori_loop(0, (hi - lo) // 2, step, 0)


def add_kernel(groups, fresh, entries, starts, tiles, *refs):
    arrays, acc = refs[: len(groups)], refs[-1]
    if fresh:
        acc[...] = jnp.zeros_like(acc)
    for g, array in zip(groups, arrays):
        add_group(entries, starts[g], starts[g + 1], tiles, array, acc)


def late_kernel(groups, entries, starts, tiles, *refs):
    arrays, (acc, keep, give) = refs[: len(groups)], refs[len(groups) + 1 :]
    for g, array in zip(groups, arrays):
        add_group(entries, starts[g], starts[g + 1], tiles, array, acc)
    half = keep.shape[0]
    keep[...] = acc[:half]
    give[...] = acc[half : 2 * half]


def whole(space):
    return pl.BlockSpec(memory_space=space)


def add_groups(work, arrays, groups, acc, row_blocks, name, cost=4000000000):
    entries, starts, tiles = work
    shape = VMEM((row_blocks + 1, 128, arrays[0].shape[1]), jnp.float32)
    fresh = acc is None
    return pl.pallas_call(
        functools.partial(add_kernel, groups, fresh),
        out_shape=shape,
        in_specs=[whole(SMEM)] * 2 + [whole(VMEM)] * (1 + len(arrays) + (not fresh)),
        out_specs=whole(VMEM),
        name=name,
        input_output_aliases={} if fresh else {3 + len(arrays): 0},
        compiler_params=pltpu.CompilerParams(vmem_limit_bytes=4 << 20),
        cost_estimate=pl.CostEstimate(flops=cost, bytes_accessed=cost // 400, transcendentals=0),
    )(entries, starts, tiles, *arrays, *([] if fresh else [acc]))


def add_late(work, arrays, groups, acc, row_blocks):
    entries, starts, tiles = work
    half = VMEM((row_blocks // 2, 128, arrays[0].shape[1]), jnp.float32)
    return pl.pallas_call(
        functools.partial(late_kernel, groups),
        out_shape=(VMEM(acc.shape, jnp.float32), half, half),
        in_specs=[whole(SMEM)] * 2 + [whole(VMEM)] * (2 + len(arrays)),
        out_specs=(whole(VMEM),) * 3,
        name="add_late",
        input_output_aliases={3 + len(arrays): 0},
        compiler_params=pltpu.CompilerParams(vmem_limit_bytes=4 << 20),
        cost_estimate=pl.CostEstimate(flops=1 << 25, bytes_accessed=2 << 20, transcendentals=0),
    )(entries, starts, tiles, *arrays, acc)[1:]


def dense_kernel(core, mine, theirs, weight, bias, grad_out, output, keep, give, full):
    hidden = (mine[...] + theirs[...]).reshape(grad_out.shape).astype(jnp.bfloat16)
    pre_act = jnp.dot(hidden, weight[...], preferred_element_type=jnp.float32) + bias[...]
    sigma = 1.0 / (1.0 + jnp.exp(-pre_act))
    output[...] = (pre_act * sigma).astype(jnp.bfloat16)
    grad_pre = grad_out[...].astype(jnp.float32) * sigma * (1.0 + pre_act * (1.0 - sigma))
    grad_low = grad_pre.astype(jnp.bfloat16)
    full[...] = lax.dot_general(
        hidden, grad_low, (((0,), (0,)), ((), ())), preferred_element_type=jnp.float32
    )
    sums = jnp.sum(grad_pre, axis=0, keepdims=True)
    sums = jnp.broadcast_to(sums, (8, sums.shape[1]))
    share = full.shape[0] // 2
    at = core[0]
    keep[:share] = full[pl.ds(pl.multiple_of(at * share, share), share), :]
    give[:share] = full[pl.ds(pl.multiple_of((1 - at) * share, share), share), :]
    keep[share:] = sums
    give[share:] = sums


def dense(core, mine, theirs, weight, bias, grad_out):
    width = weight.shape[0]
    part = VMEM((width // 2 + 8, width), jnp.float32)
    return pl.pallas_call(
        dense_kernel,
        out_shape=(jax.ShapeDtypeStruct(grad_out.shape, jnp.bfloat16), part, part),
        in_specs=[whole(SMEM)] + [whole(VMEM)] * 5,
        out_specs=(whole(VMEM),) * 3,
        scratch_shapes=[VMEM((width, width), jnp.float32)],
        name="dense",
        compiler_params=pltpu.CompilerParams(vmem_limit_bytes=16 << 20),
        cost_estimate=pl.CostEstimate(
            flops=1 << 27, bytes_accessed=2 << 20, transcendentals=1 << 17
        ),
    )(core.reshape(1), mine, theirs, weight, bias.reshape(1, width), grad_out)


def shards(features, adj_tiles, tile_index, weight, bias_vec, grad_out):
    core = lax.axis_index("replica")
    row_blocks = 2 * features.shape[0] // adj_tiles.shape[1]
    slots = adj_tiles.shape[0] // 8

    index = lax.all_gather(tile_index, "replica", axis=0, tiled=True)
    z1 = along_z(features, 1, "z1")
    z2 = along_z(features, 2, "z2")
    r0 = first_hop(features, "r0")
    pair0 = join(features, r0)
    q0 = second_hop(pair0, "q0")
    again = features
    tiles_in = adj_tiles
    z1, again = after(z1, features)
    z3 = along_z(again, 3, "z3")
    other_tiles = swap(tiles_in, "tiles")
    entries, starts = work_list(index, slots, row_blocks)
    tiles = gather_tiles(entries, starts, adj_tiles, other_tiles)
    pair1 = join(z1, first_hop(z1, "r1"))
    q1 = second_hop(pair1, "q1")
    pair2 = join(z2, first_hop(z2, "r2"))
    q2 = second_hop(pair2, "q2")
    work = (entries, starts, tiles)
    acc = add_groups(work, (pair0, q0, pair1), (0, 1, 2), None, row_blocks, "add_a")
    pair3 = join(z3, first_hop(z3, "r3"))
    q3 = second_hop(pair3, "q3")
    acc = add_groups(work, (q1, pair2), (3, 4), acc, row_blocks, "add_b")
    acc = add_groups(work, (q2, pair3), (5, 6), acc, row_blocks, "add_c")
    mine, give = add_late(work, (q3,), (7,), acc, row_blocks)
    theirs = swap(give, "rows")
    output, keep, give = dense(core, mine, theirs, weight, bias_vec, grad_out)
    part = keep + swap(give, "halves")
    part = part + first_hop(part, "sum1")
    part = part + second_hop(part, "sum2")
    low_part = part.astype(jnp.bfloat16)
    z_parts = [lax.reduce_precision(part, 8, 7)]
    z_parts += [along_z(low_part, k, f"sum{2 + k}").astype(jnp.float32) for k in (1, 2, 3)]
    part = (z_parts[0] + z_parts[1]) + (z_parts[2] + z_parts[3])
    rest = swap(part, "back")
    share = part.shape[0] - 8
    top = jnp.where(core == 0, part, rest)
    low = jnp.where(core == 0, rest, part)
    grad_weight = jnp.concatenate([top[:share], low[:share]], axis=0)
    return output, grad_weight, top[share]


def solution(mesh):
    placed = (
        P(BOTH, None),
        P(BOTH, None, None),
        P(BOTH, None),
        P(),
        P(),
        P(BOTH, None),
    )
    small = mesh.shape["section"] == 16 and mesh.shape["replica"] == 2
    return jax.shard_map(
        shards if small else general_shards,
        mesh=mesh,
        in_specs=placed,
        out_specs=(P(BOTH, None), P(), P()),
        check_vma=False,
    )
```

profile of v0, /device:TPU:0, one launch (start us, length us, event | category | flops | bytes accessed | tf_op | source)
XLA Modules:
  0.0 80.6 jit_solution(10787007971246047622)
XLA Ops:
  1.1 2.7 %collective-permute-start.1 = (bf16[512,256]{1,0:T(8,128)(2,1)}, bf16[512,256]{1,0:T(8,128)(2,1)S(1)}, u32[]{:S(2)}, u32[]{:S(2)}) collective-permute-start(bf16[512,256]{1,0:T(8,128)(2,1)} %param.6), channel_id=1, source_target_pairs={{0,8},{1,9},{2,10},{3,11},{4,12},{5,13},{6,14},{7,15},{8,0},{9,1},... | collective-permute-start | bytes 786440 | tf_op jit(solution)/shard_map/z1/ppermute | solution.py:70
  3.8 1.5 %collective-permute-start.10 = (bf16[512,256]{1,0:T(8,128)(2,1)}, bf16[512,256]{1,0:T(8,128)(2,1)S(1)}, u32[]{:S(2)}, u32[]{:S(2)}) collective-permute-start(bf16[512,256]{1,0:T(8,128)(2,1)} %param.6), channel_id=1, source_target_pairs={{0,2},{1,5},{2,0},{3,7},{4,6},{5,1},{6,4},{7,3},{8,10},{9,13},{10,... | collective-permute-start | bytes 786440 | tf_op jit(solution)/shard_map/r0/ppermute | solution.py:70
  5.3 2.6 %collective-permute-start.5 = (bf16[512,256]{1,0:T(8,128)(2,1)}, bf16[512,256]{1,0:T(8,128)(2,1)S(1)}, u32[]{:S(2)}, u32[]{:S(2)}) collective-permute-start(bf16[512,256]{1,0:T(8,128)(2,1)} %param.6), channel_id=1, source_target_pairs={{0,16},{1,17},{2,18},{3,19},{4,20},{5,21},{6,22},{7,23},{8,24},{9,... | collective-permute-start | bytes 786440 | tf_op jit(solution)/shard_map/z2/ppermute | solution.py:70
  7.9 2.0 %all_gather.3 = s32[256,2]{0,1:T(2,128)S(1)} all-gather(s32[128,2]{0,1:T(2,128)} %param.8), channel_id=1, replica_groups=mesh['section'=16,'replica'=2] {'replica'}, dimensions={0}, use_global_device_ids=true | all-gather | bytes 3072 | tf_op jit(solution)/shard_map/all_gather | solution.py:286
  11.7 3.4 %collective-permute-done.1 = bf16[512,256]{1,0:T(8,128)(2,1)S(1)} collective-permute-done((bf16[512,256]{1,0:T(8,128)(2,1)}, bf16[512,256]{1,0:T(8,128)(2,1)S(1)}, u32[]{:S(2)}, u32[]{:S(2)}) %collective-permute-start.1) | collective-permute-done | bytes 262176 | tf_op jit(solution)/shard_map/z1/ppermute | solution.py:70
  15.2 1.7 %collective-permute-start.8 = (bf16[512,256]{1,0:T(8,128)(2,1)S(1)}, bf16[512,256]{1,0:T(8,128)(2,1)S(1)}, u32[]{:S(2)}, u32[]{:S(2)}) collective-permute-start(bf16[512,256]{1,0:T(8,128)(2,1)S(1)} %collective-permute-done.1), channel_id=1, source_target_pairs={{0,2},{1,5},{2,0},{3,7},{4,6},{5,1},{6,4},{7,3},{8,10},{9,13},{10,... | collective-permute-start | bytes 786440 | tf_op jit(solution)/shard_map/r1/ppermute | solution.py:70
  16.8 2.5 %collective-permute-start.2 = (bf16[512,256]{1,0:T(8,128)(2,1)}, bf16[512,256]{1,0:T(8,128)(2,1)S(1)}, u32[]{:S(2)}, u32[]{:S(2)}) collective-permute-start(bf16[512,256]{1,0:T(8,128)(2,1)} %param.6), channel_id=1, source_target_pairs={{0,24},{1,25},{2,26},{3,27},{4,28},{5,29},{6,30},{7,31},{8,16},{9,... | collective-permute-start | bytes 786440 | tf_op jit(solution)/shard_map/z3/ppermute | solution.py:70
  19.3 1.9 %collective-permute-done.5 = bf16[512,256]{1,0:T(8,128)(2,1)S(1)} collective-permute-done((bf16[512,256]{1,0:T(8,128)(2,1)}, bf16[512,256]{1,0:T(8,128)(2,1)S(1)}, u32[]{:S(2)}, u32[]{:S(2)}) %collective-permute-start.5) | collective-permute-done | bytes 262176 | tf_op jit(solution)/shard_map/z2/ppermute | solution.py:70
  22.6 5.0 %collective-permute-done.2 = bf16[512,256]{1,0:T(8,128)(2,1)S(1)} collective-permute-done((bf16[512,256]{1,0:T(8,128)(2,1)}, bf16[512,256]{1,0:T(8,128)(2,1)S(1)}, u32[]{:S(2)}, u32[]{:S(2)}) %collective-permute-start.2) | collective-permute-done | bytes 262176 | tf_op jit(solution)/shard_map/z3/ppermute | solution.py:70
  28.0 1.5 %collective-permute-start.9 = (bf16[1024,256]{1,0:T(8,128)(2,1)S(1)}, bf16[1024,256]{1,0:T(8,128)(2,1)S(1)}, u32[]{:S(2)}, u32[]{:S(2)}) collective-permute-start(bf16[1024,256]{1,0:T(8,128)(2,1)S(1)} %constant_dynamic-update-slice_fusion.4.refs_2_), channel_id=1, source_target_pairs={{0,4},{1,3},{2,6},{3,1},{4,0},{5,7},{6,2},{7,5},{8,12},{9,11},{10,... | collective-permute-start | bytes 1572872 | tf_op jit(solution)/shard_map/q1/ppermute | solution.py:70
  31.2 5.6 %collective-permute-done.3 = bf16[512,256]{1,0:T(8,128)(2,1)S(1)} collective-permute-done((bf16[512,256]{1,0:T(8,128)(2,1)S(1)}, bf16[512,256]{1,0:T(8,128)(2,1)S(1)}, u32[]{:S(2)}, u32[]{:S(2)}) %collective-permute-start.3) | collective-permute-done | bytes 262176 | tf_op jit(solution)/shard_map/r3/ppermute | solution.py:70
  37.2 3.5 %gather_tiles.1.tiles = bf16[272,128,128]{2,1,0:T(8,128)(2,1)S(1)} custom-call(s32[272]{0:T(512)S(1)} %broadcast_add_fusion.entries, s32[9]{0:T(128)S(1)} %select_reduce_fusion.2.starts, bf16[128,128,128]{2,1,0:T(8,128)(2,1)S(1)} %copy-done, bf16[128,128,128]{2,1,0:T(8,128)(2,1)} %collective-permute-done.other), custom_call_target="tpu_custom_call" | custom-call | flops 4000000000 | bytes 10000000 | tf_op jit(solution)/shard_map/gather_tiles/pallas_call | solution.py:161
  40.7 2.9 %add_a.1.refs_2_ = f32[9,128,256]{2,1,0:T(8,128)S(1)} custom-call(s32[272]{0:T(512)S(1)} %broadcast_add_fusion.entries, s32[9]{0:T(128)S(1)} %select_reduce_fusion.2.starts, bf16[272,128,128]{2,1,0:T(8,128)(2,1)S(1)} %gather_tiles.1.tiles, bf16[1024,256]{1,0:T(8,128)(2,1)S(1)} %constant_dynamic-update-slice_fusion.6.refs_0_, ...), custom_call_target="tpu_custom_call" | custom-call | flops 4000000000 | bytes 10000000 | tf_op jit(solution)/shard_map/add_a/pallas_call | solution.py:217
  43.7 1.7 %add_b.1.refs_2_ = f32[9,128,256]{2,1,0:T(8,128)S(1)} custom-call(s32[272]{0:T(512)S(1)} %broadcast_add_fusion.entries, s32[9]{0:T(128)S(1)} %select_reduce_fusion.2.starts, bf16[272,128,128]{2,1,0:T(8,128)(2,1)S(1)} %gather_tiles.1.tiles, bf16[1024,256]{1,0:T(8,128)(2,1)S(1)} %collective-permute-done.9.refs_0_, ...), custom_call_target="tpu_custom_call", output_to_operand_aliasing={{}: (5, {})} | custom-call | flops 4000000000 | bytes 10000000 | tf_op jit(solution)/shard_map/add_b/pallas_call | solution.py:217
  45.4 2.1 %add_c.1.refs_1_ = f32[9,128,256]{2,1,0:T(8,128)S(1)} custom-call(s32[272]{0:T(512)S(1)} %broadcast_add_fusion.entries, s32[9]{0:T(128)S(1)} %select_reduce_fusion.2.starts, bf16[272,128,128]{2,1,0:T(8,128)(2,1)S(1)} %gather_tiles.1.tiles, bf16[1024,256]{1,0:T(8,128)(2,1)S(1)} %collective-permute-done.7.refs_0_, ...), custom_call_target="tpu_custom_call", output_to_operand_aliasing={{}: (5, {})} | custom-call | flops 4000000000 | bytes 10000000 | tf_op jit(solution)/shard_map/add_c/pallas_call | solution.py:217
  47.5 3.2 %collective-permute-done.4.refs_0_ = bf16[1024,256]{1,0:T(8,128)(2,1)S(1)} collective-permute-done((bf16[1024,256]{1,0:T(8,128)(2,1)S(1)}, bf16[1024,256]{1,0:T(8,128)(2,1)S(1)}, u32[]{:S(2)}, u32[]{:S(2)}) %collective-permute-start.4) | collective-permute-done | bytes 524320 | tf_op jit(solution)/shard_map/q3/ppermute | solution.py:70
  52.0 1.9 %collective-permute-done.12.theirs = f32[4,128,256]{2,1,0:T(8,128)S(1)} collective-permute-done((f32[4,128,256]{2,1,0:T(8,128)S(1)}, f32[4,128,256]{2,1,0:T(8,128)S(1)}, u32[]{:S(2)}, u32[]{:S(2)}) %collective-permute-start.12) | collective-permute-done | bytes 524320 | tf_op jit(solution)/shard_map/rows/ppermute | solution.py:75
  56.4 2.1 %collective-permute-start.14 = (f32[136,256]{1,0:T(8,128)S(1)}, f32[136,256]{1,0:T(8,128)S(1)}, u32[]{:S(2)}, u32[]{:S(2)}) collective-permute-start(f32[136,256]{1,0:T(8,128)S(1)} %add.135), channel_id=1, source_target_pairs={{0,2},{1,5},{2,0},{3,7},{4,6},{5,1},{6,4},{7,3},{8,10},{9,13},{10,... | collective-permute-start | bytes 417800 | tf_op jit(solution)/shard_map/sum1/ppermute | solution.py:70
  58.6 3.0 %collective-permute-done.14 = f32[136,256]{1,0:T(8,128)S(1)} collective-permute-done((f32[136,256]{1,0:T(8,128)S(1)}, f32[136,256]{1,0:T(8,128)S(1)}, u32[]{:S(2)}, u32[]{:S(2)}) %collective-permute-start.14) | collective-permute-done | bytes 139296 | tf_op jit(solution)/shard_map/sum1/ppermute | solution.py:70
  62.7 4.0 %collective-permute-done.15 = f32[136,256]{1,0:T(8,128)S(1)} collective-permute-done((f32[136,256]{1,0:T(8,128)S(1)}, f32[136,256]{1,0:T(8,128)S(1)}, u32[]{:S(2)}, u32[]{:S(2)}) %collective-permute-start.15) | collective-permute-done | bytes 139296 | tf_op jit(solution)/shard_map/sum2/ppermute | solution.py:70
  66.8 3.2 %collective-permute-start.16 = (bf16[136,256]{1,0:T(8,128)(2,1)S(1)}, bf16[136,256]{1,0:T(8,128)(2,1)S(1)}, u32[]{:S(2)}, u32[]{:S(2)}) collective-permute-start(bf16[136,256]{1,0:T(8,128)(2,1)S(1)} %add_convert_fusion), channel_id=1, source_target_pairs={{0,8},{1,9},{2,10},{3,11},{4,12},{5,13},{6,14},{7,15},{8,0},{9,1},... | collective-permute-start | bytes 208904 | tf_op jit(solution)/shard_map/sum3/ppermute | solution.py:70
  70.0 1.5 %collective-permute-start.17 = (bf16[136,256]{1,0:T(8,128)(2,1)S(1)}, bf16[136,256]{1,0:T(8,128)(2,1)S(1)}, u32[]{:S(2)}, u32[]{:S(2)}) collective-permute-start(bf16[136,256]{1,0:T(8,128)(2,1)S(1)} %add_convert_fusion), channel_id=1, source_target_pairs={{0,16},{1,17},{2,18},{3,19},{4,20},{5,21},{6,22},{7,23},{8,24},{9,... | collective-permute-start | bytes 208904 | tf_op jit(solution)/shard_map/sum4/ppermute | solution.py:70
  71.5 1.4 %collective-permute-start.18 = (bf16[136,256]{1,0:T(8,128)(2,1)S(1)}, bf16[136,256]{1,0:T(8,128)(2,1)S(1)}, u32[]{:S(2)}, u32[]{:S(2)}) collective-permute-start(bf16[136,256]{1,0:T(8,128)(2,1)S(1)} %add_convert_fusion), channel_id=1, source_target_pairs={{0,24},{1,25},{2,26},{3,27},{4,28},{5,29},{6,30},{7,31},{8,16},{9,... | collective-permute-start | bytes 208904 | tf_op jit(solution)/shard_map/sum5/ppermute | solution.py:70
  72.9 3.4 %collective-permute-done.17 = bf16[136,256]{1,0:T(8,128)(2,1)S(1)} collective-permute-done((bf16[136,256]{1,0:T(8,128)(2,1)S(1)}, bf16[136,256]{1,0:T(8,128)(2,1)S(1)}, u32[]{:S(2)}, u32[]{:S(2)}) %collective-permute-start.17) | collective-permute-done | bytes 69664 | tf_op jit(solution)/shard_map/sum4/ppermute | solution.py:70
  (60 shorter events, 15.4 us)
Async XLA Ops:
  0.6 36.6 %collective-permute-start = (bf16[128,128,128]{2,1,0:T(8,128)(2,1)}, bf16[128,128,128]{2,1,0:T(8,128)(2,1)}, u32[]{:S(2)}, u32[]{:S(2)}) collective-permute-start(bf16[128,128,128]{2,1,0:T(8,128)(2,1)} %own.1), channel_id=1, source_target_pairs={{0,1},{1,0},{2,3},{3,2},{4,5},{5,4},{6,7},{7,6},{8,9},{9,8},{10,11... | collective-permute-start | bytes 12582920 | tf_op jit(solution)/shard_map/tiles/ppermute | solution.py:75
  1.1 14.0 %collective-permute-start.1 = (bf16[512,256]{1,0:T(8,128)(2,1)}, bf16[512,256]{1,0:T(8,128)(2,1)S(1)}, u32[]{:S(2)}, u32[]{:S(2)}) collective-permute-start(bf16[512,256]{1,0:T(8,128)(2,1)} %param.6), channel_id=1, source_target_pairs={{0,8},{1,9},{2,10},{3,11},{4,12},{5,13},{6,14},{7,15},{8,0},{9,1},... | collective-permute-start | bytes 786440 | tf_op jit(solution)/shard_map/z1/ppermute | solution.py:70
  3.8 18.0 %collective-permute-start.10 = (bf16[512,256]{1,0:T(8,128)(2,1)}, bf16[512,256]{1,0:T(8,128)(2,1)S(1)}, u32[]{:S(2)}, u32[]{:S(2)}) collective-permute-start(bf16[512,256]{1,0:T(8,128)(2,1)} %param.6), channel_id=1, source_target_pairs={{0,2},{1,5},{2,0},{3,7},{4,6},{5,1},{6,4},{7,3},{8,10},{9,13},{10,... | collective-permute-start | bytes 786440 | tf_op jit(solution)/shard_map/r0/ppermute | solution.py:70
  5.3 15.9 %collective-permute-start.5 = (bf16[512,256]{1,0:T(8,128)(2,1)}, bf16[512,256]{1,0:T(8,128)(2,1)S(1)}, u32[]{:S(2)}, u32[]{:S(2)}) collective-permute-start(bf16[512,256]{1,0:T(8,128)(2,1)} %param.6), channel_id=1, source_target_pairs={{0,16},{1,17},{2,18},{3,19},{4,20},{5,21},{6,22},{7,23},{8,24},{9,... | collective-permute-start | bytes 786440 | tf_op jit(solution)/shard_map/z2/ppermute | solution.py:70
  10.6 26.6 %copy-start = (bf16[128,128,128]{2,1,0:T(8,128)(2,1)S(1)}, bf16[128,128,128]{2,1,0:T(8,128)(2,1)}, u32[]{:S(2)}) copy-start(bf16[128,128,128]{2,1,0:T(8,128)(2,1)} %own.1) | copy-start | bytes 12582916
  15.2 12.8 %collective-permute-start.8 = (bf16[512,256]{1,0:T(8,128)(2,1)S(1)}, bf16[512,256]{1,0:T(8,128)(2,1)S(1)}, u32[]{:S(2)}, u32[]{:S(2)}) collective-permute-start(bf16[512,256]{1,0:T(8,128)(2,1)S(1)} %collective-permute-done.1), channel_id=1, source_target_pairs={{0,2},{1,5},{2,0},{3,7},{4,6},{5,1},{6,4},{7,3},{8,10},{9,13},{10,... | collective-permute-start | bytes 786440 | tf_op jit(solution)/shard_map/r1/ppermute | solution.py:70
  16.8 10.8 %collective-permute-start.2 = (bf16[512,256]{1,0:T(8,128)(2,1)}, bf16[512,256]{1,0:T(8,128)(2,1)S(1)}, u32[]{:S(2)}, u32[]{:S(2)}) collective-permute-start(bf16[512,256]{1,0:T(8,128)(2,1)} %param.6), channel_id=1, source_target_pairs={{0,24},{1,25},{2,26},{3,27},{4,28},{5,29},{6,30},{7,31},{8,16},{9,... | collective-permute-start | bytes 786440 | tf_op jit(solution)/shard_map/z3/ppermute | solution.py:70
  21.2 9.2 %collective-permute-start.6 = (bf16[512,256]{1,0:T(8,128)(2,1)S(1)}, bf16[512,256]{1,0:T(8,128)(2,1)S(1)}, u32[]{:S(2)}, u32[]{:S(2)}) collective-permute-start(bf16[512,256]{1,0:T(8,128)(2,1)S(1)} %collective-permute-done.5), channel_id=1, source_target_pairs={{0,2},{1,5},{2,0},{3,7},{4,6},{5,1},{6,4},{7,3},{8,10},{9,13},{10,... | collective-permute-start | bytes 786440 | tf_op jit(solution)/shard_map/r2/ppermute | solution.py:70
  21.8 18.9 %collective-permute-start.11 = (bf16[1024,256]{1,0:T(8,128)(2,1)S(1)}, bf16[1024,256]{1,0:T(8,128)(2,1)S(1)}, u32[]{:S(2)}, u32[]{:S(2)}) collective-permute-start(bf16[1024,256]{1,0:T(8,128)(2,1)S(1)} %constant_dynamic-update-slice_fusion.6.refs_0_), channel_id=1, source_target_pairs={{0,4},{1,3},{2,6},{3,1},{4,0},{5,7},{6,2},{7,5},{8,12},{9,11},{10,... | collective-permute-start | bytes 1572872 | tf_op jit(solution)/shard_map/q0/ppermute | solution.py:70
  27.6 9.2 %collective-permute-start.3 = (bf16[512,256]{1,0:T(8,128)(2,1)S(1)}, bf16[512,256]{1,0:T(8,128)(2,1)S(1)}, u32[]{:S(2)}, u32[]{:S(2)}) collective-permute-start(bf16[512,256]{1,0:T(8,128)(2,1)S(1)} %collective-permute-done.2), channel_id=1, source_target_pairs={{0,2},{1,5},{2,0},{3,7},{4,6},{5,1},{6,4},{7,3},{8,10},{9,13},{10,... | collective-permute-start | bytes 786440 | tf_op jit(solution)/shard_map/r3/ppermute | solution.py:70
  28.0 15.7 %collective-permute-start.9 = (bf16[1024,256]{1,0:T(8,128)(2,1)S(1)}, bf16[1024,256]{1,0:T(8,128)(2,1)S(1)}, u32[]{:S(2)}, u32[]{:S(2)}) collective-permute-start(bf16[1024,256]{1,0:T(8,128)(2,1)S(1)} %constant_dynamic-update-slice_fusion.4.refs_2_), channel_id=1, source_target_pairs={{0,4},{1,3},{2,6},{3,1},{4,0},{5,7},{6,2},{7,5},{8,12},{9,11},{10,... | collective-permute-start | bytes 1572872 | tf_op jit(solution)/shard_map/q1/ppermute | solution.py:70
  30.5 14.9 %collective-permute-start.7 = (bf16[1024,256]{1,0:T(8,128)(2,1)S(1)}, bf16[1024,256]{1,0:T(8,128)(2,1)S(1)}, u32[]{:S(2)}, u32[]{:S(2)}) collective-permute-start(bf16[1024,256]{1,0:T(8,128)(2,1)S(1)} %constant_dynamic-update-slice_fusion.2.refs_1_), channel_id=1, source_target_pairs={{0,4},{1,3},{2,6},{3,1},{4,0},{5,7},{6,2},{7,5},{8,12},{9,11},{10,... | collective-permute-start | bytes 1572872 | tf_op jit(solution)/shard_map/q2/ppermute | solution.py:70
  36.8 13.9 %collective-permute-start.4 = (bf16[1024,256]{1,0:T(8,128)(2,1)S(1)}, bf16[1024,256]{1,0:T(8,128)(2,1)S(1)}, u32[]{:S(2)}, u32[]{:S(2)}) collective-permute-start(bf16[1024,256]{1,0:T(8,128)(2,1)S(1)} %constant_dynamic-update-slice_fusion.refs_1_), channel_id=1, source_target_pairs={{0,4},{1,3},{2,6},{3,1},{4,0},{5,7},{6,2},{7,5},{8,12},{9,11},{10,... | collective-permute-start | bytes 1572872 | tf_op jit(solution)/shard_map/q3/ppermute | solution.py:70
  47.5 6.4 %copy-start.1 = (bf16[512,256]{1,0:T(8,128)(2,1)S(1)}, bf16[512,256]{1,0:T(8,128)(2,1)}, u32[]{:S(2)}) copy-start(bf16[512,256]{1,0:T(8,128)(2,1)} %grad_out.1) | copy-start | bytes 786436
  47.5 6.4 %copy-start.2 = (bf16[256,256]{1,0:T(8,128)(2,1)S(1)}, bf16[256,256]{1,0:T(8,128)(2,1)}, u32[]{:S(2)}) copy-start(bf16[256,256]{1,0:T(8,128)(2,1)} %weight.1) | copy-start | bytes 393220
  47.5 6.4 %copy-start.3 = (f32[256]{0:T(256)S(1)}, f32[256]{0:T(256)}, u32[]{:S(2)}) copy-start(f32[256]{0:T(256)} %param.10) | copy-start | bytes 3076
  51.9 2.0 %collective-permute-start.12 = (f32[4,128,256]{2,1,0:T(8,128)S(1)}, f32[4,128,256]{2,1,0:T(8,128)S(1)}, u32[]{:S(2)}, u32[]{:S(2)}) collective-permute-start(f32[4,128,256]{2,1,0:T(8,128)S(1)} %get-tuple-element.13), channel_id=1, source_target_pairs={{0,1},{1,0},{2,3},{3,2},{4,5},{5,4},{6,7},{7,6},{8,9},{9,8},{10,11... | collective-permute-start | bytes 1572872 | tf_op jit(solution)/shard_map/rows/ppermute | solution.py:75
  55.1 1.4 %collective-permute-start.13 = (f32[136,256]{1,0:T(8,128)S(1)}, f32[136,256]{1,0:T(8,128)S(1)}, u32[]{:S(2)}, u32[]{:S(2)}) collective-permute-start(f32[136,256]{1,0:T(8,128)S(1)} %get-tuple-element.16), channel_id=1, source_target_pairs={{0,1},{1,0},{2,3},{3,2},{4,5},{5,4},{6,7},{7,6},{8,9},{9,8},{10,11... | collective-permute-start | bytes 417800 | tf_op jit(solution)/shard_map/halves/ppermute | solution.py:75
  56.4 5.2 %collective-permute-start.14 = (f32[136,256]{1,0:T(8,128)S(1)}, f32[136,256]{1,0:T(8,128)S(1)}, u32[]{:S(2)}, u32[]{:S(2)}) collective-permute-start(f32[136,256]{1,0:T(8,128)S(1)} %add.135), channel_id=1, source_target_pairs={{0,2},{1,5},{2,0},{3,7},{4,6},{5,1},{6,4},{7,3},{8,10},{9,13},{10,... | collective-permute-start | bytes 417800 | tf_op jit(solution)/shard_map/sum1/ppermute | solution.py:70
  61.6 5.1 %collective-permute-start.15 = (f32[136,256]{1,0:T(8,128)S(1)}, f32[136,256]{1,0:T(8,128)S(1)}, u32[]{:S(2)}, u32[]{:S(2)}) collective-permute-start(f32[136,256]{1,0:T(8,128)S(1)} %add.136), channel_id=1, source_target_pairs={{0,4},{1,3},{2,6},{3,1},{4,0},{5,7},{6,2},{7,5},{8,12},{9,11},{10,... | collective-permute-start | bytes 417800 | tf_op jit(solution)/shard_map/sum2/ppermute | solution.py:70
  66.8 6.1 %collective-permute-start.16 = (bf16[136,256]{1,0:T(8,128)(2,1)S(1)}, bf16[136,256]{1,0:T(8,128)(2,1)S(1)}, u32[]{:S(2)}, u32[]{:S(2)}) collective-permute-start(bf16[136,256]{1,0:T(8,128)(2,1)S(1)} %add_convert_fusion), channel_id=1, source_target_pairs={{0,8},{1,9},{2,10},{3,11},{4,12},{5,13},{6,14},{7,15},{8,0},{9,1},... | collective-permute-start | bytes 208904 | tf_op jit(solution)/shard_map/sum3/ppermute | solution.py:70
  70.0 6.3 %collective-permute-start.17 = (bf16[136,256]{1,0:T(8,128)(2,1)S(1)}, bf16[136,256]{1,0:T(8,128)(2,1)S(1)}, u32[]{:S(2)}, u32[]{:S(2)}) collective-permute-start(bf16[136,256]{1,0:T(8,128)(2,1)S(1)} %add_convert_fusion), channel_id=1, source_target_pairs={{0,16},{1,17},{2,18},{3,19},{4,20},{5,21},{6,22},{7,23},{8,24},{9,... | collective-permute-start | bytes 208904 | tf_op jit(solution)/shard_map/sum4/ppermute | solution.py:70
  71.5 6.2 %collective-permute-start.18 = (bf16[136,256]{1,0:T(8,128)(2,1)S(1)}, bf16[136,256]{1,0:T(8,128)(2,1)S(1)}, u32[]{:S(2)}, u32[]{:S(2)}) collective-permute-start(bf16[136,256]{1,0:T(8,128)(2,1)S(1)} %add_convert_fusion), channel_id=1, source_target_pairs={{0,24},{1,25},{2,26},{3,27},{4,28},{5,29},{6,30},{7,31},{8,16},{9,... | collective-permute-start | bytes 208904 | tf_op jit(solution)/shard_map/sum5/ppermute | solution.py:70
  77.8 1.4 %collective-permute-start.19 = (f32[136,256]{1,0:T(8,128)S(1)}, f32[136,256]{1,0:T(8,128)S(1)}, u32[]{:S(2)}, u32[]{:S(2)}) collective-permute-start(f32[136,256]{1,0:T(8,128)S(1)} %add_add_fusion), channel_id=1, source_target_pairs={{0,1},{1,0},{2,3},{3,2},{4,5},{5,4},{6,7},{7,6},{8,9},{9,8},{10,11... | collective-permute-start | bytes 417800 | tf_op jit(solution)/shard_map/back/ppermute | solution.py:75
where the time goes:
time: 80.6 us
  waiting for transfers between devices  36.4 us (45%)
  starting transfers between devices  25.3 us (31%)
  Pallas kernels  12.6 us (16%)
  blocking collectives  1.98 us (2%)
  local copies, waits for them, and re-layouts  1.85 us (2%)
  other arithmetic  1.56 us (2%)
  between operations  0.85 us (1%)
    ppermute x16, waiting for transfers between devices, send(): return lax.ppermute(x, BOTH, perm)  32 us
    ppermute x16, starting transfers between devices, send(): return lax.ppermute(x, BOTH, perm)  24.5 us
    pallas_call x3, Pallas kernels, add_groups(): pl.pallas_call(functools.partial(add_kernel, groups, fresh), out_shape=sh...  6.74 us
    ppermute x4, waiting for transfers between devices, swap(): return lax.ppermute(x, 'replica', [(0, 1), (1, 0)])  4.47 us
    pallas_call x1, Pallas kernels, gather_tiles(): pl.pallas_call(functools.partial(gather_kernel, own.shape[0]), out_shape=...  3.51 us
    all_gather x1, blocking collectives, shards(): index = lax.all_gather(tile_index, 'replica', axis=0, tiled=True)  1.98 us
  transfers between devices with their start and end apart: 20, of which 13 were waited for; matrix products, arithmetic and copies ran while one was open for 2% of the time, Pallas kernels for 13%

commit v1 on v0

--- a/solution.py
+++ b/solution.py
@@ -133,9 +133,9 @@
 
 
 def gather_kernel(count, entries, starts, own, other, out, sem):
-    total = starts[8]
-
-    def begin(m, carry):
+    pairs = starts[8] // 2
+
+    def fetch(m):
         tile = entries[m] & 255
 
         @pl.when(tile < count)
@@ -146,14 +146,22 @@
         def _():
             pltpu.make_async_copy(other.at[tile - count], out.at[m], sem).start()
 
+    def begin(j, carry):
+        fetch(2 * j)
+        fetch(2 * j + 1)
         return carry
 
-    def finish(m, carry):
-        pltpu.make_async_copy(own.at[0], out.at[0], sem).wait()
-        return carry
-
-    lax.fori_loop(0, total, begin, 0)
-    lax.fori_loop(0, total, finish, 0)
+    def finish(size):
+        def step(j, carry):
+            block = out.at[pl.ds(0, size)]
+            pltpu.make_async_copy(own.at[pl.ds(0, size)], block, sem).wait()
+            return carry
+
+        return step
+
+    lax.fori_loop(0, pairs, begin, 0)
+    lax.fori_loop(0, pairs // 8, finish(16), 0)
+    lax.fori_loop(0, pairs % 8, finish(2), 0)
 
 
 def gather_tiles(entries, starts, own, other):
@@ -165,8 +173,8 @@
         out_specs=pl.BlockSpec(memory_space=VMEM),
         scratch_shapes=[pltpu.SemaphoreType.DMA],
         name="gather_tiles",
-        compiler_params=pltpu.CompilerParams(vmem_limit_bytes=1 << 20),
-        cost_estimate=pl.CostEstimate(flops=4000000000, bytes_accessed=10000000, transcendentals=0),
+        compiler_params=pltpu.CompilerParams(vmem_limit_bytes=47 << 20),
+        cost_estimate=pl.CostEstimate(flops=0, bytes_accessed=1 << 10, transcendentals=0),
     )(entries, starts, own, other)
 
 
@@ -198,11 +206,10 @@
 
 
 def late_kernel(groups, entries, starts, tiles, *refs):
-    arrays, (acc, keep, give) = refs[: len(groups)], refs[len(groups) + 1 :]
+    arrays, (acc, give) = refs[: len(groups)], refs[len(groups) + 1 :]
     for g, array in zip(groups, arrays):
         add_group(entries, starts[g], starts[g + 1], tiles, array, acc)
-    half = keep.shape[0]
-    keep[...] = acc[:half]
+    half = give.shape[0]
     give[...] = acc[half : 2 * half]
 
 
@@ -210,7 +217,7 @@
     return pl.BlockSpec(memory_space=space)
 
 
-def add_groups(work, arrays, groups, acc, row_blocks, name, cost=4000000000):
+def add_groups(work, arrays, groups, acc, row_blocks, name):
     entries, starts, tiles = work
     shape = VMEM((row_blocks + 1, 128, arrays[0].shape[1]), jnp.float32)
     fresh = acc is None
@@ -222,7 +229,7 @@
         name=name,
         input_output_aliases={} if fresh else {3 + len(arrays): 0},
         compiler_params=pltpu.CompilerParams(vmem_limit_bytes=4 << 20),
-        cost_estimate=pl.CostEstimate(flops=cost, bytes_accessed=cost // 400, transcendentals=0),
+        cost_estimate=pl.CostEstimate(flops=16 << 28, bytes_accessed=4 << 20, transcendentals=0),
     )(entries, starts, tiles, *arrays, *([] if fresh else [acc]))
 
 
@@ -231,18 +238,18 @@
     half = VMEM((row_blocks // 2, 128, arrays[0].shape[1]), jnp.float32)
     return pl.pallas_call(
         functools.partial(late_kernel, groups),
-        out_shape=(VMEM(acc.shape, jnp.float32), half, half),
+        out_shape=(VMEM(acc.shape, jnp.float32), half),
         in_specs=[whole(SMEM)] * 2 + [whole(VMEM)] * (2 + len(arrays)),
-        out_specs=(whole(VMEM),) * 3,
+        out_specs=(whole(VMEM),) * 2,
         name="add_late",
         input_output_aliases={3 + len(arrays): 0},
         compiler_params=pltpu.CompilerParams(vmem_limit_bytes=4 << 20),
         cost_estimate=pl.CostEstimate(flops=1 << 25, bytes_accessed=2 << 20, transcendentals=0),
-    )(entries, starts, tiles, *arrays, acc)[1:]
+    )(entries, starts, tiles, *arrays, acc)
 
 
 def dense_kernel(core, mine, theirs, weight, bias, grad_out, output, keep, give, full):
-    hidden = (mine[...] + theirs[...]).reshape(grad_out.shape).astype(jnp.bfloat16)
+    hidden = (mine[: theirs.shape[0]] + theirs[...]).reshape(grad_out.shape).astype(jnp.bfloat16)
     pre_act = jnp.dot(hidden, weight[...], preferred_element_type=jnp.float32) + bias[...]
     sigma = 1.0 / (1.0 + jnp.exp(-pre_act))
     output[...] = (pre_act * sigma).astype(jnp.bfloat16)
@@ -278,32 +285,64 @@
     )(core.reshape(1), mine, theirs, weight, bias.reshape(1, width), grad_out)
 
 
+def finish_kernel(core, part, rest, weight, bias):
+    share = part.shape[0] - 8
+    at = core[0]
+    weight[pl.ds(pl.multiple_of(at * share, share), share), :] = part[:share]
+    weight[pl.ds(pl.multiple_of((1 - at) * share, share), share), :] = rest[:share]
+
+    @pl.when(at == 0)
+    def _():
+        bias[...] = part[pl.ds(share, 1), :]
+
+    @pl.when(at != 0)
+    def _():
+        bias[...] = rest[pl.ds(share, 1), :]
+
+
+def finish(core, part, rest):
+    rows, width = part.shape
+    return pl.pallas_call(
+        finish_kernel,
+        out_shape=(
+            jax.ShapeDtypeStruct((2 * (rows - 8), width), jnp.float32),
+            jax.ShapeDtypeStruct((1, width), jnp.float32),
+        ),
+        in_specs=[whole(SMEM)] + [whole(VMEM)] * 2,
+        out_specs=(whole(VMEM),) * 2,
+        name="finish",
+        compiler_params=pltpu.CompilerParams(vmem_limit_bytes=4 << 20),
+    )(core.reshape(1), part, rest)
+
+
 def shards(features, adj_tiles, tile_index, weight, bias_vec, grad_out):
     core = lax.axis_index("replica")
     row_blocks = 2 * features.shape[0] // adj_tiles.shape[1]
     slots = adj_tiles.shape[0] // 8
 
-    index = lax.all_gather(tile_index, "replica", axis=0, tiled=True)
     z1 = along_z(features, 1, "z1")
     z2 = along_z(features, 2, "z2")
     r0 = first_hop(features, "r0")
+    r0, index = after(r0, tile_index)
+    index = lax.all_gather(index, "replica", axis=0, tiled=True)
     pair0 = join(features, r0)
     q0 = second_hop(pair0, "q0")
-    again = features
-    tiles_in = adj_tiles
+    other_tiles = swap(adj_tiles, "tiles")
     z1, again = after(z1, features)
     z3 = along_z(again, 3, "z3")
-    other_tiles = swap(tiles_in, "tiles")
+    pair1 = join(z1, first_hop(z1, "r1"))
+    q1 = along_z(q0, 1, "q1")
+    z2, q0, other_tiles = after(z2, q0, other_tiles)
+    pair2 = join(z2, first_hop(z2, "r2"))
+    pair2, other_tiles = after(pair2, other_tiles)
+    q2 = second_hop(pair2, "q2")
+    z3, pair1, pair2 = after(z3, pair1, pair2)
+    pair3 = join(z3, first_hop(z3, "r3"))
+    q3 = second_hop(pair3, "q3")
     entries, starts = work_list(index, slots, row_blocks)
     tiles = gather_tiles(entries, starts, adj_tiles, other_tiles)
-    pair1 = join(z1, first_hop(z1, "r1"))
-    q1 = second_hop(pair1, "q1")
-    pair2 = join(z2, first_hop(z2, "r2"))
-    q2 = second_hop(pair2, "q2")
     work = (entries, starts, tiles)
     acc = add_groups(work, (pair0, q0, pair1), (0, 1, 2), None, row_blocks, "add_a")
-    pair3 = join(z3, first_hop(z3, "r3"))
-    q3 = second_hop(pair3, "q3")
     acc = add_groups(work, (q1, pair2), (3, 4), acc, row_blocks, "add_b")
     acc = add_groups(work, (q2, pair3), (5, 6), acc, row_blocks, "add_c")
     mine, give = add_late(work, (q3,), (7,), acc, row_blocks)
@@ -317,11 +356,8 @@
     z_parts += [along_z(low_part, k, f"sum{2 + k}").astype(jnp.float32) for k in (1, 2, 3)]
     part = (z_parts[0] + z_parts[1]) + (z_parts[2] + z_parts[3])
     rest = swap(part, "back")
-    share = part.shape[0] - 8
-    top = jnp.where(core == 0, part, rest)
-    low = jnp.where(core == 0, rest, part)
-    grad_weight = jnp.concatenate([top[:share], low[:share]], axis=0)
-    return output, grad_weight, top[share]
+    grad_weight, grad_bias = finish(core, part, rest)
+    return output, grad_weight, grad_bias.reshape(bias_vec.shape)
 
 
 def solution(mesh):

time: 80.6 us -> 76.3 us (0.947)
  starting transfers between devices: 25.3 us -> 22.8 us
  Pallas kernels: 12.6 us -> 11.1 us
    ppermute x16, starting transfers between devices: 24.5 us -> 22 us  [send(): return lax.ppermute(x, BOTH, perm)]
    pallas_call x1, Pallas kernels: 3.51 us -> 2.1 us  [gather_tiles(): pl.pallas_call(functools.partial(gather_kernel, own.shape[0]), out_shape=...]
    unnamed x12 -> x14, local copies, waits for them, and re-layouts: 1.2 us -> 1.7 us
  transfers between devices with their start and end apart: 20 -> 20, of which waited for: 13 -> 11; matrix products, arithmetic and copies ran while one was open for 2% -> 3% of each run, Pallas kernels for 13% -> 11%
where the time goes in v1:
time: 76.3 us; the launch traced here: 75.9 us
  waiting for transfers between devices  35.9 us (47%)
  starting transfers between devices  22.8 us (30%)
  Pallas kernels  11.1 us (15%)
  blocking collectives  1.98 us (3%)
  local copies, waits for them, and re-layouts  1.74 us (2%)
  other arithmetic  1.43 us (2%)
  between operations  0.88 us (1%)
    ppermute x16, waiting for transfers between devices, send(): return lax.ppermute(x, BOTH, perm)  31.4 us
    ppermute x16, starting transfers between devices, send(): return lax.ppermute(x, BOTH, perm)  22 us
    pallas_call x3, Pallas kernels, add_groups(): pl.pallas_call(functools.partial(add_kernel, groups, fresh), out_shape=sh...  5.98 us
    ppermute x4, waiting for transfers between devices, swap(): return lax.ppermute(x, 'replica', [(0, 1), (1, 0)])  4.47 us
    pallas_call x1, Pallas kernels, gather_tiles(): pl.pallas_call(functools.partial(gather_kernel, own.shape[0]), out_shape=...  2.1 us
    all_gather x1, blocking collectives, shards(): index = lax.all_gather(index, 'replica', axis=0, tiled=True)  1.98 us
    unnamed x14, local copies, waits for them, and re-layouts  1.7 us
  transfers between devices with their start and end apart: 20, of which 11 were waited for; matrix products, arithmetic and copies ran while one was open for 3% of the time, Pallas kernels for 11%

profile of v1, /device:TPU:0, one launch (start us, length us, event | category | flops | bytes accessed | tf_op | source)
XLA Modules:
  0.0 75.9 jit_solution(16457996186872474501)
XLA Ops:
  1.1 2.6 %collective-permute-start = (bf16[512,256]{1,0:T(8,128)(2,1)}, bf16[512,256]{1,0:T(8,128)(2,1)S(1)}, u32[]{:S(2)}, u32[]{:S(2)}) collective-permute-start(bf16[512,256]{1,0:T(8,128)(2,1)} %param.6), channel_id=1, source_target_pairs={{0,2},{1,5},{2,0},{3,7},{4,6},{5,1},{6,4},{7,3},{8,10},{9,13},{10,... | collective-permute-start | bytes 786440 | tf_op jit(solution)/shard_map/r0/ppermute | solution.py:70
  3.7 1.6 %collective-permute-start.5 = (bf16[512,256]{1,0:T(8,128)(2,1)}, bf16[512,256]{1,0:T(8,128)(2,1)S(1)}, u32[]{:S(2)}, u32[]{:S(2)}) collective-permute-start(bf16[512,256]{1,0:T(8,128)(2,1)} %param.6), channel_id=1, source_target_pairs={{0,8},{1,9},{2,10},{3,11},{4,12},{5,13},{6,14},{7,15},{8,0},{9,1},... | collective-permute-start | bytes 786440 | tf_op jit(solution)/shard_map/z1/ppermute | solution.py:70
  5.3 2.6 %collective-permute-start.1 = (bf16[512,256]{1,0:T(8,128)(2,1)}, bf16[512,256]{1,0:T(8,128)(2,1)S(1)}, u32[]{:S(2)}, u32[]{:S(2)}) collective-permute-start(bf16[512,256]{1,0:T(8,128)(2,1)} %param.6), channel_id=1, source_target_pairs={{0,16},{1,17},{2,18},{3,19},{4,20},{5,21},{6,22},{7,23},{8,24},{9,... | collective-permute-start | bytes 786440 | tf_op jit(solution)/shard_map/z2/ppermute | solution.py:70
  8.9 1.6 %collective-permute-start.2 = (bf16[1024,256]{1,0:T(8,128)(2,1)S(1)}, bf16[1024,256]{1,0:T(8,128)(2,1)S(1)}, u32[]{:S(2)}, u32[]{:S(2)}) collective-permute-start(bf16[1024,256]{1,0:T(8,128)(2,1)S(1)} %constant_dynamic-update-slice_fusion.refs_0_), channel_id=1, source_target_pairs={{0,4},{1,3},{2,6},{3,1},{4,0},{5,7},{6,2},{7,5},{8,12},{9,11},{10,... | collective-permute-start | bytes 1572872 | tf_op jit(solution)/shard_map/q0/ppermute | solution.py:70
  10.5 7.3 %collective-permute-done.5 = bf16[512,256]{1,0:T(8,128)(2,1)S(1)} collective-permute-done((bf16[512,256]{1,0:T(8,128)(2,1)}, bf16[512,256]{1,0:T(8,128)(2,1)S(1)}, u32[]{:S(2)}, u32[]{:S(2)}) %collective-permute-start.5) | collective-permute-done | bytes 262176 | tf_op jit(solution)/shard_map/z1/ppermute | solution.py:70
  18.0 3.3 %collective-permute-start.6 = (bf16[512,256]{1,0:T(8,128)(2,1)}, bf16[512,256]{1,0:T(8,128)(2,1)S(1)}, u32[]{:S(2)}, u32[]{:S(2)}) collective-permute-start(bf16[512,256]{1,0:T(8,128)(2,1)} %param.6), channel_id=1, source_target_pairs={{0,24},{1,25},{2,26},{3,27},{4,28},{5,29},{6,30},{7,31},{8,16},{9,... | collective-permute-start | bytes 786440 | tf_op jit(solution)/shard_map/z3/ppermute | solution.py:70
  21.3 2.0 %all_gather.3 = s32[256,2]{0,1:T(2,128)S(1)} all-gather(s32[128,2]{0,1:T(2,128)} %param.8), channel_id=1, replica_groups=mesh['section'=16,'replica'=2] {'replica'}, dimensions={0}, use_global_device_ids=true | all-gather | bytes 3072 | tf_op jit(solution)/shard_map/all_gather | solution.py:327
  25.8 4.6 %collective-permute-done.4 = bf16[512,256]{1,0:T(8,128)(2,1)S(1)} collective-permute-done((bf16[512,256]{1,0:T(8,128)(2,1)S(1)}, bf16[512,256]{1,0:T(8,128)(2,1)S(1)}, u32[]{:S(2)}, u32[]{:S(2)}) %collective-permute-start.4) | collective-permute-done | bytes 262176 | tf_op jit(solution)/shard_map/r2/ppermute | solution.py:70
  32.1 2.1 %gather_tiles.1.tiles = bf16[272,128,128]{2,1,0:T(8,128)(2,1)S(1)} custom-call(s32[272]{0:T(512)} %broadcast_add_fusion.entries, s32[9]{0:T(128)} %copy-done.3, bf16[128,128,128]{2,1,0:T(8,128)(2,1)} %own.1, bf16[128,128,128]{2,1,0:T(8,128)(2,1)} %collective-permute-done.3.other), custom_call_target="tpu_custom_call" | custom-call | bytes 1024 | tf_op jit(solution)/shard_map/gather_tiles/pallas_call | solution.py:169
  34.9 2.4 %add_a.1.refs_2_ = f32[9,128,256]{2,1,0:T(8,128)S(1)} custom-call(s32[272]{0:T(512)S(1)} %copy-done.2, s32[9]{0:T(128)S(1)} %copy-done.4, bf16[272,128,128]{2,1,0:T(8,128)(2,1)S(1)} %gather_tiles.1.tiles, bf16[1024,256]{1,0:T(8,128)(2,1)S(1)} %constant_dynamic-update-slice_fusion.refs_0_, bf16[1024,256]{1,0:T(8,128)(2,1)S(1)} %collective-permute-done.2.refs_1_, ...), custom_call_target="tpu_custom_call" | custom-call | flops 4294967296 | bytes 4194304 | tf_op jit(solution)/shard_map/add_a/pallas_call | solution.py:224
  37.3 3.5 %collective-permute-done.8 = bf16[512,256]{1,0:T(8,128)(2,1)S(1)} collective-permute-done((bf16[512,256]{1,0:T(8,128)(2,1)S(1)}, bf16[512,256]{1,0:T(8,128)(2,1)S(1)}, u32[]{:S(2)}, u32[]{:S(2)}) %collective-permute-start.8) | collective-permute-done | bytes 262176 | tf_op jit(solution)/shard_map/r3/ppermute | solution.py:70
  41.9 1.1 %add_b.1.refs_2_ = f32[9,128,256]{2,1,0:T(8,128)S(1)} custom-call(s32[272]{0:T(512)S(1)} %copy-done.2, s32[9]{0:T(128)S(1)} %copy-done.4, bf16[272,128,128]{2,1,0:T(8,128)(2,1)S(1)} %gather_tiles.1.tiles, bf16[1024,256]{1,0:T(8,128)(2,1)S(1)} %collective-permute-done.11.refs_0_, ...), custom_call_target="tpu_custom_call", output_to_operand_aliasing={{}: (5, {})} | custom-call | flops 4294967296 | bytes 4194304 | tf_op jit(solution)/shard_map/add_b/pallas_call | solution.py:224
  43.1 2.5 %add_c.1.refs_1_ = f32[9,128,256]{2,1,0:T(8,128)S(1)} custom-call(s32[272]{0:T(512)S(1)} %copy-done.2, s32[9]{0:T(128)S(1)} %copy-done.4, bf16[272,128,128]{2,1,0:T(8,128)(2,1)S(1)} %gather_tiles.1.tiles, bf16[1024,256]{1,0:T(8,128)(2,1)S(1)} %collective-permute-done.10.refs_0_, ...), custom_call_target="tpu_custom_call", output_to_operand_aliasing={{}: (5, {})} | custom-call | flops 4294967296 | bytes 4194304 | tf_op jit(solution)/shard_map/add_c/pallas_call | solution.py:224
  45.6 4.5 %collective-permute-done.9.refs_0_ = bf16[1024,256]{1,0:T(8,128)(2,1)S(1)} collective-permute-done((bf16[1024,256]{1,0:T(8,128)(2,1)S(1)}, bf16[1024,256]{1,0:T(8,128)(2,1)S(1)}, u32[]{:S(2)}, u32[]{:S(2)}) %collective-permute-start.9) | collective-permute-done | bytes 524320 | tf_op jit(solution)/shard_map/q3/ppermute | solution.py:70
  50.1 1.2 %add_late.1 = (f32[9,128,256]{2,1,0:T(8,128)S(1)}, f32[4,128,256]{2,1,0:T(8,128)S(1)}) custom-call(s32[272]{0:T(512)S(1)} %copy-done.2, s32[9]{0:T(128)S(1)} %copy-done.4, bf16[272,128,128]{2,1,0:T(8,128)(2,1)S(1)} %gather_tiles.1.tiles, bf16[1024,256]{1,0:T(8,128)(2,1)S(1)} %collective-permute-done.9.refs_0_, ...), custom_call_target="tpu_custom_call", output_to_operand_aliasing={{0}: (4, {})} | custom-call | flops 33554432 | bytes 2097152 | tf_op jit(solution)/shard_map/add_late/pallas_call | solution.py:239
  51.4 1.9 %collective-permute-done.12.theirs = f32[4,128,256]{2,1,0:T(8,128)S(1)} collective-permute-done((f32[4,128,256]{2,1,0:T(8,128)S(1)}, f32[4,128,256]{2,1,0:T(8,128)S(1)}, u32[]{:S(2)}, u32[]{:S(2)}) %collective-permute-start.12) | collective-permute-done | bytes 524320 | tf_op jit(solution)/shard_map/rows/ppermute | solution.py:75
  53.3 1.1 %dense.1 = (bf16[512,256]{1,0:T(8,128)(2,1)}, f32[136,256]{1,0:T(8,128)S(1)}, f32[136,256]{1,0:T(8,128)S(1)}) custom-call(s32[1]{0:T(128)} %bitcast.core, f32[9,128,256]{2,1,0:T(8,128)S(1)} %get-tuple-element.34.mine, f32[4,128,256]{2,1,0:T(8,128)S(1)} %collective-permute-done.12.theirs, bf16[256,256]{1,0:T(8,128)(2,1)S(1)} %copy-done.1, ...), custom_call_target="tpu_custom_call" | custom-call | flops 134217728 | bytes 2097152 | tf_op jit(solution)/shard_map/dense/pallas_call | solution.py:274
  54.5 1.2 %collective-permute-done.13 = f32[136,256]{1,0:T(8,128)S(1)} collective-permute-done((f32[136,256]{1,0:T(8,128)S(1)}, f32[136,256]{1,0:T(8,128)S(1)}, u32[]{:S(2)}, u32[]{:S(2)}) %collective-permute-start.13) | collective-permute-done | bytes 139296 | tf_op jit(solution)/shard_map/halves/ppermute | solution.py:75
  56.6 4.3 %collective-permute-done.14 = f32[136,256]{1,0:T(8,128)S(1)} collective-permute-done((f32[136,256]{1,0:T(8,128)S(1)}, f32[136,256]{1,0:T(8,128)S(1)}, u32[]{:S(2)}, u32[]{:S(2)}) %collective-permute-start.14) | collective-permute-done | bytes 139296 | tf_op jit(solution)/shard_map/sum1/ppermute | solution.py:70
  62.0 4.0 %collective-permute-done.15 = f32[136,256]{1,0:T(8,128)S(1)} collective-permute-done((f32[136,256]{1,0:T(8,128)S(1)}, f32[136,256]{1,0:T(8,128)S(1)}, u32[]{:S(2)}, u32[]{:S(2)}) %collective-permute-start.15) | collective-permute-done | bytes 139296 | tf_op jit(solution)/shard_map/sum2/ppermute | solution.py:70
  67.2 3.3 %collective-permute-start.18 = (bf16[136,256]{1,0:T(8,128)(2,1)S(1)}, bf16[136,256]{1,0:T(8,128)(2,1)S(1)}, u32[]{:S(2)}, u32[]{:S(2)}) collective-permute-start(bf16[136,256]{1,0:T(8,128)(2,1)S(1)} %add_convert_fusion), channel_id=1, source_target_pairs={{0,24},{1,25},{2,26},{3,27},{4,28},{5,29},{6,30},{7,31},{8,16},{9,... | collective-permute-start | bytes 208904 | tf_op jit(solution)/shard_map/sum5/ppermute | solution.py:70
  70.6 1.4 %collective-permute-done.17 = bf16[136,256]{1,0:T(8,128)(2,1)S(1)} collective-permute-done((bf16[136,256]{1,0:T(8,128)(2,1)S(1)}, bf16[136,256]{1,0:T(8,128)(2,1)S(1)}, u32[]{:S(2)}, u32[]{:S(2)}) %collective-permute-start.17) | collective-permute-done | bytes 69664 | tf_op jit(solution)/shard_map/sum4/ppermute | solution.py:70
  71.9 1.7 %collective-permute-done.18 = bf16[136,256]{1,0:T(8,128)(2,1)S(1)} collective-permute-done((bf16[136,256]{1,0:T(8,128)(2,1)S(1)}, bf16[136,256]{1,0:T(8,128)(2,1)S(1)}, u32[]{:S(2)}, u32[]{:S(2)}) %collective-permute-start.18) | collective-permute-done | bytes 69664 | tf_op jit(solution)/shard_map/sum5/ppermute | solution.py:70
  73.8 1.3 %collective-permute-done.19.rest = f32[136,256]{1,0:T(8,128)S(1)} collective-permute-done((f32[136,256]{1,0:T(8,128)S(1)}, f32[136,256]{1,0:T(8,128)S(1)}, u32[]{:S(2)}, u32[]{:S(2)}) %collective-permute-start.19) | collective-permute-done | bytes 139296 | tf_op jit(solution)/shard_map/back/ppermute | solution.py:75
  (58 shorter events, 11.9 us)
Async XLA Ops:
  0.6 23.4 %collective-permute-start.3 = (bf16[128,128,128]{2,1,0:T(8,128)(2,1)}, bf16[128,128,128]{2,1,0:T(8,128)(2,1)}, u32[]{:S(2)}, u32[]{:S(2)}) collective-permute-start(bf16[128,128,128]{2,1,0:T(8,128)(2,1)} %own.1), channel_id=1, source_target_pairs={{0,1},{1,0},{2,3},{3,2},{4,5},{5,4},{6,7},{7,6},{8,9},{9,8},{10,11... | collective-permute-start | bytes 12582920 | tf_op jit(solution)/shard_map/tiles/ppermute | solution.py:75
  1.1 7.7 %collective-permute-start = (bf16[512,256]{1,0:T(8,128)(2,1)}, bf16[512,256]{1,0:T(8,128)(2,1)S(1)}, u32[]{:S(2)}, u32[]{:S(2)}) collective-permute-start(bf16[512,256]{1,0:T(8,128)(2,1)} %param.6), channel_id=1, source_target_pairs={{0,2},{1,5},{2,0},{3,7},{4,6},{5,1},{6,4},{7,3},{8,10},{9,13},{10,... | collective-permute-start | bytes 786440 | tf_op jit(solution)/shard_map/r0/ppermute | solution.py:70
  3.7 14.1 %collective-permute-start.5 = (bf16[512,256]{1,0:T(8,128)(2,1)}, bf16[512,256]{1,0:T(8,128)(2,1)S(1)}, u32[]{:S(2)}, u32[]{:S(2)}) collective-permute-start(bf16[512,256]{1,0:T(8,128)(2,1)} %param.6), channel_id=1, source_target_pairs={{0,8},{1,9},{2,10},{3,11},{4,12},{5,13},{6,14},{7,15},{8,0},{9,1},... | collective-permute-start | bytes 786440 | tf_op jit(solution)/shard_map/z1/ppermute | solution.py:70
  5.3 18.7 %collective-permute-start.1 = (bf16[512,256]{1,0:T(8,128)(2,1)}, bf16[512,256]{1,0:T(8,128)(2,1)S(1)}, u32[]{:S(2)}, u32[]{:S(2)}) collective-permute-start(bf16[512,256]{1,0:T(8,128)(2,1)} %param.6), channel_id=1, source_target_pairs={{0,16},{1,17},{2,18},{3,19},{4,20},{5,21},{6,22},{7,23},{8,24},{9,... | collective-permute-start | bytes 786440 | tf_op jit(solution)/shard_map/z2/ppermute | solution.py:70
  8.9 15.1 %collective-permute-start.2 = (bf16[1024,256]{1,0:T(8,128)(2,1)S(1)}, bf16[1024,256]{1,0:T(8,128)(2,1)S(1)}, u32[]{:S(2)}, u32[]{:S(2)}) collective-permute-start(bf16[1024,256]{1,0:T(8,128)(2,1)S(1)} %constant_dynamic-update-slice_fusion.refs_0_), channel_id=1, source_target_pairs={{0,4},{1,3},{2,6},{3,1},{4,0},{5,7},{6,2},{7,5},{8,12},{9,11},{10,... | collective-permute-start | bytes 1572872 | tf_op jit(solution)/shard_map/q0/ppermute | solution.py:70
  17.8 7.9 %collective-permute-start.7 = (bf16[512,256]{1,0:T(8,128)(2,1)S(1)}, bf16[512,256]{1,0:T(8,128)(2,1)S(1)}, u32[]{:S(2)}, u32[]{:S(2)}) collective-permute-start(bf16[512,256]{1,0:T(8,128)(2,1)S(1)} %collective-permute-done.5), channel_id=1, source_target_pairs={{0,2},{1,5},{2,0},{3,7},{4,6},{5,1},{6,4},{7,3},{8,10},{9,13},{10,... | collective-permute-start | bytes 786440 | tf_op jit(solution)/shard_map/r1/ppermute | solution.py:70
  18.0 13.6 %collective-permute-start.6 = (bf16[512,256]{1,0:T(8,128)(2,1)}, bf16[512,256]{1,0:T(8,128)(2,1)S(1)}, u32[]{:S(2)}, u32[]{:S(2)}) collective-permute-start(bf16[512,256]{1,0:T(8,128)(2,1)} %param.6), channel_id=1, source_target_pairs={{0,24},{1,25},{2,26},{3,27},{4,28},{5,29},{6,30},{7,31},{8,16},{9,... | collective-permute-start | bytes 786440 | tf_op jit(solution)/shard_map/z3/ppermute | solution.py:70
  23.5 8.6 %copy-start.3 = (s32[9]{0:T(128)}, s32[9]{0:T(128)S(1)}, u32[]{:S(2)}) copy-start(s32[9]{0:T(128)S(1)} %select_reduce_fusion.2.starts) | copy-start | bytes 112
  24.0 6.4 %collective-permute-start.4 = (bf16[512,256]{1,0:T(8,128)(2,1)S(1)}, bf16[512,256]{1,0:T(8,128)(2,1)S(1)}, u32[]{:S(2)}, u32[]{:S(2)}) collective-permute-start(bf16[512,256]{1,0:T(8,128)(2,1)S(1)} %collective-permute-done.1), channel_id=1, source_target_pairs={{0,2},{1,5},{2,0},{3,7},{4,6},{5,1},{6,4},{7,3},{8,10},{9,13},{10,... | collective-permute-start | bytes 786440 | tf_op jit(solution)/shard_map/r2/ppermute | solution.py:70
  25.7 16.2 %collective-permute-start.11 = (bf16[1024,256]{1,0:T(8,128)(2,1)S(1)}, bf16[1024,256]{1,0:T(8,128)(2,1)S(1)}, u32[]{:S(2)}, u32[]{:S(2)}) collective-permute-start(bf16[1024,256]{1,0:T(8,128)(2,1)S(1)} %collective-permute-done.2.refs_1_), channel_id=1, source_target_pairs={{0,8},{1,9},{2,10},{3,11},{4,12},{5,13},{6,14},{7,15},{8,0},{9,1},... | collective-permute-start | bytes 1572872 | tf_op jit(solution)/shard_map/q1/ppermute | solution.py:70
  30.5 12.6 %collective-permute-start.10 = (bf16[1024,256]{1,0:T(8,128)(2,1)S(1)}, bf16[1024,256]{1,0:T(8,128)(2,1)S(1)}, u32[]{:S(2)}, u32[]{:S(2)}) collective-permute-start(bf16[1024,256]{1,0:T(8,128)(2,1)S(1)} %pad_maximum_fusion.refs_1_), channel_id=1, source_target_pairs={{0,4},{1,3},{2,6},{3,1},{4,0},{5,7},{6,2},{7,5},{8,12},{9,11},{10,... | collective-permute-start | bytes 1572872 | tf_op jit(solution)/shard_map/q2/ppermute | solution.py:70
  31.6 9.2 %collective-permute-start.8 = (bf16[512,256]{1,0:T(8,128)(2,1)S(1)}, bf16[512,256]{1,0:T(8,128)(2,1)S(1)}, u32[]{:S(2)}, u32[]{:S(2)}) collective-permute-start(bf16[512,256]{1,0:T(8,128)(2,1)S(1)} %collective-permute-done.6), channel_id=1, source_target_pairs={{0,2},{1,5},{2,0},{3,7},{4,6},{5,1},{6,4},{7,3},{8,10},{9,13},{10,... | collective-permute-start | bytes 786440 | tf_op jit(solution)/shard_map/r3/ppermute | solution.py:70
  40.8 9.2 %collective-permute-start.9 = (bf16[1024,256]{1,0:T(8,128)(2,1)S(1)}, bf16[1024,256]{1,0:T(8,128)(2,1)S(1)}, u32[]{:S(2)}, u32[]{:S(2)}) collective-permute-start(bf16[1024,256]{1,0:T(8,128)(2,1)S(1)} %constant_dynamic-update-slice_fusion.2.refs_1_), channel_id=1, source_target_pairs={{0,4},{1,3},{2,6},{3,1},{4,0},{5,7},{6,2},{7,5},{8,12},{9,11},{10,... | collective-permute-start | bytes 1572872 | tf_op jit(solution)/shard_map/q3/ppermute | solution.py:70
  45.6 7.7 %copy-start = (bf16[512,256]{1,0:T(8,128)(2,1)S(1)}, bf16[512,256]{1,0:T(8,128)(2,1)}, u32[]{:S(2)}) copy-start(bf16[512,256]{1,0:T(8,128)(2,1)} %grad_out.1) | copy-start | bytes 786436
  45.6 7.6 %copy-start.1 = (bf16[256,256]{1,0:T(8,128)(2,1)S(1)}, bf16[256,256]{1,0:T(8,128)(2,1)}, u32[]{:S(2)}) copy-start(bf16[256,256]{1,0:T(8,128)(2,1)} %weight.1) | copy-start | bytes 393220
  45.6 7.6 %copy-start.5 = (f32[256]{0:T(256)S(1)}, f32[256]{0:T(256)}, u32[]{:S(2)}) copy-start(f32[256]{0:T(256)} %param.10) | copy-start | bytes 3076
  51.3 2.0 %collective-permute-start.12 = (f32[4,128,256]{2,1,0:T(8,128)S(1)}, f32[4,128,256]{2,1,0:T(8,128)S(1)}, u32[]{:S(2)}, u32[]{:S(2)}) collective-permute-start(f32[4,128,256]{2,1,0:T(8,128)S(1)} %get-tuple-element.35), channel_id=1, source_target_pairs={{0,1},{1,0},{2,3},{3,2},{4,5},{5,4},{6,7},{7,6},{8,9},{9,8},{10,11... | collective-permute-start | bytes 1572872 | tf_op jit(solution)/shard_map/rows/ppermute | solution.py:75
  54.4 1.4 %collective-permute-start.13 = (f32[136,256]{1,0:T(8,128)S(1)}, f32[136,256]{1,0:T(8,128)S(1)}, u32[]{:S(2)}, u32[]{:S(2)}) collective-permute-start(f32[136,256]{1,0:T(8,128)S(1)} %get-tuple-element.38), channel_id=1, source_target_pairs={{0,1},{1,0},{2,3},{3,2},{4,5},{5,4},{6,7},{7,6},{8,9},{9,8},{10,11... | collective-permute-start | bytes 417800 | tf_op jit(solution)/shard_map/halves/ppermute | solution.py:75
  55.8 5.1 %collective-permute-start.14 = (f32[136,256]{1,0:T(8,128)S(1)}, f32[136,256]{1,0:T(8,128)S(1)}, u32[]{:S(2)}, u32[]{:S(2)}) collective-permute-start(f32[136,256]{1,0:T(8,128)S(1)} %add.135), channel_id=1, source_target_pairs={{0,2},{1,5},{2,0},{3,7},{4,6},{5,1},{6,4},{7,3},{8,10},{9,13},{10,... | collective-permute-start | bytes 417800 | tf_op jit(solution)/shard_map/sum1/ppermute | solution.py:70
  60.9 5.1 %collective-permute-start.15 = (f32[136,256]{1,0:T(8,128)S(1)}, f32[136,256]{1,0:T(8,128)S(1)}, u32[]{:S(2)}, u32[]{:S(2)}) collective-permute-start(f32[136,256]{1,0:T(8,128)S(1)} %add.136), channel_id=1, source_target_pairs={{0,4},{1,3},{2,6},{3,1},{4,0},{5,7},{6,2},{7,5},{8,12},{9,11},{10,... | collective-permute-start | bytes 417800 | tf_op jit(solution)/shard_map/sum2/ppermute | solution.py:70
  66.1 4.5 %collective-permute-start.16 = (bf16[136,256]{1,0:T(8,128)(2,1)S(1)}, bf16[136,256]{1,0:T(8,128)(2,1)S(1)}, u32[]{:S(2)}, u32[]{:S(2)}) collective-permute-start(bf16[136,256]{1,0:T(8,128)(2,1)S(1)} %add_convert_fusion), channel_id=1, source_target_pairs={{0,8},{1,9},{2,10},{3,11},{4,12},{5,13},{6,14},{7,15},{8,0},{9,1},... | collective-permute-start | bytes 208904 | tf_op jit(solution)/shard_map/sum3/ppermute | solution.py:70
  66.2 5.8 %collective-permute-start.17 = (bf16[136,256]{1,0:T(8,128)(2,1)S(1)}, bf16[136,256]{1,0:T(8,128)(2,1)S(1)}, u32[]{:S(2)}, u32[]{:S(2)}) collective-permute-start(bf16[136,256]{1,0:T(8,128)(2,1)S(1)} %add_convert_fusion), channel_id=1, source_target_pairs={{0,16},{1,17},{2,18},{3,19},{4,20},{5,21},{6,22},{7,23},{8,24},{9,... | collective-permute-start | bytes 208904 | tf_op jit(solution)/shard_map/sum4/ppermute | solution.py:70
  67.2 6.4 %collective-permute-start.18 = (bf16[136,256]{1,0:T(8,128)(2,1)S(1)}, bf16[136,256]{1,0:T(8,128)(2,1)S(1)}, u32[]{:S(2)}, u32[]{:S(2)}) collective-permute-start(bf16[136,256]{1,0:T(8,128)(2,1)S(1)} %add_convert_fusion), channel_id=1, source_target_pairs={{0,24},{1,25},{2,26},{3,27},{4,28},{5,29},{6,30},{7,31},{8,16},{9,... | collective-permute-start | bytes 208904 | tf_op jit(solution)/shard_map/sum5/ppermute | solution.py:70
  73.7 1.4 %collective-permute-start.19 = (f32[136,256]{1,0:T(8,128)S(1)}, f32[136,256]{1,0:T(8,128)S(1)}, u32[]{:S(2)}, u32[]{:S(2)}) collective-permute-start(f32[136,256]{1,0:T(8,128)S(1)} %add_add_fusion.part), channel_id=1, source_target_pairs={{0,1},{1,0},{2,3},{3,2},{4,5},{5,4},{6,7},{7,6},{8,9},{9,8},{10,11... | collective-permute-start | bytes 417800 | tf_op jit(solution)/shard_map/back/ppermute | solution.py:75
  (2 other events, 4.4 us)

commit v2 on v1

--- a/solution.py
+++ b/solution.py
@@ -179,22 +179,25 @@
 
 
 def add_group(entries, lo, hi, tiles, blocks, acc):
-    def step(j, carry):
-        m = lo + 2 * j
-        e0, e1 = entries[m], entries[m + 1]
-
-        def product(e, m):
-            at = pl.multiple_of(((e >> 8) & 15) * 128, 128)
-            return jnp.dot(
-                tiles[m], blocks[pl.ds(at, 128), :], preferred_element_type=jnp.float32
-            )
-
-        p0, p1 = product(e0, m), product(e1, m + 1)
-        acc[e0 >> 12] += p0
-        acc[e1 >> 12] += p1
+    def product(m):
+        at = pl.multiple_of(((entries[m] >> 8) & 15) * 128, 128)
+        return jnp.dot(tiles[m], blocks[pl.ds(at, 128), :], preferred_element_type=jnp.float32)
+
+    def add(first, count):
+        products = [product(first + i) for i in range(count)]
+        for i, p in enumerate(products):
+            acc[entries[first + i] >> 12] += p
+
+    def four(j, carry):
+        add(lo + 4 * j, 4)
         return carry
 
-    lax.fori_loop(0, (hi - lo) // 2, step, 0)
+    fours = (hi - lo) // 4
+    lax.fori_loop(0, fours, four, 0)
+
+    @pl.when((hi - lo) % 4 != 0)
+    def _():
+        add(lo + 4 * fours, 2)
 
 
 def add_kernel(groups, fresh, entries, starts, tiles, *refs):
@@ -328,15 +331,16 @@
     pair0 = join(features, r0)
     q0 = second_hop(pair0, "q0")
     other_tiles = swap(adj_tiles, "tiles")
-    z1, again = after(z1, features)
+    pair0, again = after(pair0, features)
     z3 = along_z(again, 3, "z3")
+    z1, index = after(z1, index)
     pair1 = join(z1, first_hop(z1, "r1"))
     q1 = along_z(q0, 1, "q1")
-    z2, q0, other_tiles = after(z2, q0, other_tiles)
+    z2, other_tiles = after(z2, other_tiles)
     pair2 = join(z2, first_hop(z2, "r2"))
     pair2, other_tiles = after(pair2, other_tiles)
     q2 = second_hop(pair2, "q2")
-    z3, pair1, pair2 = after(z3, pair1, pair2)
+    z3, pair1, pair2, q0 = after(z3, pair1, pair2, q0)
     pair3 = join(z3, first_hop(z3, "r3"))
     q3 = second_hop(pair3, "q3")
     entries, starts = work_list(index, slots, row_blocks)

time: 76.3 us -> 73.8 us (0.967)
  waiting for transfers between devices: 35.9 us -> 31.9 us
  starting transfers between devices: 22.8 us -> 25.4 us
  Pallas kernels: 11.1 us -> 10.1 us
    ppermute x16, waiting for transfers between devices: 31.4 us -> 27.5 us  [send(): return lax.ppermute(x, BOTH, perm)]
    ppermute x16, starting transfers between devices: 22 us -> 24.6 us  [send(): return lax.ppermute(x, BOTH, perm)]
    pallas_call x3, Pallas kernels: 5.98 us -> 4.96 us  [add_groups(): pl.pallas_call(functools.partial(add_kernel, groups, fresh), out_shape=sh...]
  transfers between devices with their start and end apart: 20 -> 20, of which waited for: 11 -> 12; matrix products, arithmetic and copies ran while one was open for 3% -> 3% of each run, Pallas kernels for 11% -> 10%
where the time goes in v2:
time: 73.8 us; the launch traced here: 73.4 us
  waiting for transfers between devices  31.9 us (43%)
  starting transfers between devices  25.4 us (34%)
  Pallas kernels  10.1 us (14%)
  blocking collectives  1.98 us (3%)
  local copies, waits for them, and re-layouts  1.74 us (2%)
  other arithmetic  1.44 us (2%)
  between operations  0.87 us (1%)
    ppermute x16, waiting for transfers between devices, send(): return lax.ppermute(x, BOTH, perm)  27.5 us
    ppermute x16, starting transfers between devices, send(): return lax.ppermute(x, BOTH, perm)  24.6 us
    pallas_call x3, Pallas kernels, add_groups(): pl.pallas_call(functools.partial(add_kernel, groups, fresh), out_shape=sh...  4.96 us
    ppermute x4, waiting for transfers between devices, swap(): return lax.ppermute(x, 'replica', [(0, 1), (1, 0)])  4.47 us
    pallas_call x1, Pallas kernels, gather_tiles(): pl.pallas_call(functools.partial(gather_kernel, own.shape[0]), out_shape=...  2.19 us
    all_gather x1, blocking collectives, shards(): index = lax.all_gather(index, 'replica', axis=0, tiled=True)  1.98 us
    unnamed x14, local copies, waits for them, and re-layouts  1.7 us
  transfers between devices with their start and end apart: 20, of which 12 were waited for; matrix products, arithmetic and copies ran while one was open for 3% of the time, Pallas kernels for 10%

profile of v2, /device:TPU:0, one launch (start us, length us, event | category | flops | bytes accessed | tf_op | source)
XLA Modules:
  0.0 73.4 jit_solution(17494923149713417357)
XLA Ops:
  1.1 2.6 %collective-permute-start.1 = (bf16[512,256]{1,0:T(8,128)(2,1)}, bf16[512,256]{1,0:T(8,128)(2,1)S(1)}, u32[]{:S(2)}, u32[]{:S(2)}) collective-permute-start(bf16[512,256]{1,0:T(8,128)(2,1)} %param.6), channel_id=1, source_target_pairs={{0,2},{1,5},{2,0},{3,7},{4,6},{5,1},{6,4},{7,3},{8,10},{9,13},{10,... | collective-permute-start | bytes 786440 | tf_op jit(solution)/shard_map/r0/ppermute | solution.py:70
  3.7 1.6 %collective-permute-start = (bf16[512,256]{1,0:T(8,128)(2,1)}, bf16[512,256]{1,0:T(8,128)(2,1)S(1)}, u32[]{:S(2)}, u32[]{:S(2)}) collective-permute-start(bf16[512,256]{1,0:T(8,128)(2,1)} %param.6), channel_id=1, source_target_pairs={{0,8},{1,9},{2,10},{3,11},{4,12},{5,13},{6,14},{7,15},{8,0},{9,1},... | collective-permute-start | bytes 786440 | tf_op jit(solution)/shard_map/z1/ppermute | solution.py:70
  5.3 2.6 %collective-permute-start.2 = (bf16[512,256]{1,0:T(8,128)(2,1)}, bf16[512,256]{1,0:T(8,128)(2,1)S(1)}, u32[]{:S(2)}, u32[]{:S(2)}) collective-permute-start(bf16[512,256]{1,0:T(8,128)(2,1)} %param.6), channel_id=1, source_target_pairs={{0,16},{1,17},{2,18},{3,19},{4,20},{5,21},{6,22},{7,23},{8,24},{9,... | collective-permute-start | bytes 786440 | tf_op jit(solution)/shard_map/z2/ppermute | solution.py:70
  8.9 1.6 %collective-permute-start.7 = (bf16[1024,256]{1,0:T(8,128)(2,1)S(1)}, bf16[1024,256]{1,0:T(8,128)(2,1)S(1)}, u32[]{:S(2)}, u32[]{:S(2)}) collective-permute-start(bf16[1024,256]{1,0:T(8,128)(2,1)S(1)} %constant_dynamic-update-slice_fusion.refs_0_), channel_id=1, source_target_pairs={{0,4},{1,3},{2,6},{3,1},{4,0},{5,7},{6,2},{7,5},{8,12},{9,11},{10,... | collective-permute-start | bytes 1572872 | tf_op jit(solution)/shard_map/q0/ppermute | solution.py:70
  10.5 2.0 %all_gather.3 = s32[256,2]{0,1:T(2,128)S(1)} all-gather(s32[128,2]{0,1:T(2,128)} %param.8), channel_id=1, replica_groups=mesh['section'=16,'replica'=2] {'replica'}, dimensions={0}, use_global_device_ids=true | all-gather | bytes 3072 | tf_op jit(solution)/shard_map/all_gather | solution.py:330
  12.5 5.3 %collective-permute-done = bf16[512,256]{1,0:T(8,128)(2,1)S(1)} collective-permute-done((bf16[512,256]{1,0:T(8,128)(2,1)}, bf16[512,256]{1,0:T(8,128)(2,1)S(1)}, u32[]{:S(2)}, u32[]{:S(2)}) %collective-permute-start) | collective-permute-done | bytes 262176 | tf_op jit(solution)/shard_map/z1/ppermute | solution.py:70
  18.0 3.3 %collective-permute-start.5 = (bf16[512,256]{1,0:T(8,128)(2,1)}, bf16[512,256]{1,0:T(8,128)(2,1)S(1)}, u32[]{:S(2)}, u32[]{:S(2)}) collective-permute-start(bf16[512,256]{1,0:T(8,128)(2,1)} %param.6), channel_id=1, source_target_pairs={{0,24},{1,25},{2,26},{3,27},{4,28},{5,29},{6,30},{7,31},{8,16},{9,... | collective-permute-start | bytes 786440 | tf_op jit(solution)/shard_map/z3/ppermute | solution.py:70
  24.3 4.2 %collective-permute-done.4 = bf16[512,256]{1,0:T(8,128)(2,1)S(1)} collective-permute-done((bf16[512,256]{1,0:T(8,128)(2,1)S(1)}, bf16[512,256]{1,0:T(8,128)(2,1)S(1)}, u32[]{:S(2)}, u32[]{:S(2)}) %collective-permute-start.4) | collective-permute-done | bytes 262176 | tf_op jit(solution)/shard_map/r2/ppermute | solution.py:70
  30.1 2.2 %gather_tiles.1.tiles = bf16[272,128,128]{2,1,0:T(8,128)(2,1)S(1)} custom-call(s32[272]{0:T(512)} %broadcast_add_fusion.entries, s32[9]{0:T(128)} %copy-done.3, bf16[128,128,128]{2,1,0:T(8,128)(2,1)} %own.1, bf16[128,128,128]{2,1,0:T(8,128)(2,1)} %collective-permute-done.3.other), custom_call_target="tpu_custom_call" | custom-call | bytes 1024 | tf_op jit(solution)/shard_map/gather_tiles/pallas_call | solution.py:169
  33.0 2.5 %add_a.1.refs_2_ = f32[9,128,256]{2,1,0:T(8,128)S(1)} custom-call(s32[272]{0:T(512)S(1)} %copy-done.2, s32[9]{0:T(128)S(1)} %copy-done.4, bf16[272,128,128]{2,1,0:T(8,128)(2,1)S(1)} %gather_tiles.1.tiles, bf16[1024,256]{1,0:T(8,128)(2,1)S(1)} %constant_dynamic-update-slice_fusion.refs_0_, bf16[1024,256]{1,0:T(8,128)(2,1)S(1)} %collective-permute-done.7.refs_1_, ...), custom_call_target="tpu_custom_call" | custom-call | flops 4294967296 | bytes 4194304 | tf_op jit(solution)/shard_map/add_a/pallas_call | solution.py:227
  35.5 1.7 %collective-permute-done.8 = bf16[512,256]{1,0:T(8,128)(2,1)S(1)} collective-permute-done((bf16[512,256]{1,0:T(8,128)(2,1)S(1)}, bf16[512,256]{1,0:T(8,128)(2,1)S(1)}, u32[]{:S(2)}, u32[]{:S(2)}) %collective-permute-start.8) | collective-permute-done | bytes 262176 | tf_op jit(solution)/shard_map/r3/ppermute | solution.py:70
  37.2 1.6 %collective-permute-start.9 = (bf16[1024,256]{1,0:T(8,128)(2,1)S(1)}, bf16[1024,256]{1,0:T(8,128)(2,1)S(1)}, u32[]{:S(2)}, u32[]{:S(2)}) collective-permute-start(bf16[1024,256]{1,0:T(8,128)(2,1)S(1)} %constant_dynamic-update-slice_fusion.2.refs_1_), channel_id=1, source_target_pairs={{0,4},{1,3},{2,6},{3,1},{4,0},{5,7},{6,2},{7,5},{8,12},{9,11},{10,... | collective-permute-start | bytes 1572872 | tf_op jit(solution)/shard_map/q3/ppermute | solution.py:70
  40.1 1.2 %add_c.1.refs_1_ = f32[9,128,256]{2,1,0:T(8,128)S(1)} custom-call(s32[272]{0:T(512)S(1)} %copy-done.2, s32[9]{0:T(128)S(1)} %copy-done.4, bf16[272,128,128]{2,1,0:T(8,128)(2,1)S(1)} %gather_tiles.1.tiles, bf16[1024,256]{1,0:T(8,128)(2,1)S(1)} %collective-permute-done.10.refs_0_, ...), custom_call_target="tpu_custom_call", output_to_operand_aliasing={{}: (5, {})} | custom-call | flops 4294967296 | bytes 4194304 | tf_op jit(solution)/shard_map/add_c/pallas_call | solution.py:227
  41.4 5.1 %collective-permute-done.9.refs_0_ = bf16[1024,256]{1,0:T(8,128)(2,1)S(1)} collective-permute-done((bf16[1024,256]{1,0:T(8,128)(2,1)S(1)}, bf16[1024,256]{1,0:T(8,128)(2,1)S(1)}, u32[]{:S(2)}, u32[]{:S(2)}) %collective-permute-start.9) | collective-permute-done | bytes 524320 | tf_op jit(solution)/shard_map/q3/ppermute | solution.py:70
  47.6 1.9 %collective-permute-done.12.theirs = f32[4,128,256]{2,1,0:T(8,128)S(1)} collective-permute-done((f32[4,128,256]{2,1,0:T(8,128)S(1)}, f32[4,128,256]{2,1,0:T(8,128)S(1)}, u32[]{:S(2)}, u32[]{:S(2)}) %collective-permute-start.12) | collective-permute-done | bytes 524320 | tf_op jit(solution)/shard_map/rows/ppermute | solution.py:75
  52.1 2.4 %collective-permute-start.14 = (f32[136,256]{1,0:T(8,128)S(1)}, f32[136,256]{1,0:T(8,128)S(1)}, u32[]{:S(2)}, u32[]{:S(2)}) collective-permute-start(f32[136,256]{1,0:T(8,128)S(1)} %add.135), channel_id=1, source_target_pairs={{0,2},{1,5},{2,0},{3,7},{4,6},{5,1},{6,4},{7,3},{8,10},{9,13},{10,... | collective-permute-start | bytes 417800 | tf_op jit(solution)/shard_map/sum1/ppermute | solution.py:70
  54.5 3.0 %collective-permute-done.14 = f32[136,256]{1,0:T(8,128)S(1)} collective-permute-done((f32[136,256]{1,0:T(8,128)S(1)}, f32[136,256]{1,0:T(8,128)S(1)}, u32[]{:S(2)}, u32[]{:S(2)}) %collective-permute-start.14) | collective-permute-done | bytes 139296 | tf_op jit(solution)/shard_map/sum1/ppermute | solution.py:70
  57.5 1.5 %collective-permute-start.15 = (f32[136,256]{1,0:T(8,128)S(1)}, f32[136,256]{1,0:T(8,128)S(1)}, u32[]{:S(2)}, u32[]{:S(2)}) collective-permute-start(f32[136,256]{1,0:T(8,128)S(1)} %add.136), channel_id=1, source_target_pairs={{0,4},{1,3},{2,6},{3,1},{4,0},{5,7},{6,2},{7,5},{8,12},{9,11},{10,... | collective-permute-start | bytes 417800 | tf_op jit(solution)/shard_map/sum2/ppermute | solution.py:70
  59.1 3.6 %collective-permute-done.15 = f32[136,256]{1,0:T(8,128)S(1)} collective-permute-done((f32[136,256]{1,0:T(8,128)S(1)}, f32[136,256]{1,0:T(8,128)S(1)}, u32[]{:S(2)}, u32[]{:S(2)}) %collective-permute-start.15) | collective-permute-done | bytes 139296 | tf_op jit(solution)/shard_map/sum2/ppermute | solution.py:70
  63.6 1.4 %collective-permute-start.17 = (bf16[136,256]{1,0:T(8,128)(2,1)S(1)}, bf16[136,256]{1,0:T(8,128)(2,1)S(1)}, u32[]{:S(2)}, u32[]{:S(2)}) collective-permute-start(bf16[136,256]{1,0:T(8,128)(2,1)S(1)} %add_convert_fusion), channel_id=1, source_target_pairs={{0,16},{1,17},{2,18},{3,19},{4,20},{5,21},{6,22},{7,23},{8,24},{9,... | collective-permute-start | bytes 208904 | tf_op jit(solution)/shard_map/sum4/ppermute | solution.py:70
  65.0 2.1 %collective-permute-start.18 = (bf16[136,256]{1,0:T(8,128)(2,1)S(1)}, bf16[136,256]{1,0:T(8,128)(2,1)S(1)}, u32[]{:S(2)}, u32[]{:S(2)}) collective-permute-start(bf16[136,256]{1,0:T(8,128)(2,1)S(1)} %add_convert_fusion), channel_id=1, source_target_pairs={{0,24},{1,25},{2,26},{3,27},{4,28},{5,29},{6,30},{7,31},{8,16},{9,... | collective-permute-start | bytes 208904 | tf_op jit(solution)/shard_map/sum5/ppermute | solution.py:70
  67.1 2.6 %collective-permute-done.17 = bf16[136,256]{1,0:T(8,128)(2,1)S(1)} collective-permute-done((bf16[136,256]{1,0:T(8,128)(2,1)S(1)}, bf16[136,256]{1,0:T(8,128)(2,1)S(1)}, u32[]{:S(2)}, u32[]{:S(2)}) %collective-permute-start.17) | collective-permute-done | bytes 69664 | tf_op jit(solution)/shard_map/sum4/ppermute | solution.py:70
  69.7 1.5 %collective-permute-done.18 = bf16[136,256]{1,0:T(8,128)(2,1)S(1)} collective-permute-done((bf16[136,256]{1,0:T(8,128)(2,1)S(1)}, bf16[136,256]{1,0:T(8,128)(2,1)S(1)}, u32[]{:S(2)}, u32[]{:S(2)}) %collective-permute-start.18) | collective-permute-done | bytes 69664 | tf_op jit(solution)/shard_map/sum5/ppermute | solution.py:70
  71.3 1.3 %collective-permute-done.19.rest = f32[136,256]{1,0:T(8,128)S(1)} collective-permute-done((f32[136,256]{1,0:T(8,128)S(1)}, f32[136,256]{1,0:T(8,128)S(1)}, u32[]{:S(2)}, u32[]{:S(2)}) %collective-permute-start.19) | collective-permute-done | bytes 139296 | tf_op jit(solution)/shard_map/back/ppermute | solution.py:75
  (58 shorter events, 13.8 us)
Async XLA Ops:
  0.6 21.4 %collective-permute-start.3 = (bf16[128,128,128]{2,1,0:T(8,128)(2,1)}, bf16[128,128,128]{2,1,0:T(8,128)(2,1)}, u32[]{:S(2)}, u32[]{:S(2)}) collective-permute-start(bf16[128,128,128]{2,1,0:T(8,128)(2,1)} %own.1), channel_id=1, source_target_pairs={{0,1},{1,0},{2,3},{3,2},{4,5},{5,4},{6,7},{7,6},{8,9},{9,8},{10,11... | collective-permute-start | bytes 12582920 | tf_op jit(solution)/shard_map/tiles/ppermute | solution.py:75
  1.1 7.7 %collective-permute-start.1 = (bf16[512,256]{1,0:T(8,128)(2,1)}, bf16[512,256]{1,0:T(8,128)(2,1)S(1)}, u32[]{:S(2)}, u32[]{:S(2)}) collective-permute-start(bf16[512,256]{1,0:T(8,128)(2,1)} %param.6), channel_id=1, source_target_pairs={{0,2},{1,5},{2,0},{3,7},{4,6},{5,1},{6,4},{7,3},{8,10},{9,13},{10,... | collective-permute-start | bytes 786440 | tf_op jit(solution)/shard_map/r0/ppermute | solution.py:70
  3.7 14.1 %collective-permute-start = (bf16[512,256]{1,0:T(8,128)(2,1)}, bf16[512,256]{1,0:T(8,128)(2,1)S(1)}, u32[]{:S(2)}, u32[]{:S(2)}) collective-permute-start(bf16[512,256]{1,0:T(8,128)(2,1)} %param.6), channel_id=1, source_target_pairs={{0,8},{1,9},{2,10},{3,11},{4,12},{5,13},{6,14},{7,15},{8,0},{9,1},... | collective-permute-start | bytes 786440 | tf_op jit(solution)/shard_map/z1/ppermute | solution.py:70
  5.3 16.7 %collective-permute-start.2 = (bf16[512,256]{1,0:T(8,128)(2,1)}, bf16[512,256]{1,0:T(8,128)(2,1)S(1)}, u32[]{:S(2)}, u32[]{:S(2)}) collective-permute-start(bf16[512,256]{1,0:T(8,128)(2,1)} %param.6), channel_id=1, source_target_pairs={{0,16},{1,17},{2,18},{3,19},{4,20},{5,21},{6,22},{7,23},{8,24},{9,... | collective-permute-start | bytes 786440 | tf_op jit(solution)/shard_map/z2/ppermute | solution.py:70
  8.9 15.3 %collective-permute-start.7 = (bf16[1024,256]{1,0:T(8,128)(2,1)S(1)}, bf16[1024,256]{1,0:T(8,128)(2,1)S(1)}, u32[]{:S(2)}, u32[]{:S(2)}) collective-permute-start(bf16[1024,256]{1,0:T(8,128)(2,1)S(1)} %constant_dynamic-update-slice_fusion.refs_0_), channel_id=1, source_target_pairs={{0,4},{1,3},{2,6},{3,1},{4,0},{5,7},{6,2},{7,5},{8,12},{9,11},{10,... | collective-permute-start | bytes 1572872 | tf_op jit(solution)/shard_map/q0/ppermute | solution.py:70
  17.8 6.4 %collective-permute-start.6 = (bf16[512,256]{1,0:T(8,128)(2,1)S(1)}, bf16[512,256]{1,0:T(8,128)(2,1)S(1)}, u32[]{:S(2)}, u32[]{:S(2)}) collective-permute-start(bf16[512,256]{1,0:T(8,128)(2,1)S(1)} %collective-permute-done), channel_id=1, source_target_pairs={{0,2},{1,5},{2,0},{3,7},{4,6},{5,1},{6,4},{7,3},{8,10},{9,13},{10,... | collective-permute-start | bytes 786440 | tf_op jit(solution)/shard_map/r1/ppermute | solution.py:70
  18.0 11.6 %collective-permute-start.5 = (bf16[512,256]{1,0:T(8,128)(2,1)}, bf16[512,256]{1,0:T(8,128)(2,1)S(1)}, u32[]{:S(2)}, u32[]{:S(2)}) collective-permute-start(bf16[512,256]{1,0:T(8,128)(2,1)} %param.6), channel_id=1, source_target_pairs={{0,24},{1,25},{2,26},{3,27},{4,28},{5,29},{6,30},{7,31},{8,16},{9,... | collective-permute-start | bytes 786440 | tf_op jit(solution)/shard_map/z3/ppermute | solution.py:70
  21.6 8.6 %copy-start.3 = (s32[9]{0:T(128)}, s32[9]{0:T(128)S(1)}, u32[]{:S(2)}) copy-start(s32[9]{0:T(128)S(1)} %select_reduce_fusion.2.starts) | copy-start | bytes 112
  22.0 6.4 %collective-permute-start.4 = (bf16[512,256]{1,0:T(8,128)(2,1)S(1)}, bf16[512,256]{1,0:T(8,128)(2,1)S(1)}, u32[]{:S(2)}, u32[]{:S(2)}) collective-permute-start(bf16[512,256]{1,0:T(8,128)(2,1)S(1)} %collective-permute-done.2), channel_id=1, source_target_pairs={{0,2},{1,5},{2,0},{3,7},{4,6},{5,1},{6,4},{7,3},{8,10},{9,13},{10,... | collective-permute-start | bytes 786440 | tf_op jit(solution)/shard_map/r2/ppermute | solution.py:70
  24.2 14.6 %collective-permute-start.11 = (bf16[1024,256]{1,0:T(8,128)(2,1)S(1)}, bf16[1024,256]{1,0:T(8,128)(2,1)S(1)}, u32[]{:S(2)}, u32[]{:S(2)}) collective-permute-start(bf16[1024,256]{1,0:T(8,128)(2,1)S(1)} %collective-permute-done.7.refs_1_), channel_id=1, source_target_pairs={{0,8},{1,9},{2,10},{3,11},{4,12},{5,13},{6,14},{7,15},{8,0},{9,1},... | collective-permute-start | bytes 1572872 | tf_op jit(solution)/shard_map/q1/ppermute | solution.py:70
  28.5 11.6 %collective-permute-start.10 = (bf16[1024,256]{1,0:T(8,128)(2,1)S(1)}, bf16[1024,256]{1,0:T(8,128)(2,1)S(1)}, u32[]{:S(2)}, u32[]{:S(2)}) collective-permute-start(bf16[1024,256]{1,0:T(8,128)(2,1)S(1)} %pad_maximum_fusion.refs_1_), channel_id=1, source_target_pairs={{0,4},{1,3},{2,6},{3,1},{4,0},{5,7},{6,2},{7,5},{8,12},{9,11},{10,... | collective-permute-start | bytes 1572872 | tf_op jit(solution)/shard_map/q2/ppermute | solution.py:70
  29.6 7.6 %collective-permute-start.8 = (bf16[512,256]{1,0:T(8,128)(2,1)S(1)}, bf16[512,256]{1,0:T(8,128)(2,1)S(1)}, u32[]{:S(2)}, u32[]{:S(2)}) collective-permute-start(bf16[512,256]{1,0:T(8,128)(2,1)S(1)} %collective-permute-done.5), channel_id=1, source_target_pairs={{0,2},{1,5},{2,0},{3,7},{4,6},{5,1},{6,4},{7,3},{8,10},{9,13},{10,... | collective-permute-start | bytes 786440 | tf_op jit(solution)/shard_map/r3/ppermute | solution.py:70
  37.2 9.2 %collective-permute-start.9 = (bf16[1024,256]{1,0:T(8,128)(2,1)S(1)}, bf16[1024,256]{1,0:T(8,128)(2,1)S(1)}, u32[]{:S(2)}, u32[]{:S(2)}) collective-permute-start(bf16[1024,256]{1,0:T(8,128)(2,1)S(1)} %constant_dynamic-update-slice_fusion.2.refs_1_), channel_id=1, source_target_pairs={{0,4},{1,3},{2,6},{3,1},{4,0},{5,7},{6,2},{7,5},{8,12},{9,11},{10,... | collective-permute-start | bytes 1572872 | tf_op jit(solution)/shard_map/q3/ppermute | solution.py:70
  41.4 8.2 %copy-start = (bf16[512,256]{1,0:T(8,128)(2,1)S(1)}, bf16[512,256]{1,0:T(8,128)(2,1)}, u32[]{:S(2)}) copy-start(bf16[512,256]{1,0:T(8,128)(2,1)} %grad_out.1) | copy-start | bytes 786436
  41.4 8.2 %copy-start.1 = (bf16[256,256]{1,0:T(8,128)(2,1)S(1)}, bf16[256,256]{1,0:T(8,128)(2,1)}, u32[]{:S(2)}) copy-start(bf16[256,256]{1,0:T(8,128)(2,1)} %weight.1) | copy-start | bytes 393220
  41.4 8.2 %copy-start.5 = (f32[256]{0:T(256)S(1)}, f32[256]{0:T(256)}, u32[]{:S(2)}) copy-start(f32[256]{0:T(256)} %param.10) | copy-start | bytes 3076
  47.6 2.0 %collective-permute-start.12 = (f32[4,128,256]{2,1,0:T(8,128)S(1)}, f32[4,128,256]{2,1,0:T(8,128)S(1)}, u32[]{:S(2)}, u32[]{:S(2)}) collective-permute-start(f32[4,128,256]{2,1,0:T(8,128)S(1)} %get-tuple-element.39), channel_id=1, source_target_pairs={{0,1},{1,0},{2,3},{3,2},{4,5},{5,4},{6,7},{7,6},{8,9},{9,8},{10,11... | collective-permute-start | bytes 1572872 | tf_op jit(solution)/shard_map/rows/ppermute | solution.py:75
  50.7 1.4 %collective-permute-start.13 = (f32[136,256]{1,0:T(8,128)S(1)}, f32[136,256]{1,0:T(8,128)S(1)}, u32[]{:S(2)}, u32[]{:S(2)}) collective-permute-start(f32[136,256]{1,0:T(8,128)S(1)} %get-tuple-element.42), channel_id=1, source_target_pairs={{0,1},{1,0},{2,3},{3,2},{4,5},{5,4},{6,7},{7,6},{8,9},{9,8},{10,11... | collective-permute-start | bytes 417800 | tf_op jit(solution)/shard_map/halves/ppermute | solution.py:75
  52.1 5.4 %collective-permute-start.14 = (f32[136,256]{1,0:T(8,128)S(1)}, f32[136,256]{1,0:T(8,128)S(1)}, u32[]{:S(2)}, u32[]{:S(2)}) collective-permute-start(f32[136,256]{1,0:T(8,128)S(1)} %add.135), channel_id=1, source_target_pairs={{0,2},{1,5},{2,0},{3,7},{4,6},{5,1},{6,4},{7,3},{8,10},{9,13},{10,... | collective-permute-start | bytes 417800 | tf_op jit(solution)/shard_map/sum1/ppermute | solution.py:70
  57.5 5.1 %collective-permute-start.15 = (f32[136,256]{1,0:T(8,128)S(1)}, f32[136,256]{1,0:T(8,128)S(1)}, u32[]{:S(2)}, u32[]{:S(2)}) collective-permute-start(f32[136,256]{1,0:T(8,128)S(1)} %add.136), channel_id=1, source_target_pairs={{0,4},{1,3},{2,6},{3,1},{4,0},{5,7},{6,2},{7,5},{8,12},{9,11},{10,... | collective-permute-start | bytes 417800 | tf_op jit(solution)/shard_map/sum2/ppermute | solution.py:70
  62.7 4.5 %collective-permute-start.16 = (bf16[136,256]{1,0:T(8,128)(2,1)S(1)}, bf16[136,256]{1,0:T(8,128)(2,1)S(1)}, u32[]{:S(2)}, u32[]{:S(2)}) collective-permute-start(bf16[136,256]{1,0:T(8,128)(2,1)S(1)} %add_convert_fusion), channel_id=1, source_target_pairs={{0,8},{1,9},{2,10},{3,11},{4,12},{5,13},{6,14},{7,15},{8,0},{9,1},... | collective-permute-start | bytes 208904 | tf_op jit(solution)/shard_map/sum3/ppermute | solution.py:70
  63.6 6.1 %collective-permute-start.17 = (bf16[136,256]{1,0:T(8,128)(2,1)S(1)}, bf16[136,256]{1,0:T(8,128)(2,1)S(1)}, u32[]{:S(2)}, u32[]{:S(2)}) collective-permute-start(bf16[136,256]{1,0:T(8,128)(2,1)S(1)} %add_convert_fusion), channel_id=1, source_target_pairs={{0,16},{1,17},{2,18},{3,19},{4,20},{5,21},{6,22},{7,23},{8,24},{9,... | collective-permute-start | bytes 208904 | tf_op jit(solution)/shard_map/sum4/ppermute | solution.py:70
  65.0 6.2 %collective-permute-start.18 = (bf16[136,256]{1,0:T(8,128)(2,1)S(1)}, bf16[136,256]{1,0:T(8,128)(2,1)S(1)}, u32[]{:S(2)}, u32[]{:S(2)}) collective-permute-start(bf16[136,256]{1,0:T(8,128)(2,1)S(1)} %add_convert_fusion), channel_id=1, source_target_pairs={{0,24},{1,25},{2,26},{3,27},{4,28},{5,29},{6,30},{7,31},{8,16},{9,... | collective-permute-start | bytes 208904 | tf_op jit(solution)/shard_map/sum5/ppermute | solution.py:70
  71.2 1.4 %collective-permute-start.19 = (f32[136,256]{1,0:T(8,128)S(1)}, f32[136,256]{1,0:T(8,128)S(1)}, u32[]{:S(2)}, u32[]{:S(2)}) collective-permute-start(f32[136,256]{1,0:T(8,128)S(1)} %add_add_fusion.part), channel_id=1, source_target_pairs={{0,1},{1,0},{2,3},{3,2},{4,5},{5,4},{6,7},{7,6},{8,9},{9,8},{10,11... | collective-permute-start | bytes 417800 | tf_op jit(solution)/shard_map/back/ppermute | solution.py:75
  (2 other events, 4.5 us)

commit v3 on v2

--- a/solution.py
+++ b/solution.py
@@ -97,6 +97,18 @@
 
 def after(*arrays):
     return lax.optimization_barrier(arrays)
+
+
+def narrow(x):
+    return x.astype(jnp.bfloat16)
+
+
+def rounded(x):
+    return lax.reduce_precision(x, 8, 7)
+
+
+def widen(x):
+    return x.astype(jnp.float32)
 
 
 def work_list(index, slots, row_blocks):
@@ -353,12 +365,15 @@
     theirs = swap(give, "rows")
     output, keep, give = dense(core, mine, theirs, weight, bias_vec, grad_out)
     part = keep + swap(give, "halves")
-    part = part + first_hop(part, "sum1")
-    part = part + second_hop(part, "sum2")
+    low = narrow(part)
+    near = widen(first_hop(low, "sum1"))
+    far = widen(second_hop(low, "sum2"))
+    across = widen(diagonal(low, "sumd"))
+    part = (rounded(part) + across) + (near + far)
     low_part = part.astype(jnp.bfloat16)
     z_parts = [lax.reduce_precision(part, 8, 7)]
-    z_parts += [along_z(low_part, k, f"sum{2 + k}").astype(jnp.float32) for k in (1, 2, 3)]
-    part = (z_parts[0] + z_parts[1]) + (z_parts[2] + z_parts[3])
+    z_parts += [along_z(low_part, k, f"sum{2 + k}").astype(jnp.float32) for k in (3, 2, 1)]
+    part = (z_parts[0] + z_parts[3]) + (z_parts[2] + z_parts[1])
     rest = swap(part, "back")
     grad_weight, grad_bias = finish(core, part, rest)
     return output, grad_weight, grad_bias.reshape(bias_vec.shape)

time: 73.8 us -> 71 us (0.962)
  waiting for transfers between devices: 31.9 us -> 30 us
    ppermute x16 -> x17, waiting for transfers between devices: 27.5 us -> 25.6 us  [send(): return lax.ppermute(x, BOTH, perm)]
    ppermute x16 -> x17, starting transfers between devices: 24.6 us -> 23.9 us  [send(): return lax.ppermute(x, BOTH, perm)]
  transfers between devices with their start and end apart: 20 -> 21, of which waited for: 12 -> 12; matrix products, arithmetic and copies ran while one was open for 3% -> 3% of each run, Pallas kernels for 10% -> 10%
where the time goes in v3:
time: 71 us; the launch traced here: 70.6 us
  waiting for transfers between devices  30 us (42%)
  starting transfers between devices  24.7 us (35%)
  Pallas kernels  9.81 us (14%)
  blocking collectives  1.98 us (3%)
  local copies, waits for them, and re-layouts  1.74 us (2%)
  other arithmetic  1.45 us (2%)
  between operations  0.87 us (1%)
    ppermute x17, waiting for transfers between devices, send(): return lax.ppermute(x, BOTH, perm)  25.6 us
    ppermute x17, starting transfers between devices, send(): return lax.ppermute(x, BOTH, perm)  23.9 us
    pallas_call x3, Pallas kernels, add_groups(): pl.pallas_call(functools.partial(add_kernel, groups, fresh), out_shape=sh...  4.73 us
    ppermute x4, waiting for transfers between devices, swap(): return lax.ppermute(x, 'replica', [(0, 1), (1, 0)])  4.47 us
    pallas_call x1, Pallas kernels, gather_tiles(): pl.pallas_call(functools.partial(gather_kernel, own.shape[0]), out_shape=...  2.14 us
    all_gather x1, blocking collectives, shards(): index = lax.all_gather(index, 'replica', axis=0, tiled=True)  1.98 us
    unnamed x14, local copies, waits for them, and re-layouts  1.7 us
  transfers between devices with their start and end apart: 21, of which 12 were waited for; matrix products, arithmetic and copies ran while one was open for 3% of the time, Pallas kernels for 10%

profile of v3, /device:TPU:0, one launch (start us, length us, event | category | flops | bytes accessed | tf_op | source)
XLA Modules:
  0.0 70.6 jit_solution(7623612932612364449)
XLA Ops:
  1.1 2.6 %collective-permute-start.1 = (bf16[512,256]{1,0:T(8,128)(2,1)}, bf16[512,256]{1,0:T(8,128)(2,1)S(1)}, u32[]{:S(2)}, u32[]{:S(2)}) collective-permute-start(bf16[512,256]{1,0:T(8,128)(2,1)} %param.6), channel_id=1, source_target_pairs={{0,2},{1,5},{2,0},{3,7},{4,6},{5,1},{6,4},{7,3},{8,10},{9,13},{10,... | collective-permute-start | bytes 786440 | tf_op jit(solution)/shard_map/r0/ppermute | solution.py:70
  3.7 1.6 %collective-permute-start = (bf16[512,256]{1,0:T(8,128)(2,1)}, bf16[512,256]{1,0:T(8,128)(2,1)S(1)}, u32[]{:S(2)}, u32[]{:S(2)}) collective-permute-start(bf16[512,256]{1,0:T(8,128)(2,1)} %param.6), channel_id=1, source_target_pairs={{0,8},{1,9},{2,10},{3,11},{4,12},{5,13},{6,14},{7,15},{8,0},{9,1},... | collective-permute-start | bytes 786440 | tf_op jit(solution)/shard_map/z1/ppermute | solution.py:70
  5.3 2.6 %collective-permute-start.2 = (bf16[512,256]{1,0:T(8,128)(2,1)}, bf16[512,256]{1,0:T(8,128)(2,1)S(1)}, u32[]{:S(2)}, u32[]{:S(2)}) collective-permute-start(bf16[512,256]{1,0:T(8,128)(2,1)} %param.6), channel_id=1, source_target_pairs={{0,16},{1,17},{2,18},{3,19},{4,20},{5,21},{6,22},{7,23},{8,24},{9,... | collective-permute-start | bytes 786440 | tf_op jit(solution)/shard_map/z2/ppermute | solution.py:70
  8.9 1.6 %collective-permute-start.7 = (bf16[1024,256]{1,0:T(8,128)(2,1)S(1)}, bf16[1024,256]{1,0:T(8,128)(2,1)S(1)}, u32[]{:S(2)}, u32[]{:S(2)}) collective-permute-start(bf16[1024,256]{1,0:T(8,128)(2,1)S(1)} %constant_dynamic-update-slice_fusion.refs_0_), channel_id=1, source_target_pairs={{0,4},{1,3},{2,6},{3,1},{4,0},{5,7},{6,2},{7,5},{8,12},{9,11},{10,... | collective-permute-start | bytes 1572872 | tf_op jit(solution)/shard_map/q0/ppermute | solution.py:70
  10.5 2.0 %all_gather.3 = s32[256,2]{0,1:T(2,128)S(1)} all-gather(s32[128,2]{0,1:T(2,128)} %param.8), channel_id=1, replica_groups=mesh['section'=16,'replica'=2] {'replica'}, dimensions={0}, use_global_device_ids=true | all-gather | bytes 3072 | tf_op jit(solution)/shard_map/all_gather | solution.py:342
  12.5 5.3 %collective-permute-done = bf16[512,256]{1,0:T(8,128)(2,1)S(1)} collective-permute-done((bf16[512,256]{1,0:T(8,128)(2,1)}, bf16[512,256]{1,0:T(8,128)(2,1)S(1)}, u32[]{:S(2)}, u32[]{:S(2)}) %collective-permute-start) | collective-permute-done | bytes 262176 | tf_op jit(solution)/shard_map/z1/ppermute | solution.py:70
  18.0 3.3 %collective-permute-start.5 = (bf16[512,256]{1,0:T(8,128)(2,1)}, bf16[512,256]{1,0:T(8,128)(2,1)S(1)}, u32[]{:S(2)}, u32[]{:S(2)}) collective-permute-start(bf16[512,256]{1,0:T(8,128)(2,1)} %param.6), channel_id=1, source_target_pairs={{0,24},{1,25},{2,26},{3,27},{4,28},{5,29},{6,30},{7,31},{8,16},{9,... | collective-permute-start | bytes 786440 | tf_op jit(solution)/shard_map/z3/ppermute | solution.py:70
  24.3 4.2 %collective-permute-done.4 = bf16[512,256]{1,0:T(8,128)(2,1)S(1)} collective-permute-done((bf16[512,256]{1,0:T(8,128)(2,1)S(1)}, bf16[512,256]{1,0:T(8,128)(2,1)S(1)}, u32[]{:S(2)}, u32[]{:S(2)}) %collective-permute-start.4) | collective-permute-done | bytes 262176 | tf_op jit(solution)/shard_map/r2/ppermute | solution.py:70
  30.1 2.1 %gather_tiles.1.tiles = bf16[272,128,128]{2,1,0:T(8,128)(2,1)S(1)} custom-call(s32[272]{0:T(512)} %broadcast_add_fusion.entries, s32[9]{0:T(128)} %copy-done.3, bf16[128,128,128]{2,1,0:T(8,128)(2,1)} %own.1, bf16[128,128,128]{2,1,0:T(8,128)(2,1)} %collective-permute-done.3.other), custom_call_target="tpu_custom_call" | custom-call | bytes 1024 | tf_op jit(solution)/shard_map/gather_tiles/pallas_call | solution.py:181
  32.9 1.8 %add_a.1.refs_2_ = f32[9,128,256]{2,1,0:T(8,128)S(1)} custom-call(s32[272]{0:T(512)S(1)} %copy-done.2, s32[9]{0:T(128)S(1)} %copy-done.4, bf16[272,128,128]{2,1,0:T(8,128)(2,1)S(1)} %gather_tiles.1.tiles, bf16[1024,256]{1,0:T(8,128)(2,1)S(1)} %constant_dynamic-update-slice_fusion.refs_0_, bf16[1024,256]{1,0:T(8,128)(2,1)S(1)} %collective-permute-done.7.refs_1_, ...), custom_call_target="tpu_custom_call" | custom-call | flops 4294967296 | bytes 4194304 | tf_op jit(solution)/shard_map/add_a/pallas_call | solution.py:239
  34.8 2.7 %collective-permute-done.8 = bf16[512,256]{1,0:T(8,128)(2,1)S(1)} collective-permute-done((bf16[512,256]{1,0:T(8,128)(2,1)S(1)}, bf16[512,256]{1,0:T(8,128)(2,1)S(1)}, u32[]{:S(2)}, u32[]{:S(2)}) %collective-permute-start.8) | collective-permute-done | bytes 262176 | tf_op jit(solution)/shard_map/r3/ppermute | solution.py:70
  37.5 1.4 %collective-permute-start.9 = (bf16[1024,256]{1,0:T(8,128)(2,1)S(1)}, bf16[1024,256]{1,0:T(8,128)(2,1)S(1)}, u32[]{:S(2)}, u32[]{:S(2)}) collective-permute-start(bf16[1024,256]{1,0:T(8,128)(2,1)S(1)} %constant_dynamic-update-slice_fusion.2.refs_1_), channel_id=1, source_target_pairs={{0,4},{1,3},{2,6},{3,1},{4,0},{5,7},{6,2},{7,5},{8,12},{9,11},{10,... | collective-permute-start | bytes 1572872 | tf_op jit(solution)/shard_map/q3/ppermute | solution.py:70
  38.8 1.7 %add_b.1.refs_2_ = f32[9,128,256]{2,1,0:T(8,128)S(1)} custom-call(s32[272]{0:T(512)S(1)} %copy-done.2, s32[9]{0:T(128)S(1)} %copy-done.4, bf16[272,128,128]{2,1,0:T(8,128)(2,1)S(1)} %gather_tiles.1.tiles, bf16[1024,256]{1,0:T(8,128)(2,1)S(1)} %collective-permute-done.11.refs_0_, ...), custom_call_target="tpu_custom_call", output_to_operand_aliasing={{}: (5, {})} | custom-call | flops 4294967296 | bytes 4194304 | tf_op jit(solution)/shard_map/add_b/pallas_call | solution.py:239
  40.6 1.2 %add_c.1.refs_1_ = f32[9,128,256]{2,1,0:T(8,128)S(1)} custom-call(s32[272]{0:T(512)S(1)} %copy-done.2, s32[9]{0:T(128)S(1)} %copy-done.4, bf16[272,128,128]{2,1,0:T(8,128)(2,1)S(1)} %gather_tiles.1.tiles, bf16[1024,256]{1,0:T(8,128)(2,1)S(1)} %collective-permute-done.10.refs_0_, ...), custom_call_target="tpu_custom_call", output_to_operand_aliasing={{}: (5, {})} | custom-call | flops 4294967296 | bytes 4194304 | tf_op jit(solution)/shard_map/add_c/pallas_call | solution.py:239
  41.9 4.9 %collective-permute-done.9.refs_0_ = bf16[1024,256]{1,0:T(8,128)(2,1)S(1)} collective-permute-done((bf16[1024,256]{1,0:T(8,128)(2,1)S(1)}, bf16[1024,256]{1,0:T(8,128)(2,1)S(1)}, u32[]{:S(2)}, u32[]{:S(2)}) %collective-permute-start.9) | collective-permute-done | bytes 524320 | tf_op jit(solution)/shard_map/q3/ppermute | solution.py:70
  47.9 1.9 %collective-permute-done.12.theirs = f32[4,128,256]{2,1,0:T(8,128)S(1)} collective-permute-done((f32[4,128,256]{2,1,0:T(8,128)S(1)}, f32[4,128,256]{2,1,0:T(8,128)S(1)}, u32[]{:S(2)}, u32[]{:S(2)}) %collective-permute-start.12) | collective-permute-done | bytes 524320 | tf_op jit(solution)/shard_map/rows/ppermute | solution.py:75
  51.1 1.2 %collective-permute-done.13 = f32[136,256]{1,0:T(8,128)S(1)} collective-permute-done((f32[136,256]{1,0:T(8,128)S(1)}, f32[136,256]{1,0:T(8,128)S(1)}, u32[]{:S(2)}, u32[]{:S(2)}) %collective-permute-start.13) | collective-permute-done | bytes 139296 | tf_op jit(solution)/shard_map/halves/ppermute | solution.py:75
  52.3 2.6 %collective-permute-start.14 = (bf16[136,256]{1,0:T(8,128)(2,1)S(1)}, bf16[136,256]{1,0:T(8,128)(2,1)S(1)}, u32[]{:S(2)}, u32[]{:S(2)}) collective-permute-start(bf16[136,256]{1,0:T(8,128)(2,1)S(1)} %add_convert_fusion), channel_id=1, source_target_pairs={{0,6},{1,7},{2,4},{3,5},{4,2},{5,3},{6,0},{7,1},{8,14},{9,15},{10,... | collective-permute-start | bytes 208904 | tf_op jit(solution)/shard_map/sumd/ppermute | solution.py:70
  55.9 1.7 %collective-permute-done.14 = bf16[136,256]{1,0:T(8,128)(2,1)S(1)} collective-permute-done((bf16[136,256]{1,0:T(8,128)(2,1)S(1)}, bf16[136,256]{1,0:T(8,128)(2,1)S(1)}, u32[]{:S(2)}, u32[]{:S(2)}) %collective-permute-start.14) | collective-permute-done | bytes 69664 | tf_op jit(solution)/shard_map/sumd/ppermute | solution.py:70
  57.6 1.8 %collective-permute-done.15 = bf16[136,256]{1,0:T(8,128)(2,1)S(1)} collective-permute-done((bf16[136,256]{1,0:T(8,128)(2,1)S(1)}, bf16[136,256]{1,0:T(8,128)(2,1)S(1)}, u32[]{:S(2)}, u32[]{:S(2)}) %collective-permute-start.15) | collective-permute-done | bytes 69664 | tf_op jit(solution)/shard_map/sum1/ppermute | solution.py:70
  60.0 1.6 %collective-permute-start.18 = (bf16[136,256]{1,0:T(8,128)(2,1)S(1)}, bf16[136,256]{1,0:T(8,128)(2,1)S(1)}, u32[]{:S(2)}, u32[]{:S(2)}) collective-permute-start(bf16[136,256]{1,0:T(8,128)(2,1)S(1)} %get-tuple-element.45), channel_id=1, source_target_pairs={{0,16},{1,17},{2,18},{3,19},{4,20},{5,21},{6,22},{7,23},{8,24},{9,... | collective-permute-start | bytes 208904 | tf_op jit(solution)/shard_map/sum4/ppermute | solution.py:70
  61.6 2.3 %collective-permute-start.19 = (bf16[136,256]{1,0:T(8,128)(2,1)S(1)}, bf16[136,256]{1,0:T(8,128)(2,1)S(1)}, u32[]{:S(2)}, u32[]{:S(2)}) collective-permute-start(bf16[136,256]{1,0:T(8,128)(2,1)S(1)} %get-tuple-element.45), channel_id=1, source_target_pairs={{0,24},{1,25},{2,26},{3,27},{4,28},{5,29},{6,30},{7,31},{8,16},{9,... | collective-permute-start | bytes 208904 | tf_op jit(solution)/shard_map/sum5/ppermute | solution.py:70
  64.4 4.0 %collective-permute-done.18 = bf16[136,256]{1,0:T(8,128)(2,1)S(1)} collective-permute-done((bf16[136,256]{1,0:T(8,128)(2,1)S(1)}, bf16[136,256]{1,0:T(8,128)(2,1)S(1)}, u32[]{:S(2)}, u32[]{:S(2)}) %collective-permute-start.18) | collective-permute-done | bytes 69664 | tf_op jit(solution)/shard_map/sum4/ppermute | solution.py:70
  68.5 1.3 %collective-permute-done.20.rest = f32[136,256]{1,0:T(8,128)S(1)} collective-permute-done((f32[136,256]{1,0:T(8,128)S(1)}, f32[136,256]{1,0:T(8,128)S(1)}, u32[]{:S(2)}, u32[]{:S(2)}) %collective-permute-start.20) | collective-permute-done | bytes 139296 | tf_op jit(solution)/shard_map/back/ppermute | solution.py:75
  (59 shorter events, 12.4 us)
Async XLA Ops:
  0.6 21.4 %collective-permute-start.3 = (bf16[128,128,128]{2,1,0:T(8,128)(2,1)}, bf16[128,128,128]{2,1,0:T(8,128)(2,1)}, u32[]{:S(2)}, u32[]{:S(2)}) collective-permute-start(bf16[128,128,128]{2,1,0:T(8,128)(2,1)} %own.1), channel_id=1, source_target_pairs={{0,1},{1,0},{2,3},{3,2},{4,5},{5,4},{6,7},{7,6},{8,9},{9,8},{10,11... | collective-permute-start | bytes 12582920 | tf_op jit(solution)/shard_map/tiles/ppermute | solution.py:75
  1.1 7.7 %collective-permute-start.1 = (bf16[512,256]{1,0:T(8,128)(2,1)}, bf16[512,256]{1,0:T(8,128)(2,1)S(1)}, u32[]{:S(2)}, u32[]{:S(2)}) collective-permute-start(bf16[512,256]{1,0:T(8,128)(2,1)} %param.6), channel_id=1, source_target_pairs={{0,2},{1,5},{2,0},{3,7},{4,6},{5,1},{6,4},{7,3},{8,10},{9,13},{10,... | collective-permute-start | bytes 786440 | tf_op jit(solution)/shard_map/r0/ppermute | solution.py:70
  3.7 14.1 %collective-permute-start = (bf16[512,256]{1,0:T(8,128)(2,1)}, bf16[512,256]{1,0:T(8,128)(2,1)S(1)}, u32[]{:S(2)}, u32[]{:S(2)}) collective-permute-start(bf16[512,256]{1,0:T(8,128)(2,1)} %param.6), channel_id=1, source_target_pairs={{0,8},{1,9},{2,10},{3,11},{4,12},{5,13},{6,14},{7,15},{8,0},{9,1},... | collective-permute-start | bytes 786440 | tf_op jit(solution)/shard_map/z1/ppermute | solution.py:70
  5.3 16.7 %collective-permute-start.2 = (bf16[512,256]{1,0:T(8,128)(2,1)}, bf16[512,256]{1,0:T(8,128)(2,1)S(1)}, u32[]{:S(2)}, u32[]{:S(2)}) collective-permute-start(bf16[512,256]{1,0:T(8,128)(2,1)} %param.6), channel_id=1, source_target_pairs={{0,16},{1,17},{2,18},{3,19},{4,20},{5,21},{6,22},{7,23},{8,24},{9,... | collective-permute-start | bytes 786440 | tf_op jit(solution)/shard_map/z2/ppermute | solution.py:70
  8.9 15.3 %collective-permute-start.7 = (bf16[1024,256]{1,0:T(8,128)(2,1)S(1)}, bf16[1024,256]{1,0:T(8,128)(2,1)S(1)}, u32[]{:S(2)}, u32[]{:S(2)}) collective-permute-start(bf16[1024,256]{1,0:T(8,128)(2,1)S(1)} %constant_dynamic-update-slice_fusion.refs_0_), channel_id=1, source_target_pairs={{0,4},{1,3},{2,6},{3,1},{4,0},{5,7},{6,2},{7,5},{8,12},{9,11},{10,... | collective-permute-start | bytes 1572872 | tf_op jit(solution)/shard_map/q0/ppermute | solution.py:70
  17.8 6.4 %collective-permute-start.6 = (bf16[512,256]{1,0:T(8,128)(2,1)S(1)}, bf16[512,256]{1,0:T(8,128)(2,1)S(1)}, u32[]{:S(2)}, u32[]{:S(2)}) collective-permute-start(bf16[512,256]{1,0:T(8,128)(2,1)S(1)} %collective-permute-done), channel_id=1, source_target_pairs={{0,2},{1,5},{2,0},{3,7},{4,6},{5,1},{6,4},{7,3},{8,10},{9,13},{10,... | collective-permute-start | bytes 786440 | tf_op jit(solution)/shard_map/r1/ppermute | solution.py:70
  18.0 11.6 %collective-permute-start.5 = (bf16[512,256]{1,0:T(8,128)(2,1)}, bf16[512,256]{1,0:T(8,128)(2,1)S(1)}, u32[]{:S(2)}, u32[]{:S(2)}) collective-permute-start(bf16[512,256]{1,0:T(8,128)(2,1)} %param.6), channel_id=1, source_target_pairs={{0,24},{1,25},{2,26},{3,27},{4,28},{5,29},{6,30},{7,31},{8,16},{9,... | collective-permute-start | bytes 786440 | tf_op jit(solution)/shard_map/z3/ppermute | solution.py:70
  21.6 8.6 %copy-start.3 = (s32[9]{0:T(128)}, s32[9]{0:T(128)S(1)}, u32[]{:S(2)}) copy-start(s32[9]{0:T(128)S(1)} %select_reduce_fusion.2.starts) | copy-start | bytes 112
  22.0 6.4 %collective-permute-start.4 = (bf16[512,256]{1,0:T(8,128)(2,1)S(1)}, bf16[512,256]{1,0:T(8,128)(2,1)S(1)}, u32[]{:S(2)}, u32[]{:S(2)}) collective-permute-start(bf16[512,256]{1,0:T(8,128)(2,1)S(1)} %collective-permute-done.2), channel_id=1, source_target_pairs={{0,2},{1,5},{2,0},{3,7},{4,6},{5,1},{6,4},{7,3},{8,10},{9,13},{10,... | collective-permute-start | bytes 786440 | tf_op jit(solution)/shard_map/r2/ppermute | solution.py:70
  24.2 14.6 %collective-permute-start.11 = (bf16[1024,256]{1,0:T(8,128)(2,1)S(1)}, bf16[1024,256]{1,0:T(8,128)(2,1)S(1)}, u32[]{:S(2)}, u32[]{:S(2)}) collective-permute-start(bf16[1024,256]{1,0:T(8,128)(2,1)S(1)} %collective-permute-done.7.refs_1_), channel_id=1, source_target_pairs={{0,8},{1,9},{2,10},{3,11},{4,12},{5,13},{6,14},{7,15},{8,0},{9,1},... | collective-permute-start | bytes 1572872 | tf_op jit(solution)/shard_map/q1/ppermute | solution.py:70
  28.5 12.0 %collective-permute-start.10 = (bf16[1024,256]{1,0:T(8,128)(2,1)S(1)}, bf16[1024,256]{1,0:T(8,128)(2,1)S(1)}, u32[]{:S(2)}, u32[]{:S(2)}) collective-permute-start(bf16[1024,256]{1,0:T(8,128)(2,1)S(1)} %pad_maximum_fusion.refs_1_), channel_id=1, source_target_pairs={{0,4},{1,3},{2,6},{3,1},{4,0},{5,7},{6,2},{7,5},{8,12},{9,11},{10,... | collective-permute-start | bytes 1572872 | tf_op jit(solution)/shard_map/q2/ppermute | solution.py:70
  29.6 7.9 %collective-permute-start.8 = (bf16[512,256]{1,0:T(8,128)(2,1)S(1)}, bf16[512,256]{1,0:T(8,128)(2,1)S(1)}, u32[]{:S(2)}, u32[]{:S(2)}) collective-permute-start(bf16[512,256]{1,0:T(8,128)(2,1)S(1)} %collective-permute-done.5), channel_id=1, source_target_pairs={{0,2},{1,5},{2,0},{3,7},{4,6},{5,1},{6,4},{7,3},{8,10},{9,13},{10,... | collective-permute-start | bytes 786440 | tf_op jit(solution)/shard_map/r3/ppermute | solution.py:70
  37.5 9.2 %collective-permute-start.9 = (bf16[1024,256]{1,0:T(8,128)(2,1)S(1)}, bf16[1024,256]{1,0:T(8,128)(2,1)S(1)}, u32[]{:S(2)}, u32[]{:S(2)}) collective-permute-start(bf16[1024,256]{1,0:T(8,128)(2,1)S(1)} %constant_dynamic-update-slice_fusion.2.refs_1_), channel_id=1, source_target_pairs={{0,4},{1,3},{2,6},{3,1},{4,0},{5,7},{6,2},{7,5},{8,12},{9,11},{10,... | collective-permute-start | bytes 1572872 | tf_op jit(solution)/shard_map/q3/ppermute | solution.py:70
  41.8 8.0 %copy-start = (bf16[512,256]{1,0:T(8,128)(2,1)S(1)}, bf16[512,256]{1,0:T(8,128)(2,1)}, u32[]{:S(2)}) copy-start(bf16[512,256]{1,0:T(8,128)(2,1)} %grad_out.1) | copy-start | bytes 786436
  41.8 8.0 %copy-start.1 = (bf16[256,256]{1,0:T(8,128)(2,1)S(1)}, bf16[256,256]{1,0:T(8,128)(2,1)}, u32[]{:S(2)}) copy-start(bf16[256,256]{1,0:T(8,128)(2,1)} %weight.1) | copy-start | bytes 393220
  47.8 2.0 %collective-permute-start.12 = (f32[4,128,256]{2,1,0:T(8,128)S(1)}, f32[4,128,256]{2,1,0:T(8,128)S(1)}, u32[]{:S(2)}, u32[]{:S(2)}) collective-permute-start(f32[4,128,256]{2,1,0:T(8,128)S(1)} %get-tuple-element.39), channel_id=1, source_target_pairs={{0,1},{1,0},{2,3},{3,2},{4,5},{5,4},{6,7},{7,6},{8,9},{9,8},{10,11... | collective-permute-start | bytes 1572872 | tf_op jit(solution)/shard_map/rows/ppermute | solution.py:75
  50.9 1.4 %collective-permute-start.13 = (f32[136,256]{1,0:T(8,128)S(1)}, f32[136,256]{1,0:T(8,128)S(1)}, u32[]{:S(2)}, u32[]{:S(2)}) collective-permute-start(f32[136,256]{1,0:T(8,128)S(1)} %get-tuple-element.42), channel_id=1, source_target_pairs={{0,1},{1,0},{2,3},{3,2},{4,5},{5,4},{6,7},{7,6},{8,9},{9,8},{10,11... | collective-permute-start | bytes 417800 | tf_op jit(solution)/shard_map/halves/ppermute | solution.py:75
  52.3 5.3 %collective-permute-start.14 = (bf16[136,256]{1,0:T(8,128)(2,1)S(1)}, bf16[136,256]{1,0:T(8,128)(2,1)S(1)}, u32[]{:S(2)}, u32[]{:S(2)}) collective-permute-start(bf16[136,256]{1,0:T(8,128)(2,1)S(1)} %add_convert_fusion), channel_id=1, source_target_pairs={{0,6},{1,7},{2,4},{3,5},{4,2},{5,3},{6,0},{7,1},{8,14},{9,15},{10,... | collective-permute-start | bytes 208904 | tf_op jit(solution)/shard_map/sumd/ppermute | solution.py:70
  54.9 4.4 %collective-permute-start.15 = (bf16[136,256]{1,0:T(8,128)(2,1)S(1)}, bf16[136,256]{1,0:T(8,128)(2,1)S(1)}, u32[]{:S(2)}, u32[]{:S(2)}) collective-permute-start(bf16[136,256]{1,0:T(8,128)(2,1)S(1)} %add_convert_fusion), channel_id=1, source_target_pairs={{0,2},{1,5},{2,0},{3,7},{4,6},{5,1},{6,4},{7,3},{8,10},{9,13},{10,... | collective-permute-start | bytes 208904 | tf_op jit(solution)/shard_map/sum1/ppermute | solution.py:70
  55.1 4.3 %collective-permute-start.16 = (bf16[136,256]{1,0:T(8,128)(2,1)S(1)}, bf16[136,256]{1,0:T(8,128)(2,1)S(1)}, u32[]{:S(2)}, u32[]{:S(2)}) collective-permute-start(bf16[136,256]{1,0:T(8,128)(2,1)S(1)} %add_convert_fusion), channel_id=1, source_target_pairs={{0,4},{1,3},{2,6},{3,1},{4,0},{5,7},{6,2},{7,5},{8,12},{9,11},{10,... | collective-permute-start | bytes 208904 | tf_op jit(solution)/shard_map/sum2/ppermute | solution.py:70
  59.5 5.0 %collective-permute-start.17 = (bf16[136,256]{1,0:T(8,128)(2,1)S(1)}, bf16[136,256]{1,0:T(8,128)(2,1)S(1)}, u32[]{:S(2)}, u32[]{:S(2)}) collective-permute-start(bf16[136,256]{1,0:T(8,128)(2,1)S(1)} %get-tuple-element.45), channel_id=1, source_target_pairs={{0,8},{1,9},{2,10},{3,11},{4,12},{5,13},{6,14},{7,15},{8,0},{9,1},... | collective-permute-start | bytes 208904 | tf_op jit(solution)/shard_map/sum3/ppermute | solution.py:70
  60.0 8.4 %collective-permute-start.18 = (bf16[136,256]{1,0:T(8,128)(2,1)S(1)}, bf16[136,256]{1,0:T(8,128)(2,1)S(1)}, u32[]{:S(2)}, u32[]{:S(2)}) collective-permute-start(bf16[136,256]{1,0:T(8,128)(2,1)S(1)} %get-tuple-element.45), channel_id=1, source_target_pairs={{0,16},{1,17},{2,18},{3,19},{4,20},{5,21},{6,22},{7,23},{8,24},{9,... | collective-permute-start | bytes 208904 | tf_op jit(solution)/shard_map/sum4/ppermute | solution.py:70
  61.6 6.8 %collective-permute-start.19 = (bf16[136,256]{1,0:T(8,128)(2,1)S(1)}, bf16[136,256]{1,0:T(8,128)(2,1)S(1)}, u32[]{:S(2)}, u32[]{:S(2)}) collective-permute-start(bf16[136,256]{1,0:T(8,128)(2,1)S(1)} %get-tuple-element.45), channel_id=1, source_target_pairs={{0,24},{1,25},{2,26},{3,27},{4,28},{5,29},{6,30},{7,31},{8,16},{9,... | collective-permute-start | bytes 208904 | tf_op jit(solution)/shard_map/sum5/ppermute | solution.py:70
  68.5 1.4 %collective-permute-start.20 = (f32[136,256]{1,0:T(8,128)S(1)}, f32[136,256]{1,0:T(8,128)S(1)}, u32[]{:S(2)}, u32[]{:S(2)}) collective-permute-start(f32[136,256]{1,0:T(8,128)S(1)} %add_add_fusion.part), channel_id=1, source_target_pairs={{0,1},{1,0},{2,3},{3,2},{4,5},{5,4},{6,7},{7,6},{8,9},{9,8},{10,11... | collective-permute-start | bytes 417800 | tf_op jit(solution)/shard_map/back/ppermute | solution.py:75
  (3 other events, 12.4 us)

commit v4 on v3

--- a/solution.py
+++ b/solution.py
@@ -225,7 +225,7 @@
     for g, array in zip(groups, arrays):
         add_group(entries, starts[g], starts[g + 1], tiles, array, acc)
     half = give.shape[0]
-    give[...] = acc[half : 2 * half]
+    give[...] = acc[half : 2 * half].astype(give.dtype)
 
 
 def whole(space):
@@ -250,7 +250,7 @@
 
 def add_late(work, arrays, groups, acc, row_blocks):
     entries, starts, tiles = work
-    half = VMEM((row_blocks // 2, 128, arrays[0].shape[1]), jnp.float32)
+    half = VMEM((row_blocks // 2, 128, arrays[0].shape[1]), jnp.bfloat16)
     return pl.pallas_call(
         functools.partial(late_kernel, groups),
         out_shape=(VMEM(acc.shape, jnp.float32), half),
@@ -264,7 +264,7 @@
 
 
 def dense_kernel(core, mine, theirs, weight, bias, grad_out, output, keep, give, full):
-    hidden = (mine[: theirs.shape[0]] + theirs[...]).reshape(grad_out.shape).astype(jnp.bfloat16)
+    hidden = (mine[: theirs.shape[0]] + theirs[...].astype(jnp.float32)).reshape(grad_out.shape).astype(jnp.bfloat16)
     pre_act = jnp.dot(hidden, weight[...], preferred_element_type=jnp.float32) + bias[...]
     sigma = 1.0 / (1.0 + jnp.exp(-pre_act))
     output[...] = (pre_act * sigma).astype(jnp.bfloat16)
@@ -349,12 +349,17 @@
     pair1 = join(z1, first_hop(z1, "r1"))
     q1 = along_z(q0, 1, "q1")
     z2, other_tiles = after(z2, other_tiles)
-    pair2 = join(z2, first_hop(z2, "r2"))
-    pair2, other_tiles = after(pair2, other_tiles)
-    q2 = second_hop(pair2, "q2")
+    r2 = first_hop(z2, "r2")
+    q2a = second_hop(z2, "q2a")
+    pair2 = join(z2, r2)
+    q2a, other_tiles = after(q2a, other_tiles)
+    q2 = join(q2a, second_hop(r2, "q2b"))
     z3, pair1, pair2, q0 = after(z3, pair1, pair2, q0)
-    pair3 = join(z3, first_hop(z3, "r3"))
-    q3 = second_hop(pair3, "q3")
+    r3 = first_hop(z3, "r3")
+    q3a = second_hop(z3, "q3a")
+    pair3 = join(z3, r3)
+    q1, pair3 = after(q1, pair3)
+    q3 = join(q3a, second_hop(r3, "q3b"))
     entries, starts = work_list(index, slots, row_blocks)
     tiles = gather_tiles(entries, starts, adj_tiles, other_tiles)
     work = (entries, starts, tiles)

time: 71 us -> 70.6 us (level)
  waiting for transfers between devices: 30 us -> 27.8 us
  starting transfers between devices: 24.7 us -> 26.8 us
    ppermute x17 -> x19, starting transfers between devices: 23.9 us -> 26 us  [send(): return lax.ppermute(x, BOTH, perm)]
    ppermute x17 -> x19, waiting for transfers between devices: 25.6 us -> 23.7 us  [send(): return lax.ppermute(x, BOTH, perm)]
    unnamed x14 -> x15, local copies, waits for them, and re-layouts: 1.7 us -> 1.69 us
  transfers between devices with their start and end apart: 21 -> 23, of which waited for: 12 -> 12; matrix products, arithmetic and copies ran while one was open for 3% -> 3% of each run, Pallas kernels for 10% -> 10%
where the time goes in v4:
time: 70.6 us; the launch traced here: 70.1 us
  waiting for transfers between devices  27.8 us (39%)
  starting transfers between devices  26.8 us (38%)
  Pallas kernels  9.39 us (13%)
  blocking collectives  1.98 us (3%)
  local copies, waits for them, and re-layouts  1.71 us (2%)
  other arithmetic  1.55 us (2%)
  between operations  0.88 us (1%)
    ppermute x19, starting transfers between devices, send(): return lax.ppermute(x, BOTH, perm)  26 us
    ppermute x19, waiting for transfers between devices, send(): return lax.ppermute(x, BOTH, perm)  23.7 us
    pallas_call x3, Pallas kernels, add_groups(): pl.pallas_call(functools.partial(add_kernel, groups, fresh), out_shape=sh...  4.63 us
    ppermute x4, waiting for transfers between devices, swap(): return lax.ppermute(x, 'replica', [(0, 1), (1, 0)])  4.1 us
    pallas_call x1, Pallas kernels, gather_tiles(): pl.pallas_call(functools.partial(gather_kernel, own.shape[0]), out_shape=...  2.06 us
    all_gather x1, blocking collectives, shards(): index = lax.all_gather(index, 'replica', axis=0, tiled=True)  1.98 us
    unnamed x15, local copies, waits for them, and re-layouts  1.69 us
  transfers between devices with their start and end apart: 23, of which 12 were waited for; matrix products, arithmetic and copies ran while one was open for 3% of the time, Pallas kernels for 10%

profile of v4, /device:TPU:0, one launch (start us, length us, event | category | flops | bytes accessed | tf_op | source)
XLA Modules:
  0.0 70.1 jit_solution(8911436306309664937)
XLA Ops:
  1.1 2.6 %collective-permute-start.1 = (bf16[512,256]{1,0:T(8,128)(2,1)}, bf16[512,256]{1,0:T(8,128)(2,1)S(1)}, u32[]{:S(2)}, u32[]{:S(2)}) collective-permute-start(bf16[512,256]{1,0:T(8,128)(2,1)} %param.6), channel_id=1, source_target_pairs={{0,2},{1,5},{2,0},{3,7},{4,6},{5,1},{6,4},{7,3},{8,10},{9,13},{10,... | collective-permute-start | bytes 786440 | tf_op jit(solution)/shard_map/r0/ppermute | solution.py:70
  3.7 1.6 %collective-permute-start = (bf16[512,256]{1,0:T(8,128)(2,1)}, bf16[512,256]{1,0:T(8,128)(2,1)S(1)}, u32[]{:S(2)}, u32[]{:S(2)}) collective-permute-start(bf16[512,256]{1,0:T(8,128)(2,1)} %param.6), channel_id=1, source_target_pairs={{0,8},{1,9},{2,10},{3,11},{4,12},{5,13},{6,14},{7,15},{8,0},{9,1},... | collective-permute-start | bytes 786440 | tf_op jit(solution)/shard_map/z1/ppermute | solution.py:70
  5.3 2.6 %collective-permute-start.2 = (bf16[512,256]{1,0:T(8,128)(2,1)}, bf16[512,256]{1,0:T(8,128)(2,1)S(1)}, u32[]{:S(2)}, u32[]{:S(2)}) collective-permute-start(bf16[512,256]{1,0:T(8,128)(2,1)} %param.6), channel_id=1, source_target_pairs={{0,16},{1,17},{2,18},{3,19},{4,20},{5,21},{6,22},{7,23},{8,24},{9,... | collective-permute-start | bytes 786440 | tf_op jit(solution)/shard_map/z2/ppermute | solution.py:70
  8.9 1.6 %collective-permute-start.8 = (bf16[1024,256]{1,0:T(8,128)(2,1)S(1)}, bf16[1024,256]{1,0:T(8,128)(2,1)S(1)}, u32[]{:S(2)}, u32[]{:S(2)}) collective-permute-start(bf16[1024,256]{1,0:T(8,128)(2,1)S(1)} %constant_dynamic-update-slice_fusion.refs_0_), channel_id=1, source_target_pairs={{0,4},{1,3},{2,6},{3,1},{4,0},{5,7},{6,2},{7,5},{8,12},{9,11},{10,... | collective-permute-start | bytes 1572872 | tf_op jit(solution)/shard_map/q0/ppermute | solution.py:70
  10.5 2.0 %all_gather.3 = s32[256,2]{0,1:T(2,128)S(1)} all-gather(s32[128,2]{0,1:T(2,128)} %param.8), channel_id=1, replica_groups=mesh['section'=16,'replica'=2] {'replica'}, dimensions={0}, use_global_device_ids=true | all-gather | bytes 3072 | tf_op jit(solution)/shard_map/all_gather | solution.py:342
  12.5 5.3 %collective-permute-done = bf16[512,256]{1,0:T(8,128)(2,1)S(1)} collective-permute-done((bf16[512,256]{1,0:T(8,128)(2,1)}, bf16[512,256]{1,0:T(8,128)(2,1)S(1)}, u32[]{:S(2)}, u32[]{:S(2)}) %collective-permute-start) | collective-permute-done | bytes 262176 | tf_op jit(solution)/shard_map/z1/ppermute | solution.py:70
  18.0 3.3 %collective-permute-start.5 = (bf16[512,256]{1,0:T(8,128)(2,1)}, bf16[512,256]{1,0:T(8,128)(2,1)S(1)}, u32[]{:S(2)}, u32[]{:S(2)}) collective-permute-start(bf16[512,256]{1,0:T(8,128)(2,1)} %param.6), channel_id=1, source_target_pairs={{0,24},{1,25},{2,26},{3,27},{4,28},{5,29},{6,30},{7,31},{8,16},{9,... | collective-permute-start | bytes 786440 | tf_op jit(solution)/shard_map/z3/ppermute | solution.py:70
  25.5 4.3 %collective-permute-done.7 = bf16[512,256]{1,0:T(8,128)(2,1)S(1)} collective-permute-done((bf16[512,256]{1,0:T(8,128)(2,1)S(1)}, bf16[512,256]{1,0:T(8,128)(2,1)S(1)}, u32[]{:S(2)}, u32[]{:S(2)}) %collective-permute-start.7) | collective-permute-done | bytes 262176 | tf_op jit(solution)/shard_map/r2/ppermute | solution.py:70
  30.4 1.7 %collective-permute-start.9 = (bf16[512,256]{1,0:T(8,128)(2,1)S(1)}, bf16[512,256]{1,0:T(8,128)(2,1)S(1)}, u32[]{:S(2)}, u32[]{:S(2)}) collective-permute-start(bf16[512,256]{1,0:T(8,128)(2,1)S(1)} %collective-permute-done.5), channel_id=1, source_target_pairs={{0,4},{1,3},{2,6},{3,1},{4,0},{5,7},{6,2},{7,5},{8,12},{9,11},{10,... | collective-permute-start | bytes 786440 | tf_op jit(solution)/shard_map/q3a/ppermute | solution.py:70
  32.2 2.1 %gather_tiles.1.tiles = bf16[272,128,128]{2,1,0:T(8,128)(2,1)S(1)} custom-call(s32[272]{0:T(512)} %broadcast_add_fusion.entries, s32[9]{0:T(128)} %copy-done.3, bf16[128,128,128]{2,1,0:T(8,128)(2,1)} %own.1, bf16[128,128,128]{2,1,0:T(8,128)(2,1)} %collective-permute-done.3.other), custom_call_target="tpu_custom_call" | custom-call | bytes 1024 | tf_op jit(solution)/shard_map/gather_tiles/pallas_call | solution.py:181
  35.4 1.8 %add_a.1.refs_2_ = f32[9,128,256]{2,1,0:T(8,128)S(1)} custom-call(s32[272]{0:T(512)S(1)} %copy-done.2, s32[9]{0:T(128)S(1)} %copy-done.4, bf16[272,128,128]{2,1,0:T(8,128)(2,1)S(1)} %gather_tiles.1.tiles, bf16[1024,256]{1,0:T(8,128)(2,1)S(1)} %constant_dynamic-update-slice_fusion.refs_0_, bf16[1024,256]{1,0:T(8,128)(2,1)S(1)} %collective-permute-done.8.refs_1_, ...), custom_call_target="tpu_custom_call" | custom-call | flops 4294967296 | bytes 4194304 | tf_op jit(solution)/shard_map/add_a/pallas_call | solution.py:239
  37.2 1.5 %collective-permute-done.10 = bf16[512,256]{1,0:T(8,128)(2,1)S(1)} collective-permute-done((bf16[512,256]{1,0:T(8,128)(2,1)S(1)}, bf16[512,256]{1,0:T(8,128)(2,1)S(1)}, u32[]{:S(2)}, u32[]{:S(2)}) %collective-permute-start.10) | collective-permute-done | bytes 262176 | tf_op jit(solution)/shard_map/r3/ppermute | solution.py:70
  38.8 1.6 %collective-permute-start.11 = (bf16[512,256]{1,0:T(8,128)(2,1)S(1)}, bf16[512,256]{1,0:T(8,128)(2,1)S(1)}, u32[]{:S(2)}, u32[]{:S(2)}) collective-permute-start(bf16[512,256]{1,0:T(8,128)(2,1)S(1)} %collective-permute-done.10), channel_id=1, source_target_pairs={{0,4},{1,3},{2,6},{3,1},{4,0},{5,7},{6,2},{7,5},{8,12},{9,11},{10,... | collective-permute-start | bytes 786440 | tf_op jit(solution)/shard_map/q3b/ppermute | solution.py:70
  40.5 1.4 %add_b.1.refs_2_ = f32[9,128,256]{2,1,0:T(8,128)S(1)} custom-call(s32[272]{0:T(512)S(1)} %copy-done.2, s32[9]{0:T(128)S(1)} %copy-done.5, bf16[272,128,128]{2,1,0:T(8,128)(2,1)S(1)} %gather_tiles.1.tiles, bf16[1024,256]{1,0:T(8,128)(2,1)S(1)} %collective-permute-done.13.refs_0_, ...), custom_call_target="tpu_custom_call", output_to_operand_aliasing={{}: (5, {})} | custom-call | flops 4294967296 | bytes 4194304 | tf_op jit(solution)/shard_map/add_b/pallas_call | solution.py:239
  41.9 1.4 %add_c.1.refs_1_ = f32[9,128,256]{2,1,0:T(8,128)S(1)} custom-call(s32[272]{0:T(512)S(1)} %copy-done.2, s32[9]{0:T(128)S(1)} %copy-done.5, bf16[272,128,128]{2,1,0:T(8,128)(2,1)S(1)} %gather_tiles.1.tiles, bf16[1024,256]{1,0:T(8,128)(2,1)S(1)} %pad_maximum_fusion.3.refs_0_, ...), custom_call_target="tpu_custom_call", output_to_operand_aliasing={{}: (5, {})} | custom-call | flops 4294967296 | bytes 4194304 | tf_op jit(solution)/shard_map/add_c/pallas_call | solution.py:239
  43.4 1.9 %collective-permute-done.11 = bf16[512,256]{1,0:T(8,128)(2,1)S(1)} collective-permute-done((bf16[512,256]{1,0:T(8,128)(2,1)S(1)}, bf16[512,256]{1,0:T(8,128)(2,1)S(1)}, u32[]{:S(2)}, u32[]{:S(2)}) %collective-permute-start.11) | collective-permute-done | bytes 262176 | tf_op jit(solution)/shard_map/q3b/ppermute | solution.py:70
  46.2 1.5 %collective-permute-done.14.theirs = bf16[4,128,256]{2,1,0:T(8,128)(2,1)S(1)} collective-permute-done((bf16[4,128,256]{2,1,0:T(8,128)(2,1)S(1)}, bf16[4,128,256]{2,1,0:T(8,128)(2,1)S(1)}, u32[]{:S(2)}, u32[]{:S(2)}) %collective-permute-start.14) | collective-permute-done | bytes 262176 | tf_op jit(solution)/shard_map/rows/ppermute | solution.py:75
  50.3 2.8 %collective-permute-start.16 = (bf16[136,256]{1,0:T(8,128)(2,1)S(1)}, bf16[136,256]{1,0:T(8,128)(2,1)S(1)}, u32[]{:S(2)}, u32[]{:S(2)}) collective-permute-start(bf16[136,256]{1,0:T(8,128)(2,1)S(1)} %add_convert_fusion), channel_id=1, source_target_pairs={{0,6},{1,7},{2,4},{3,5},{4,2},{5,3},{6,0},{7,1},{8,14},{9,15},{10,... | collective-permute-start | bytes 208904 | tf_op jit(solution)/shard_map/sumd/ppermute | solution.py:70
  53.9 1.7 %collective-permute-done.16 = bf16[136,256]{1,0:T(8,128)(2,1)S(1)} collective-permute-done((bf16[136,256]{1,0:T(8,128)(2,1)S(1)}, bf16[136,256]{1,0:T(8,128)(2,1)S(1)}, u32[]{:S(2)}, u32[]{:S(2)}) %collective-permute-start.16) | collective-permute-done | bytes 69664 | tf_op jit(solution)/shard_map/sumd/ppermute | solution.py:70
  55.6 2.0 %collective-permute-done.17 = bf16[136,256]{1,0:T(8,128)(2,1)S(1)} collective-permute-done((bf16[136,256]{1,0:T(8,128)(2,1)S(1)}, bf16[136,256]{1,0:T(8,128)(2,1)S(1)}, u32[]{:S(2)}, u32[]{:S(2)}) %collective-permute-start.17) | collective-permute-done | bytes 69664 | tf_op jit(solution)/shard_map/sum1/ppermute | solution.py:70
  58.2 1.5 %collective-permute-start.19 = (bf16[136,256]{1,0:T(8,128)(2,1)S(1)}, bf16[136,256]{1,0:T(8,128)(2,1)S(1)}, u32[]{:S(2)}, u32[]{:S(2)}) collective-permute-start(bf16[136,256]{1,0:T(8,128)(2,1)S(1)} %get-tuple-element.49), channel_id=1, source_target_pairs={{0,8},{1,9},{2,10},{3,11},{4,12},{5,13},{6,14},{7,15},{8,0},{9,1},... | collective-permute-start | bytes 208904 | tf_op jit(solution)/shard_map/sum3/ppermute | solution.py:70
  59.7 1.6 %collective-permute-start.20 = (bf16[136,256]{1,0:T(8,128)(2,1)S(1)}, bf16[136,256]{1,0:T(8,128)(2,1)S(1)}, u32[]{:S(2)}, u32[]{:S(2)}) collective-permute-start(bf16[136,256]{1,0:T(8,128)(2,1)S(1)} %get-tuple-element.49), channel_id=1, source_target_pairs={{0,16},{1,17},{2,18},{3,19},{4,20},{5,21},{6,22},{7,23},{8,24},{9,... | collective-permute-start | bytes 208904 | tf_op jit(solution)/shard_map/sum4/ppermute | solution.py:70
  61.3 1.4 %collective-permute-start.21 = (bf16[136,256]{1,0:T(8,128)(2,1)S(1)}, bf16[136,256]{1,0:T(8,128)(2,1)S(1)}, u32[]{:S(2)}, u32[]{:S(2)}) collective-permute-start(bf16[136,256]{1,0:T(8,128)(2,1)S(1)} %get-tuple-element.49), channel_id=1, source_target_pairs={{0,24},{1,25},{2,26},{3,27},{4,28},{5,29},{6,30},{7,31},{8,16},{9,... | collective-permute-start | bytes 208904 | tf_op jit(solution)/shard_map/sum5/ppermute | solution.py:70
  62.7 5.2 %collective-permute-done.20 = bf16[136,256]{1,0:T(8,128)(2,1)S(1)} collective-permute-done((bf16[136,256]{1,0:T(8,128)(2,1)S(1)}, bf16[136,256]{1,0:T(8,128)(2,1)S(1)}, u32[]{:S(2)}, u32[]{:S(2)}) %collective-permute-start.20) | collective-permute-done | bytes 69664 | tf_op jit(solution)/shard_map/sum4/ppermute | solution.py:70
  (66 shorter events, 14.8 us)
Async XLA Ops:
  0.6 21.4 %collective-permute-start.3 = (bf16[128,128,128]{2,1,0:T(8,128)(2,1)}, bf16[128,128,128]{2,1,0:T(8,128)(2,1)}, u32[]{:S(2)}, u32[]{:S(2)}) collective-permute-start(bf16[128,128,128]{2,1,0:T(8,128)(2,1)} %own.1), channel_id=1, source_target_pairs={{0,1},{1,0},{2,3},{3,2},{4,5},{5,4},{6,7},{7,6},{8,9},{9,8},{10,11... | collective-permute-start | bytes 12582920 | tf_op jit(solution)/shard_map/tiles/ppermute | solution.py:75
  1.1 7.7 %collective-permute-start.1 = (bf16[512,256]{1,0:T(8,128)(2,1)}, bf16[512,256]{1,0:T(8,128)(2,1)S(1)}, u32[]{:S(2)}, u32[]{:S(2)}) collective-permute-start(bf16[512,256]{1,0:T(8,128)(2,1)} %param.6), channel_id=1, source_target_pairs={{0,2},{1,5},{2,0},{3,7},{4,6},{5,1},{6,4},{7,3},{8,10},{9,13},{10,... | collective-permute-start | bytes 786440 | tf_op jit(solution)/shard_map/r0/ppermute | solution.py:70
  3.7 14.1 %collective-permute-start = (bf16[512,256]{1,0:T(8,128)(2,1)}, bf16[512,256]{1,0:T(8,128)(2,1)S(1)}, u32[]{:S(2)}, u32[]{:S(2)}) collective-permute-start(bf16[512,256]{1,0:T(8,128)(2,1)} %param.6), channel_id=1, source_target_pairs={{0,8},{1,9},{2,10},{3,11},{4,12},{5,13},{6,14},{7,15},{8,0},{9,1},... | collective-permute-start | bytes 786440 | tf_op jit(solution)/shard_map/z1/ppermute | solution.py:70
  5.3 16.7 %collective-permute-start.2 = (bf16[512,256]{1,0:T(8,128)(2,1)}, bf16[512,256]{1,0:T(8,128)(2,1)S(1)}, u32[]{:S(2)}, u32[]{:S(2)}) collective-permute-start(bf16[512,256]{1,0:T(8,128)(2,1)} %param.6), channel_id=1, source_target_pairs={{0,16},{1,17},{2,18},{3,19},{4,20},{5,21},{6,22},{7,23},{8,24},{9,... | collective-permute-start | bytes 786440 | tf_op jit(solution)/shard_map/z2/ppermute | solution.py:70
  8.9 16.4 %collective-permute-start.8 = (bf16[1024,256]{1,0:T(8,128)(2,1)S(1)}, bf16[1024,256]{1,0:T(8,128)(2,1)S(1)}, u32[]{:S(2)}, u32[]{:S(2)}) collective-permute-start(bf16[1024,256]{1,0:T(8,128)(2,1)S(1)} %constant_dynamic-update-slice_fusion.refs_0_), channel_id=1, source_target_pairs={{0,4},{1,3},{2,6},{3,1},{4,0},{5,7},{6,2},{7,5},{8,12},{9,11},{10,... | collective-permute-start | bytes 1572872 | tf_op jit(solution)/shard_map/q0/ppermute | solution.py:70
  17.8 7.5 %collective-permute-start.6 = (bf16[512,256]{1,0:T(8,128)(2,1)S(1)}, bf16[512,256]{1,0:T(8,128)(2,1)S(1)}, u32[]{:S(2)}, u32[]{:S(2)}) collective-permute-start(bf16[512,256]{1,0:T(8,128)(2,1)S(1)} %collective-permute-done), channel_id=1, source_target_pairs={{0,2},{1,5},{2,0},{3,7},{4,6},{5,1},{6,4},{7,3},{8,10},{9,13},{10,... | collective-permute-start | bytes 786440 | tf_op jit(solution)/shard_map/r1/ppermute | solution.py:70
  18.0 11.8 %collective-permute-start.5 = (bf16[512,256]{1,0:T(8,128)(2,1)}, bf16[512,256]{1,0:T(8,128)(2,1)S(1)}, u32[]{:S(2)}, u32[]{:S(2)}) collective-permute-start(bf16[512,256]{1,0:T(8,128)(2,1)} %param.6), channel_id=1, source_target_pairs={{0,24},{1,25},{2,26},{3,27},{4,28},{5,29},{6,30},{7,31},{8,16},{9,... | collective-permute-start | bytes 786440 | tf_op jit(solution)/shard_map/z3/ppermute | solution.py:70
  21.6 10.6 %copy-start.3 = (s32[9]{0:T(128)}, s32[9]{0:T(128)S(1)}, u32[]{:S(2)}) copy-start(s32[9]{0:T(128)S(1)} %select_reduce_fusion.2.starts) | copy-start | bytes 112
  22.0 10.2 %collective-permute-start.4 = (bf16[512,256]{1,0:T(8,128)(2,1)S(1)}, bf16[512,256]{1,0:T(8,128)(2,1)S(1)}, u32[]{:S(2)}, u32[]{:S(2)}) collective-permute-start(bf16[512,256]{1,0:T(8,128)(2,1)S(1)} %collective-permute-done.2), channel_id=1, source_target_pairs={{0,4},{1,3},{2,6},{3,1},{4,0},{5,7},{6,2},{7,5},{8,12},{9,11},{10,... | collective-permute-start | bytes 786440 | tf_op jit(solution)/shard_map/q2a/ppermute | solution.py:70
  23.1 6.7 %collective-permute-start.7 = (bf16[512,256]{1,0:T(8,128)(2,1)S(1)}, bf16[512,256]{1,0:T(8,128)(2,1)S(1)}, u32[]{:S(2)}, u32[]{:S(2)}) collective-permute-start(bf16[512,256]{1,0:T(8,128)(2,1)S(1)} %collective-permute-done.2), channel_id=1, source_target_pairs={{0,2},{1,5},{2,0},{3,7},{4,6},{5,1},{6,4},{7,3},{8,10},{9,13},{10,... | collective-permute-start | bytes 786440 | tf_op jit(solution)/shard_map/r2/ppermute | solution.py:70
  25.4 13.5 %collective-permute-start.13 = (bf16[1024,256]{1,0:T(8,128)(2,1)S(1)}, bf16[1024,256]{1,0:T(8,128)(2,1)S(1)}, u32[]{:S(2)}, u32[]{:S(2)}) collective-permute-start(bf16[1024,256]{1,0:T(8,128)(2,1)S(1)} %collective-permute-done.8.refs_1_), channel_id=1, source_target_pairs={{0,8},{1,9},{2,10},{3,11},{4,12},{5,13},{6,14},{7,15},{8,0},{9,1},... | collective-permute-start | bytes 1572872 | tf_op jit(solution)/shard_map/q1/ppermute | solution.py:70
  29.9 8.9 %collective-permute-start.10 = (bf16[512,256]{1,0:T(8,128)(2,1)S(1)}, bf16[512,256]{1,0:T(8,128)(2,1)S(1)}, u32[]{:S(2)}, u32[]{:S(2)}) collective-permute-start(bf16[512,256]{1,0:T(8,128)(2,1)S(1)} %collective-permute-done.5), channel_id=1, source_target_pairs={{0,2},{1,5},{2,0},{3,7},{4,6},{5,1},{6,4},{7,3},{8,10},{9,13},{10,... | collective-permute-start | bytes 786440 | tf_op jit(solution)/shard_map/r3/ppermute | solution.py:70
  30.4 12.9 %collective-permute-start.9 = (bf16[512,256]{1,0:T(8,128)(2,1)S(1)}, bf16[512,256]{1,0:T(8,128)(2,1)S(1)}, u32[]{:S(2)}, u32[]{:S(2)}) collective-permute-start(bf16[512,256]{1,0:T(8,128)(2,1)S(1)} %collective-permute-done.5), channel_id=1, source_target_pairs={{0,4},{1,3},{2,6},{3,1},{4,0},{5,7},{6,2},{7,5},{8,12},{9,11},{10,... | collective-permute-start | bytes 786440 | tf_op jit(solution)/shard_map/q3a/ppermute | solution.py:70
  34.3 7.6 %collective-permute-start.12 = (bf16[512,256]{1,0:T(8,128)(2,1)S(1)}, bf16[512,256]{1,0:T(8,128)(2,1)S(1)}, u32[]{:S(2)}, u32[]{:S(2)}) collective-permute-start(bf16[512,256]{1,0:T(8,128)(2,1)S(1)} %collective-permute-done.7), channel_id=1, source_target_pairs={{0,4},{1,3},{2,6},{3,1},{4,0},{5,7},{6,2},{7,5},{8,12},{9,11},{10,... | collective-permute-start | bytes 786440 | tf_op jit(solution)/shard_map/q2b/ppermute | solution.py:70
  38.8 6.4 %collective-permute-start.11 = (bf16[512,256]{1,0:T(8,128)(2,1)S(1)}, bf16[512,256]{1,0:T(8,128)(2,1)S(1)}, u32[]{:S(2)}, u32[]{:S(2)}) collective-permute-start(bf16[512,256]{1,0:T(8,128)(2,1)S(1)} %collective-permute-done.10), channel_id=1, source_target_pairs={{0,4},{1,3},{2,6},{3,1},{4,0},{5,7},{6,2},{7,5},{8,12},{9,11},{10,... | collective-permute-start | bytes 786440 | tf_op jit(solution)/shard_map/q3b/ppermute | solution.py:70
  46.2 1.6 %collective-permute-start.14 = (bf16[4,128,256]{2,1,0:T(8,128)(2,1)S(1)}, bf16[4,128,256]{2,1,0:T(8,128)(2,1)S(1)}, u32[]{:S(2)}, u32[]{:S(2)}) collective-permute-start(bf16[4,128,256]{2,1,0:T(8,128)(2,1)S(1)} %get-tuple-element.43), channel_id=1, source_target_pairs={{0,1},{1,0},{2,3},{3,2},{4,5},{5,4},{6,7},{7,6},{8,9},{9,8},{10,11... | collective-permute-start | bytes 786440 | tf_op jit(solution)/shard_map/rows/ppermute | solution.py:75
  48.9 1.4 %collective-permute-start.15 = (f32[136,256]{1,0:T(8,128)S(1)}, f32[136,256]{1,0:T(8,128)S(1)}, u32[]{:S(2)}, u32[]{:S(2)}) collective-permute-start(f32[136,256]{1,0:T(8,128)S(1)} %get-tuple-element.46), channel_id=1, source_target_pairs={{0,1},{1,0},{2,3},{3,2},{4,5},{5,4},{6,7},{7,6},{8,9},{9,8},{10,11... | collective-permute-start | bytes 417800 | tf_op jit(solution)/shard_map/halves/ppermute | solution.py:75
  50.3 5.3 %collective-permute-start.16 = (bf16[136,256]{1,0:T(8,128)(2,1)S(1)}, bf16[136,256]{1,0:T(8,128)(2,1)S(1)}, u32[]{:S(2)}, u32[]{:S(2)}) collective-permute-start(bf16[136,256]{1,0:T(8,128)(2,1)S(1)} %add_convert_fusion), channel_id=1, source_target_pairs={{0,6},{1,7},{2,4},{3,5},{4,2},{5,3},{6,0},{7,1},{8,14},{9,15},{10,... | collective-permute-start | bytes 208904 | tf_op jit(solution)/shard_map/sumd/ppermute | solution.py:70
  53.1 4.6 %collective-permute-start.17 = (bf16[136,256]{1,0:T(8,128)(2,1)S(1)}, bf16[136,256]{1,0:T(8,128)(2,1)S(1)}, u32[]{:S(2)}, u32[]{:S(2)}) collective-permute-start(bf16[136,256]{1,0:T(8,128)(2,1)S(1)} %add_convert_fusion), channel_id=1, source_target_pairs={{0,2},{1,5},{2,0},{3,7},{4,6},{5,1},{6,4},{7,3},{8,10},{9,13},{10,... | collective-permute-start | bytes 208904 | tf_op jit(solution)/shard_map/sum1/ppermute | solution.py:70
  53.9 4.3 %collective-permute-start.18 = (bf16[136,256]{1,0:T(8,128)(2,1)S(1)}, bf16[136,256]{1,0:T(8,128)(2,1)S(1)}, u32[]{:S(2)}, u32[]{:S(2)}) collective-permute-start(bf16[136,256]{1,0:T(8,128)(2,1)S(1)} %add_convert_fusion), channel_id=1, source_target_pairs={{0,4},{1,3},{2,6},{3,1},{4,0},{5,7},{6,2},{7,5},{8,12},{9,11},{10,... | collective-permute-start | bytes 208904 | tf_op jit(solution)/shard_map/sum2/ppermute | solution.py:70
  58.2 4.5 %collective-permute-start.19 = (bf16[136,256]{1,0:T(8,128)(2,1)S(1)}, bf16[136,256]{1,0:T(8,128)(2,1)S(1)}, u32[]{:S(2)}, u32[]{:S(2)}) collective-permute-start(bf16[136,256]{1,0:T(8,128)(2,1)S(1)} %get-tuple-element.49), channel_id=1, source_target_pairs={{0,8},{1,9},{2,10},{3,11},{4,12},{5,13},{6,14},{7,15},{8,0},{9,1},... | collective-permute-start | bytes 208904 | tf_op jit(solution)/shard_map/sum3/ppermute | solution.py:70
  59.7 8.1 %collective-permute-start.20 = (bf16[136,256]{1,0:T(8,128)(2,1)S(1)}, bf16[136,256]{1,0:T(8,128)(2,1)S(1)}, u32[]{:S(2)}, u32[]{:S(2)}) collective-permute-start(bf16[136,256]{1,0:T(8,128)(2,1)S(1)} %get-tuple-element.49), channel_id=1, source_target_pairs={{0,16},{1,17},{2,18},{3,19},{4,20},{5,21},{6,22},{7,23},{8,24},{9,... | collective-permute-start | bytes 208904 | tf_op jit(solution)/shard_map/sum4/ppermute | solution.py:70
  61.3 6.6 %collective-permute-start.21 = (bf16[136,256]{1,0:T(8,128)(2,1)S(1)}, bf16[136,256]{1,0:T(8,128)(2,1)S(1)}, u32[]{:S(2)}, u32[]{:S(2)}) collective-permute-start(bf16[136,256]{1,0:T(8,128)(2,1)S(1)} %get-tuple-element.49), channel_id=1, source_target_pairs={{0,24},{1,25},{2,26},{3,27},{4,28},{5,29},{6,30},{7,31},{8,16},{9,... | collective-permute-start | bytes 208904 | tf_op jit(solution)/shard_map/sum5/ppermute | solution.py:70
  67.9 1.4 %collective-permute-start.22 = (f32[136,256]{1,0:T(8,128)S(1)}, f32[136,256]{1,0:T(8,128)S(1)}, u32[]{:S(2)}, u32[]{:S(2)}) collective-permute-start(f32[136,256]{1,0:T(8,128)S(1)} %add_add_fusion.part), channel_id=1, source_target_pairs={{0,1},{1,0},{2,3},{3,2},{4,5},{5,4},{6,7},{7,6},{8,9},{9,8},{10,11... | collective-permute-start | bytes 417800 | tf_op jit(solution)/shard_map/back/ppermute | solution.py:75
  (6 other events, 18.1 us)

commit v5 on v4

--- a/solution.py
+++ b/solution.py
@@ -225,7 +225,7 @@
     for g, array in zip(groups, arrays):
         add_group(entries, starts[g], starts[g + 1], tiles, array, acc)
     half = give.shape[0]
-    give[...] = acc[half : 2 * half].astype(give.dtype)
+    give[...] = acc[half : 2 * half]
 
 
 def whole(space):
@@ -250,7 +250,7 @@
 
 def add_late(work, arrays, groups, acc, row_blocks):
     entries, starts, tiles = work
-    half = VMEM((row_blocks // 2, 128, arrays[0].shape[1]), jnp.bfloat16)
+    half = VMEM((row_blocks // 2, 128, arrays[0].shape[1]), jnp.float32)
     return pl.pallas_call(
         functools.partial(late_kernel, groups),
         out_shape=(VMEM(acc.shape, jnp.float32), half),
@@ -264,7 +264,7 @@
 
 
 def dense_kernel(core, mine, theirs, weight, bias, grad_out, output, keep, give, full):
-    hidden = (mine[: theirs.shape[0]] + theirs[...].astype(jnp.float32)).reshape(grad_out.shape).astype(jnp.bfloat16)
+    hidden = (mine[: theirs.shape[0]] + theirs[...]).reshape(grad_out.shape).astype(jnp.bfloat16)
     pre_act = jnp.dot(hidden, weight[...], preferred_element_type=jnp.float32) + bias[...]
     sigma = 1.0 / (1.0 + jnp.exp(-pre_act))
     output[...] = (pre_act * sigma).astype(jnp.bfloat16)

time: 70.6 us -> 71 us (level)
  waiting for transfers between devices: 27.8 us -> 28.6 us
  transfers between devices with their start and end apart: 23 -> 23, of which waited for: 12 -> 12; matrix products, arithmetic and copies ran while one was open for 3% -> 3% of each run, Pallas kernels for 10% -> 9%
where the time goes in v5:
time: 71 us; the launch traced here: 70.7 us
  waiting for transfers between devices  28.6 us (40%)
  starting transfers between devices  26.6 us (37%)
  Pallas kernels  9.34 us (13%)
  blocking collectives  1.98 us (3%)
  local copies, waits for them, and re-layouts  1.71 us (2%)
  other arithmetic  1.55 us (2%)
  between operations  0.88 us (1%)
    ppermute x19, starting transfers between devices, send(): return lax.ppermute(x, BOTH, perm)  25.8 us
    ppermute x19, waiting for transfers between devices, send(): return lax.ppermute(x, BOTH, perm)  24.1 us
    ppermute x4, waiting for transfers between devices, swap(): return lax.ppermute(x, 'replica', [(0, 1), (1, 0)])  4.47 us
    pallas_call x3, Pallas kernels, add_groups(): pl.pallas_call(functools.partial(add_kernel, groups, fresh), out_shape=sh...  4.18 us
    pallas_call x1, Pallas kernels, gather_tiles(): pl.pallas_call(functools.partial(gather_kernel, own.shape[0]), out_shape=...  2.04 us
    all_gather x1, blocking collectives, shards(): index = lax.all_gather(index, 'replica', axis=0, tiled=True)  1.98 us
    unnamed x15, local copies, waits for them, and re-layouts  1.69 us
  transfers between devices with their start and end apart: 23, of which 12 were waited for; matrix products, arithmetic and copies ran while one was open for 3% of the time, Pallas kernels for 9%

profile of v5, /device:TPU:0, one launch (start us, length us, event | category | flops | bytes accessed | tf_op | source)
XLA Modules:
  0.0 70.7 jit_solution(12666806191459444730)
XLA Ops:
  1.1 2.6 %collective-permute-start.1 = (bf16[512,256]{1,0:T(8,128)(2,1)}, bf16[512,256]{1,0:T(8,128)(2,1)S(1)}, u32[]{:S(2)}, u32[]{:S(2)}) collective-permute-start(bf16[512,256]{1,0:T(8,128)(2,1)} %param.6), channel_id=1, source_target_pairs={{0,2},{1,5},{2,0},{3,7},{4,6},{5,1},{6,4},{7,3},{8,10},{9,13},{10,... | collective-permute-start | bytes 786440 | tf_op jit(solution)/shard_map/r0/ppermute | solution.py:70
  3.7 1.6 %collective-permute-start = (bf16[512,256]{1,0:T(8,128)(2,1)}, bf16[512,256]{1,0:T(8,128)(2,1)S(1)}, u32[]{:S(2)}, u32[]{:S(2)}) collective-permute-start(bf16[512,256]{1,0:T(8,128)(2,1)} %param.6), channel_id=1, source_target_pairs={{0,8},{1,9},{2,10},{3,11},{4,12},{5,13},{6,14},{7,15},{8,0},{9,1},... | collective-permute-start | bytes 786440 | tf_op jit(solution)/shard_map/z1/ppermute | solution.py:70
  5.3 2.6 %collective-permute-start.2 = (bf16[512,256]{1,0:T(8,128)(2,1)}, bf16[512,256]{1,0:T(8,128)(2,1)S(1)}, u32[]{:S(2)}, u32[]{:S(2)}) collective-permute-start(bf16[512,256]{1,0:T(8,128)(2,1)} %param.6), channel_id=1, source_target_pairs={{0,16},{1,17},{2,18},{3,19},{4,20},{5,21},{6,22},{7,23},{8,24},{9,... | collective-permute-start | bytes 786440 | tf_op jit(solution)/shard_map/z2/ppermute | solution.py:70
  8.9 1.6 %collective-permute-start.8 = (bf16[1024,256]{1,0:T(8,128)(2,1)S(1)}, bf16[1024,256]{1,0:T(8,128)(2,1)S(1)}, u32[]{:S(2)}, u32[]{:S(2)}) collective-permute-start(bf16[1024,256]{1,0:T(8,128)(2,1)S(1)} %constant_dynamic-update-slice_fusion.refs_0_), channel_id=1, source_target_pairs={{0,4},{1,3},{2,6},{3,1},{4,0},{5,7},{6,2},{7,5},{8,12},{9,11},{10,... | collective-permute-start | bytes 1572872 | tf_op jit(solution)/shard_map/q0/ppermute | solution.py:70
  10.5 2.0 %all_gather.3 = s32[256,2]{0,1:T(2,128)S(1)} all-gather(s32[128,2]{0,1:T(2,128)} %param.8), channel_id=1, replica_groups=mesh['section'=16,'replica'=2] {'replica'}, dimensions={0}, use_global_device_ids=true | all-gather | bytes 3072 | tf_op jit(solution)/shard_map/all_gather | solution.py:342
  12.5 5.3 %collective-permute-done = bf16[512,256]{1,0:T(8,128)(2,1)S(1)} collective-permute-done((bf16[512,256]{1,0:T(8,128)(2,1)}, bf16[512,256]{1,0:T(8,128)(2,1)S(1)}, u32[]{:S(2)}, u32[]{:S(2)}) %collective-permute-start) | collective-permute-done | bytes 262176 | tf_op jit(solution)/shard_map/z1/ppermute | solution.py:70
  18.0 3.3 %collective-permute-start.5 = (bf16[512,256]{1,0:T(8,128)(2,1)}, bf16[512,256]{1,0:T(8,128)(2,1)S(1)}, u32[]{:S(2)}, u32[]{:S(2)}) collective-permute-start(bf16[512,256]{1,0:T(8,128)(2,1)} %param.6), channel_id=1, source_target_pairs={{0,24},{1,25},{2,26},{3,27},{4,28},{5,29},{6,30},{7,31},{8,16},{9,... | collective-permute-start | bytes 786440 | tf_op jit(solution)/shard_map/z3/ppermute | solution.py:70
  25.5 4.3 %collective-permute-done.7 = bf16[512,256]{1,0:T(8,128)(2,1)S(1)} collective-permute-done((bf16[512,256]{1,0:T(8,128)(2,1)S(1)}, bf16[512,256]{1,0:T(8,128)(2,1)S(1)}, u32[]{:S(2)}, u32[]{:S(2)}) %collective-permute-start.7) | collective-permute-done | bytes 262176 | tf_op jit(solution)/shard_map/r2/ppermute | solution.py:70
  30.4 1.7 %collective-permute-start.9 = (bf16[512,256]{1,0:T(8,128)(2,1)S(1)}, bf16[512,256]{1,0:T(8,128)(2,1)S(1)}, u32[]{:S(2)}, u32[]{:S(2)}) collective-permute-start(bf16[512,256]{1,0:T(8,128)(2,1)S(1)} %collective-permute-done.5), channel_id=1, source_target_pairs={{0,4},{1,3},{2,6},{3,1},{4,0},{5,7},{6,2},{7,5},{8,12},{9,11},{10,... | collective-permute-start | bytes 786440 | tf_op jit(solution)/shard_map/q3a/ppermute | solution.py:70
  32.2 2.0 %gather_tiles.1.tiles = bf16[272,128,128]{2,1,0:T(8,128)(2,1)S(1)} custom-call(s32[272]{0:T(512)} %broadcast_add_fusion.entries, s32[9]{0:T(128)} %copy-done.3, bf16[128,128,128]{2,1,0:T(8,128)(2,1)} %own.1, bf16[128,128,128]{2,1,0:T(8,128)(2,1)} %collective-permute-done.3.other), custom_call_target="tpu_custom_call" | custom-call | bytes 1024 | tf_op jit(solution)/shard_map/gather_tiles/pallas_call | solution.py:181
  35.2 1.5 %add_a.1.refs_2_ = f32[9,128,256]{2,1,0:T(8,128)S(1)} custom-call(s32[272]{0:T(512)S(1)} %copy-done.2, s32[9]{0:T(128)S(1)} %copy-done.4, bf16[272,128,128]{2,1,0:T(8,128)(2,1)S(1)} %gather_tiles.1.tiles, bf16[1024,256]{1,0:T(8,128)(2,1)S(1)} %constant_dynamic-update-slice_fusion.refs_0_, bf16[1024,256]{1,0:T(8,128)(2,1)S(1)} %collective-permute-done.8.refs_1_, ...), custom_call_target="tpu_custom_call" | custom-call | flops 4294967296 | bytes 4194304 | tf_op jit(solution)/shard_map/add_a/pallas_call | solution.py:239
  36.7 2.1 %collective-permute-done.10 = bf16[512,256]{1,0:T(8,128)(2,1)S(1)} collective-permute-done((bf16[512,256]{1,0:T(8,128)(2,1)S(1)}, bf16[512,256]{1,0:T(8,128)(2,1)S(1)}, u32[]{:S(2)}, u32[]{:S(2)}) %collective-permute-start.10) | collective-permute-done | bytes 262176 | tf_op jit(solution)/shard_map/r3/ppermute | solution.py:70
  38.8 1.6 %collective-permute-start.11 = (bf16[512,256]{1,0:T(8,128)(2,1)S(1)}, bf16[512,256]{1,0:T(8,128)(2,1)S(1)}, u32[]{:S(2)}, u32[]{:S(2)}) collective-permute-start(bf16[512,256]{1,0:T(8,128)(2,1)S(1)} %collective-permute-done.10), channel_id=1, source_target_pairs={{0,4},{1,3},{2,6},{3,1},{4,0},{5,7},{6,2},{7,5},{8,12},{9,11},{10,... | collective-permute-start | bytes 786440 | tf_op jit(solution)/shard_map/q3b/ppermute | solution.py:70
  40.5 1.4 %add_b.1.refs_2_ = f32[9,128,256]{2,1,0:T(8,128)S(1)} custom-call(s32[272]{0:T(512)S(1)} %copy-done.2, s32[9]{0:T(128)S(1)} %copy-done.5, bf16[272,128,128]{2,1,0:T(8,128)(2,1)S(1)} %gather_tiles.1.tiles, bf16[1024,256]{1,0:T(8,128)(2,1)S(1)} %collective-permute-done.13.refs_0_, ...), custom_call_target="tpu_custom_call", output_to_operand_aliasing={{}: (5, {})} | custom-call | flops 4294967296 | bytes 4194304 | tf_op jit(solution)/shard_map/add_b/pallas_call | solution.py:239
  43.2 2.0 %collective-permute-done.11 = bf16[512,256]{1,0:T(8,128)(2,1)S(1)} collective-permute-done((bf16[512,256]{1,0:T(8,128)(2,1)S(1)}, bf16[512,256]{1,0:T(8,128)(2,1)S(1)}, u32[]{:S(2)}, u32[]{:S(2)}) %collective-permute-start.11) | collective-permute-done | bytes 262176 | tf_op jit(solution)/shard_map/q3b/ppermute | solution.py:70
  46.7 1.9 %collective-permute-done.14.theirs = f32[4,128,256]{2,1,0:T(8,128)S(1)} collective-permute-done((f32[4,128,256]{2,1,0:T(8,128)S(1)}, f32[4,128,256]{2,1,0:T(8,128)S(1)}, u32[]{:S(2)}, u32[]{:S(2)}) %collective-permute-start.14) | collective-permute-done | bytes 524320 | tf_op jit(solution)/shard_map/rows/ppermute | solution.py:75
  51.1 2.4 %collective-permute-start.16 = (bf16[136,256]{1,0:T(8,128)(2,1)S(1)}, bf16[136,256]{1,0:T(8,128)(2,1)S(1)}, u32[]{:S(2)}, u32[]{:S(2)}) collective-permute-start(bf16[136,256]{1,0:T(8,128)(2,1)S(1)} %add_convert_fusion), channel_id=1, source_target_pairs={{0,6},{1,7},{2,4},{3,5},{4,2},{5,3},{6,0},{7,1},{8,14},{9,15},{10,... | collective-permute-start | bytes 208904 | tf_op jit(solution)/shard_map/sumd/ppermute | solution.py:70
  54.7 1.8 %collective-permute-done.16 = bf16[136,256]{1,0:T(8,128)(2,1)S(1)} collective-permute-done((bf16[136,256]{1,0:T(8,128)(2,1)S(1)}, bf16[136,256]{1,0:T(8,128)(2,1)S(1)}, u32[]{:S(2)}, u32[]{:S(2)}) %collective-permute-start.16) | collective-permute-done | bytes 69664 | tf_op jit(solution)/shard_map/sumd/ppermute | solution.py:70
  56.4 1.4 %collective-permute-done.17 = bf16[136,256]{1,0:T(8,128)(2,1)S(1)} collective-permute-done((bf16[136,256]{1,0:T(8,128)(2,1)S(1)}, bf16[136,256]{1,0:T(8,128)(2,1)S(1)}, u32[]{:S(2)}, u32[]{:S(2)}) %collective-permute-start.17) | collective-permute-done | bytes 69664 | tf_op jit(solution)/shard_map/sum1/ppermute | solution.py:70
  58.1 2.0 %collective-permute-start.19 = (bf16[136,256]{1,0:T(8,128)(2,1)S(1)}, bf16[136,256]{1,0:T(8,128)(2,1)S(1)}, u32[]{:S(2)}, u32[]{:S(2)}) collective-permute-start(bf16[136,256]{1,0:T(8,128)(2,1)S(1)} %get-tuple-element.49), channel_id=1, source_target_pairs={{0,8},{1,9},{2,10},{3,11},{4,12},{5,13},{6,14},{7,15},{8,0},{9,1},... | collective-permute-start | bytes 208904 | tf_op jit(solution)/shard_map/sum3/ppermute | solution.py:70
  60.1 1.3 %collective-permute-start.20 = (bf16[136,256]{1,0:T(8,128)(2,1)S(1)}, bf16[136,256]{1,0:T(8,128)(2,1)S(1)}, u32[]{:S(2)}, u32[]{:S(2)}) collective-permute-start(bf16[136,256]{1,0:T(8,128)(2,1)S(1)} %get-tuple-element.49), channel_id=1, source_target_pairs={{0,16},{1,17},{2,18},{3,19},{4,20},{5,21},{6,22},{7,23},{8,24},{9,... | collective-permute-start | bytes 208904 | tf_op jit(solution)/shard_map/sum4/ppermute | solution.py:70
  61.4 1.4 %collective-permute-start.21 = (bf16[136,256]{1,0:T(8,128)(2,1)S(1)}, bf16[136,256]{1,0:T(8,128)(2,1)S(1)}, u32[]{:S(2)}, u32[]{:S(2)}) collective-permute-start(bf16[136,256]{1,0:T(8,128)(2,1)S(1)} %get-tuple-element.49), channel_id=1, source_target_pairs={{0,24},{1,25},{2,26},{3,27},{4,28},{5,29},{6,30},{7,31},{8,16},{9,... | collective-permute-start | bytes 208904 | tf_op jit(solution)/shard_map/sum5/ppermute | solution.py:70
  62.7 5.7 %collective-permute-done.20 = bf16[136,256]{1,0:T(8,128)(2,1)S(1)} collective-permute-done((bf16[136,256]{1,0:T(8,128)(2,1)S(1)}, bf16[136,256]{1,0:T(8,128)(2,1)S(1)}, u32[]{:S(2)}, u32[]{:S(2)}) %collective-permute-start.20) | collective-permute-done | bytes 69664 | tf_op jit(solution)/shard_map/sum4/ppermute | solution.py:70
  68.6 1.3 %collective-permute-done.22.rest = f32[136,256]{1,0:T(8,128)S(1)} collective-permute-done((f32[136,256]{1,0:T(8,128)S(1)}, f32[136,256]{1,0:T(8,128)S(1)}, u32[]{:S(2)}, u32[]{:S(2)}) %collective-permute-start.22) | collective-permute-done | bytes 139296 | tf_op jit(solution)/shard_map/back/ppermute | solution.py:75
  (66 shorter events, 15.1 us)
Async XLA Ops:
  0.6 21.4 %collective-permute-start.3 = (bf16[128,128,128]{2,1,0:T(8,128)(2,1)}, bf16[128,128,128]{2,1,0:T(8,128)(2,1)}, u32[]{:S(2)}, u32[]{:S(2)}) collective-permute-start(bf16[128,128,128]{2,1,0:T(8,128)(2,1)} %own.1), channel_id=1, source_target_pairs={{0,1},{1,0},{2,3},{3,2},{4,5},{5,4},{6,7},{7,6},{8,9},{9,8},{10,11... | collective-permute-start | bytes 12582920 | tf_op jit(solution)/shard_map/tiles/ppermute | solution.py:75
  1.1 7.7 %collective-permute-start.1 = (bf16[512,256]{1,0:T(8,128)(2,1)}, bf16[512,256]{1,0:T(8,128)(2,1)S(1)}, u32[]{:S(2)}, u32[]{:S(2)}) collective-permute-start(bf16[512,256]{1,0:T(8,128)(2,1)} %param.6), channel_id=1, source_target_pairs={{0,2},{1,5},{2,0},{3,7},{4,6},{5,1},{6,4},{7,3},{8,10},{9,13},{10,... | collective-permute-start | bytes 786440 | tf_op jit(solution)/shard_map/r0/ppermute | solution.py:70
  3.7 14.1 %collective-permute-start = (bf16[512,256]{1,0:T(8,128)(2,1)}, bf16[512,256]{1,0:T(8,128)(2,1)S(1)}, u32[]{:S(2)}, u32[]{:S(2)}) collective-permute-start(bf16[512,256]{1,0:T(8,128)(2,1)} %param.6), channel_id=1, source_target_pairs={{0,8},{1,9},{2,10},{3,11},{4,12},{5,13},{6,14},{7,15},{8,0},{9,1},... | collective-permute-start | bytes 786440 | tf_op jit(solution)/shard_map/z1/ppermute | solution.py:70
  5.3 16.7 %collective-permute-start.2 = (bf16[512,256]{1,0:T(8,128)(2,1)}, bf16[512,256]{1,0:T(8,128)(2,1)S(1)}, u32[]{:S(2)}, u32[]{:S(2)}) collective-permute-start(bf16[512,256]{1,0:T(8,128)(2,1)} %param.6), channel_id=1, source_target_pairs={{0,16},{1,17},{2,18},{3,19},{4,20},{5,21},{6,22},{7,23},{8,24},{9,... | collective-permute-start | bytes 786440 | tf_op jit(solution)/shard_map/z2/ppermute | solution.py:70
  8.9 16.4 %collective-permute-start.8 = (bf16[1024,256]{1,0:T(8,128)(2,1)S(1)}, bf16[1024,256]{1,0:T(8,128)(2,1)S(1)}, u32[]{:S(2)}, u32[]{:S(2)}) collective-permute-start(bf16[1024,256]{1,0:T(8,128)(2,1)S(1)} %constant_dynamic-update-slice_fusion.refs_0_), channel_id=1, source_target_pairs={{0,4},{1,3},{2,6},{3,1},{4,0},{5,7},{6,2},{7,5},{8,12},{9,11},{10,... | collective-permute-start | bytes 1572872 | tf_op jit(solution)/shard_map/q0/ppermute | solution.py:70
  17.8 7.5 %collective-permute-start.6 = (bf16[512,256]{1,0:T(8,128)(2,1)S(1)}, bf16[512,256]{1,0:T(8,128)(2,1)S(1)}, u32[]{:S(2)}, u32[]{:S(2)}) collective-permute-start(bf16[512,256]{1,0:T(8,128)(2,1)S(1)} %collective-permute-done), channel_id=1, source_target_pairs={{0,2},{1,5},{2,0},{3,7},{4,6},{5,1},{6,4},{7,3},{8,10},{9,13},{10,... | collective-permute-start | bytes 786440 | tf_op jit(solution)/shard_map/r1/ppermute | solution.py:70
  18.0 11.8 %collective-permute-start.5 = (bf16[512,256]{1,0:T(8,128)(2,1)}, bf16[512,256]{1,0:T(8,128)(2,1)S(1)}, u32[]{:S(2)}, u32[]{:S(2)}) collective-permute-start(bf16[512,256]{1,0:T(8,128)(2,1)} %param.6), channel_id=1, source_target_pairs={{0,24},{1,25},{2,26},{3,27},{4,28},{5,29},{6,30},{7,31},{8,16},{9,... | collective-permute-start | bytes 786440 | tf_op jit(solution)/shard_map/z3/ppermute | solution.py:70
  21.6 10.6 %copy-start.3 = (s32[9]{0:T(128)}, s32[9]{0:T(128)S(1)}, u32[]{:S(2)}) copy-start(s32[9]{0:T(128)S(1)} %select_reduce_fusion.2.starts) | copy-start | bytes 112
  22.0 10.2 %collective-permute-start.4 = (bf16[512,256]{1,0:T(8,128)(2,1)S(1)}, bf16[512,256]{1,0:T(8,128)(2,1)S(1)}, u32[]{:S(2)}, u32[]{:S(2)}) collective-permute-start(bf16[512,256]{1,0:T(8,128)(2,1)S(1)} %collective-permute-done.2), channel_id=1, source_target_pairs={{0,4},{1,3},{2,6},{3,1},{4,0},{5,7},{6,2},{7,5},{8,12},{9,11},{10,... | collective-permute-start | bytes 786440 | tf_op jit(solution)/shard_map/q2a/ppermute | solution.py:70
  23.1 6.7 %collective-permute-start.7 = (bf16[512,256]{1,0:T(8,128)(2,1)S(1)}, bf16[512,256]{1,0:T(8,128)(2,1)S(1)}, u32[]{:S(2)}, u32[]{:S(2)}) collective-permute-start(bf16[512,256]{1,0:T(8,128)(2,1)S(1)} %collective-permute-done.2), channel_id=1, source_target_pairs={{0,2},{1,5},{2,0},{3,7},{4,6},{5,1},{6,4},{7,3},{8,10},{9,13},{10,... | collective-permute-start | bytes 786440 | tf_op jit(solution)/shard_map/r2/ppermute | solution.py:70
  25.4 13.5 %collective-permute-start.13 = (bf16[1024,256]{1,0:T(8,128)(2,1)S(1)}, bf16[1024,256]{1,0:T(8,128)(2,1)S(1)}, u32[]{:S(2)}, u32[]{:S(2)}) collective-permute-start(bf16[1024,256]{1,0:T(8,128)(2,1)S(1)} %collective-permute-done.8.refs_1_), channel_id=1, source_target_pairs={{0,8},{1,9},{2,10},{3,11},{4,12},{5,13},{6,14},{7,15},{8,0},{9,1},... | collective-permute-start | bytes 1572872 | tf_op jit(solution)/shard_map/q1/ppermute | solution.py:70
  29.9 8.9 %collective-permute-start.10 = (bf16[512,256]{1,0:T(8,128)(2,1)S(1)}, bf16[512,256]{1,0:T(8,128)(2,1)S(1)}, u32[]{:S(2)}, u32[]{:S(2)}) collective-permute-start(bf16[512,256]{1,0:T(8,128)(2,1)S(1)} %collective-permute-done.5), channel_id=1, source_target_pairs={{0,2},{1,5},{2,0},{3,7},{4,6},{5,1},{6,4},{7,3},{8,10},{9,13},{10,... | collective-permute-start | bytes 786440 | tf_op jit(solution)/shard_map/r3/ppermute | solution.py:70
  30.4 12.8 %collective-permute-start.9 = (bf16[512,256]{1,0:T(8,128)(2,1)S(1)}, bf16[512,256]{1,0:T(8,128)(2,1)S(1)}, u32[]{:S(2)}, u32[]{:S(2)}) collective-permute-start(bf16[512,256]{1,0:T(8,128)(2,1)S(1)} %collective-permute-done.5), channel_id=1, source_target_pairs={{0,4},{1,3},{2,6},{3,1},{4,0},{5,7},{6,2},{7,5},{8,12},{9,11},{10,... | collective-permute-start | bytes 786440 | tf_op jit(solution)/shard_map/q3a/ppermute | solution.py:70
  34.2 7.7 %collective-permute-start.12 = (bf16[512,256]{1,0:T(8,128)(2,1)S(1)}, bf16[512,256]{1,0:T(8,128)(2,1)S(1)}, u32[]{:S(2)}, u32[]{:S(2)}) collective-permute-start(bf16[512,256]{1,0:T(8,128)(2,1)S(1)} %collective-permute-done.7), channel_id=1, source_target_pairs={{0,4},{1,3},{2,6},{3,1},{4,0},{5,7},{6,2},{7,5},{8,12},{9,11},{10,... | collective-permute-start | bytes 786440 | tf_op jit(solution)/shard_map/q2b/ppermute | solution.py:70
  38.8 6.4 %collective-permute-start.11 = (bf16[512,256]{1,0:T(8,128)(2,1)S(1)}, bf16[512,256]{1,0:T(8,128)(2,1)S(1)}, u32[]{:S(2)}, u32[]{:S(2)}) collective-permute-start(bf16[512,256]{1,0:T(8,128)(2,1)S(1)} %collective-permute-done.10), channel_id=1, source_target_pairs={{0,4},{1,3},{2,6},{3,1},{4,0},{5,7},{6,2},{7,5},{8,12},{9,11},{10,... | collective-permute-start | bytes 786440 | tf_op jit(solution)/shard_map/q3b/ppermute | solution.py:70
  46.6 2.0 %collective-permute-start.14 = (f32[4,128,256]{2,1,0:T(8,128)S(1)}, f32[4,128,256]{2,1,0:T(8,128)S(1)}, u32[]{:S(2)}, u32[]{:S(2)}) collective-permute-start(f32[4,128,256]{2,1,0:T(8,128)S(1)} %get-tuple-element.43), channel_id=1, source_target_pairs={{0,1},{1,0},{2,3},{3,2},{4,5},{5,4},{6,7},{7,6},{8,9},{9,8},{10,11... | collective-permute-start | bytes 1572872 | tf_op jit(solution)/shard_map/rows/ppermute | solution.py:75
  49.7 1.4 %collective-permute-start.15 = (f32[136,256]{1,0:T(8,128)S(1)}, f32[136,256]{1,0:T(8,128)S(1)}, u32[]{:S(2)}, u32[]{:S(2)}) collective-permute-start(f32[136,256]{1,0:T(8,128)S(1)} %get-tuple-element.46), channel_id=1, source_target_pairs={{0,1},{1,0},{2,3},{3,2},{4,5},{5,4},{6,7},{7,6},{8,9},{9,8},{10,11... | collective-permute-start | bytes 417800 | tf_op jit(solution)/shard_map/halves/ppermute | solution.py:75
  51.1 5.3 %collective-permute-start.16 = (bf16[136,256]{1,0:T(8,128)(2,1)S(1)}, bf16[136,256]{1,0:T(8,128)(2,1)S(1)}, u32[]{:S(2)}, u32[]{:S(2)}) collective-permute-start(bf16[136,256]{1,0:T(8,128)(2,1)S(1)} %add_convert_fusion), channel_id=1, source_target_pairs={{0,6},{1,7},{2,4},{3,5},{4,2},{5,3},{6,0},{7,1},{8,14},{9,15},{10,... | collective-permute-start | bytes 208904 | tf_op jit(solution)/shard_map/sumd/ppermute | solution.py:70
  53.5 4.3 %collective-permute-start.17 = (bf16[136,256]{1,0:T(8,128)(2,1)S(1)}, bf16[136,256]{1,0:T(8,128)(2,1)S(1)}, u32[]{:S(2)}, u32[]{:S(2)}) collective-permute-start(bf16[136,256]{1,0:T(8,128)(2,1)S(1)} %add_convert_fusion), channel_id=1, source_target_pairs={{0,2},{1,5},{2,0},{3,7},{4,6},{5,1},{6,4},{7,3},{8,10},{9,13},{10,... | collective-permute-start | bytes 208904 | tf_op jit(solution)/shard_map/sum1/ppermute | solution.py:70
  53.8 4.3 %collective-permute-start.18 = (bf16[136,256]{1,0:T(8,128)(2,1)S(1)}, bf16[136,256]{1,0:T(8,128)(2,1)S(1)}, u32[]{:S(2)}, u32[]{:S(2)}) collective-permute-start(bf16[136,256]{1,0:T(8,128)(2,1)S(1)} %add_convert_fusion), channel_id=1, source_target_pairs={{0,4},{1,3},{2,6},{3,1},{4,0},{5,7},{6,2},{7,5},{8,12},{9,11},{10,... | collective-permute-start | bytes 208904 | tf_op jit(solution)/shard_map/sum2/ppermute | solution.py:70
  58.1 4.6 %collective-permute-start.19 = (bf16[136,256]{1,0:T(8,128)(2,1)S(1)}, bf16[136,256]{1,0:T(8,128)(2,1)S(1)}, u32[]{:S(2)}, u32[]{:S(2)}) collective-permute-start(bf16[136,256]{1,0:T(8,128)(2,1)S(1)} %get-tuple-element.49), channel_id=1, source_target_pairs={{0,8},{1,9},{2,10},{3,11},{4,12},{5,13},{6,14},{7,15},{8,0},{9,1},... | collective-permute-start | bytes 208904 | tf_op jit(solution)/shard_map/sum3/ppermute | solution.py:70
  60.1 8.4 %collective-permute-start.20 = (bf16[136,256]{1,0:T(8,128)(2,1)S(1)}, bf16[136,256]{1,0:T(8,128)(2,1)S(1)}, u32[]{:S(2)}, u32[]{:S(2)}) collective-permute-start(bf16[136,256]{1,0:T(8,128)(2,1)S(1)} %get-tuple-element.49), channel_id=1, source_target_pairs={{0,16},{1,17},{2,18},{3,19},{4,20},{5,21},{6,22},{7,23},{8,24},{9,... | collective-permute-start | bytes 208904 | tf_op jit(solution)/shard_map/sum4/ppermute | solution.py:70
  61.4 7.1 %collective-permute-start.21 = (bf16[136,256]{1,0:T(8,128)(2,1)S(1)}, bf16[136,256]{1,0:T(8,128)(2,1)S(1)}, u32[]{:S(2)}, u32[]{:S(2)}) collective-permute-start(bf16[136,256]{1,0:T(8,128)(2,1)S(1)} %get-tuple-element.49), channel_id=1, source_target_pairs={{0,24},{1,25},{2,26},{3,27},{4,28},{5,29},{6,30},{7,31},{8,16},{9,... | collective-permute-start | bytes 208904 | tf_op jit(solution)/shard_map/sum5/ppermute | solution.py:70
  68.5 1.4 %collective-permute-start.22 = (f32[136,256]{1,0:T(8,128)S(1)}, f32[136,256]{1,0:T(8,128)S(1)}, u32[]{:S(2)}, u32[]{:S(2)}) collective-permute-start(f32[136,256]{1,0:T(8,128)S(1)} %add_add_fusion.part), channel_id=1, source_target_pairs={{0,1},{1,0},{2,3},{3,2},{4,5},{5,4},{6,7},{7,6},{8,9},{9,8},{10,11... | collective-permute-start | bytes 417800 | tf_op jit(solution)/shard_map/back/ppermute | solution.py:75
  (6 other events, 20.4 us)

commit v6 on v5

--- a/solution.py
+++ b/solution.py
@@ -124,9 +124,11 @@
     x_apart, y_apart, z_apart = apart & 1, (apart >> 1) & 1, apart >> 2
     near = jnp.where(core == 0, x_apart, y_apart)
     far = jnp.where(core == 0, y_apart, x_apart)
-    groups = 8
-    group = jnp.where(live, 2 * z_apart + far, groups)
-    block = half * near + col % half
+    groups = 9
+    array = 2 * z_apart + far
+    last = (array == 7) & (near == 1)
+    group = jnp.where(live, array + last.astype(jnp.int32), groups)
+    block = jnp.where(last, 0, half * near) + col % half
     mine = tile // count == core
     entry = (tile % count + jnp.where(mine, 0, count)) | (block << 8) | ((row ^ (half * core)) << 12)
     spare = row_blocks << 12
@@ -145,7 +147,7 @@
 
 
 def gather_kernel(count, entries, starts, own, other, out, sem):
-    pairs = starts[8] // 2
+    pairs = starts[9] // 2
 
     def fetch(m):
         tile = entries[m] & 255
@@ -359,14 +361,14 @@
     q3a = second_hop(z3, "q3a")
     pair3 = join(z3, r3)
     q1, pair3 = after(q1, pair3)
-    q3 = join(q3a, second_hop(r3, "q3b"))
+    q3b = second_hop(r3, "q3b")
     entries, starts = work_list(index, slots, row_blocks)
     tiles = gather_tiles(entries, starts, adj_tiles, other_tiles)
     work = (entries, starts, tiles)
     acc = add_groups(work, (pair0, q0, pair1), (0, 1, 2), None, row_blocks, "add_a")
     acc = add_groups(work, (q1, pair2), (3, 4), acc, row_blocks, "add_b")
-    acc = add_groups(work, (q2, pair3), (5, 6), acc, row_blocks, "add_c")
-    mine, give = add_late(work, (q3,), (7,), acc, row_blocks)
+    acc = add_groups(work, (q2, pair3, q3a), (5, 6, 7), acc, row_blocks, "add_c")
+    mine, give = add_late(work, (q3b,), (8,), acc, row_blocks)
     theirs = swap(give, "rows")
     output, keep, give = dense(core, mine, theirs, weight, bias_vec, grad_out)
     part = keep + swap(give, "halves")

time: 71 us -> 72.2 us (1.017)
    ppermute x19, waiting for transfers between devices: 24.1 us -> 24.8 us  [send(): return lax.ppermute(x, BOTH, perm)]
  transfers between devices with their start and end apart: 23 -> 23, of which waited for: 12 -> 13; matrix products, arithmetic and copies ran while one was open for 3% -> 3% of each run, Pallas kernels for 9% -> 9%
where the time goes in v6:
time: 72.2 us; the launch traced here: 71.8 us
  waiting for transfers between devices  29.3 us (41%)
  starting transfers between devices  26.9 us (37%)
  Pallas kernels  9.45 us (13%)
  blocking collectives  1.98 us (3%)
  local copies, waits for them, and re-layouts  1.71 us (2%)
  other arithmetic  1.55 us (2%)
  between operations  0.87 us (1%)
    ppermute x19, starting transfers between devices, send(): return lax.ppermute(x, BOTH, perm)  26.1 us
    ppermute x19, waiting for transfers between devices, send(): return lax.ppermute(x, BOTH, perm)  24.8 us
    ppermute x4, waiting for transfers between devices, swap(): return lax.ppermute(x, 'replica', [(0, 1), (1, 0)])  4.47 us
    pallas_call x3, Pallas kernels, add_groups(): pl.pallas_call(functools.partial(add_kernel, groups, fresh), out_shape=sh...  4.43 us
    pallas_call x1, Pallas kernels, gather_tiles(): pl.pallas_call(functools.partial(gather_kernel, own.shape[0]), out_shape=...  2.13 us
    all_gather x1, blocking collectives, shards(): index = lax.all_gather(index, 'replica', axis=0, tiled=True)  1.98 us
    unnamed x15, local copies, waits for them, and re-layouts  1.69 us
  transfers between devices with their start and end apart: 23, of which 13 were waited for; matrix products, arithmetic and copies ran while one was open for 3% of the time, Pallas kernels for 9%

profile of v6, /device:TPU:0, one launch (start us, length us, event | category | flops | bytes accessed | tf_op | source)
XLA Modules:
  0.0 71.8 jit_solution(14592386544699045247)
XLA Ops:
  1.1 2.6 %collective-permute-start.1 = (bf16[512,256]{1,0:T(8,128)(2,1)}, bf16[512,256]{1,0:T(8,128)(2,1)S(1)}, u32[]{:S(2)}, u32[]{:S(2)}) collective-permute-start(bf16[512,256]{1,0:T(8,128)(2,1)} %param.6), channel_id=1, source_target_pairs={{0,2},{1,5},{2,0},{3,7},{4,6},{5,1},{6,4},{7,3},{8,10},{9,13},{10,... | collective-permute-start | bytes 786440 | tf_op jit(solution)/shard_map/r0/ppermute | solution.py:70
  3.7 1.6 %collective-permute-start = (bf16[512,256]{1,0:T(8,128)(2,1)}, bf16[512,256]{1,0:T(8,128)(2,1)S(1)}, u32[]{:S(2)}, u32[]{:S(2)}) collective-permute-start(bf16[512,256]{1,0:T(8,128)(2,1)} %param.6), channel_id=1, source_target_pairs={{0,8},{1,9},{2,10},{3,11},{4,12},{5,13},{6,14},{7,15},{8,0},{9,1},... | collective-permute-start | bytes 786440 | tf_op jit(solution)/shard_map/z1/ppermute | solution.py:70
  5.3 2.6 %collective-permute-start.2 = (bf16[512,256]{1,0:T(8,128)(2,1)}, bf16[512,256]{1,0:T(8,128)(2,1)S(1)}, u32[]{:S(2)}, u32[]{:S(2)}) collective-permute-start(bf16[512,256]{1,0:T(8,128)(2,1)} %param.6), channel_id=1, source_target_pairs={{0,16},{1,17},{2,18},{3,19},{4,20},{5,21},{6,22},{7,23},{8,24},{9,... | collective-permute-start | bytes 786440 | tf_op jit(solution)/shard_map/z2/ppermute | solution.py:70
  8.9 1.6 %collective-permute-start.8 = (bf16[1024,256]{1,0:T(8,128)(2,1)S(1)}, bf16[1024,256]{1,0:T(8,128)(2,1)S(1)}, u32[]{:S(2)}, u32[]{:S(2)}) collective-permute-start(bf16[1024,256]{1,0:T(8,128)(2,1)S(1)} %constant_dynamic-update-slice_fusion.refs_0_), channel_id=1, source_target_pairs={{0,4},{1,3},{2,6},{3,1},{4,0},{5,7},{6,2},{7,5},{8,12},{9,11},{10,... | collective-permute-start | bytes 1572872 | tf_op jit(solution)/shard_map/q0/ppermute | solution.py:70
  10.5 2.0 %all_gather.3 = s32[256,2]{0,1:T(2,128)S(1)} all-gather(s32[128,2]{0,1:T(2,128)} %param.8), channel_id=1, replica_groups=mesh['section'=16,'replica'=2] {'replica'}, dimensions={0}, use_global_device_ids=true | all-gather | bytes 3072 | tf_op jit(solution)/shard_map/all_gather | solution.py:344
  12.5 5.3 %collective-permute-done = bf16[512,256]{1,0:T(8,128)(2,1)S(1)} collective-permute-done((bf16[512,256]{1,0:T(8,128)(2,1)}, bf16[512,256]{1,0:T(8,128)(2,1)S(1)}, u32[]{:S(2)}, u32[]{:S(2)}) %collective-permute-start) | collective-permute-done | bytes 262176 | tf_op jit(solution)/shard_map/z1/ppermute | solution.py:70
  18.0 3.3 %collective-permute-start.5 = (bf16[512,256]{1,0:T(8,128)(2,1)}, bf16[512,256]{1,0:T(8,128)(2,1)S(1)}, u32[]{:S(2)}, u32[]{:S(2)}) collective-permute-start(bf16[512,256]{1,0:T(8,128)(2,1)} %param.6), channel_id=1, source_target_pairs={{0,24},{1,25},{2,26},{3,27},{4,28},{5,29},{6,30},{7,31},{8,16},{9,... | collective-permute-start | bytes 786440 | tf_op jit(solution)/shard_map/z3/ppermute | solution.py:70
  25.4 4.4 %collective-permute-done.7 = bf16[512,256]{1,0:T(8,128)(2,1)S(1)} collective-permute-done((bf16[512,256]{1,0:T(8,128)(2,1)S(1)}, bf16[512,256]{1,0:T(8,128)(2,1)S(1)}, u32[]{:S(2)}, u32[]{:S(2)}) %collective-permute-start.7) | collective-permute-done | bytes 262176 | tf_op jit(solution)/shard_map/r2/ppermute | solution.py:70
  30.5 1.7 %collective-permute-start.13 = (bf16[512,256]{1,0:T(8,128)(2,1)S(1)}, bf16[512,256]{1,0:T(8,128)(2,1)S(1)}, u32[]{:S(2)}, u32[]{:S(2)}) collective-permute-start(bf16[512,256]{1,0:T(8,128)(2,1)S(1)} %collective-permute-done.5), channel_id=1, source_target_pairs={{0,4},{1,3},{2,6},{3,1},{4,0},{5,7},{6,2},{7,5},{8,12},{9,11},{10,... | collective-permute-start | bytes 786440 | tf_op jit(solution)/shard_map/q3a/ppermute | solution.py:70
  32.2 2.1 %gather_tiles.1.tiles = bf16[274,128,128]{2,1,0:T(8,128)(2,1)S(1)} custom-call(s32[274]{0:T(512)} %broadcast_add_fusion.entries, s32[10]{0:T(128)} %copy-done.3, bf16[128,128,128]{2,1,0:T(8,128)(2,1)} %own.1, bf16[128,128,128]{2,1,0:T(8,128)(2,1)} %collective-permute-done.3.other), custom_call_target="tpu_custom_call" | custom-call | bytes 1024 | tf_op jit(solution)/shard_map/gather_tiles/pallas_call | solution.py:183
  35.3 2.0 %add_a.1.refs_2_ = f32[9,128,256]{2,1,0:T(8,128)S(1)} custom-call(s32[274]{0:T(512)S(1)} %copy-done.2, s32[10]{0:T(128)S(1)} %copy-done.4, bf16[274,128,128]{2,1,0:T(8,128)(2,1)S(1)} %gather_tiles.1.tiles, bf16[1024,256]{1,0:T(8,128)(2,1)S(1)} %constant_dynamic-update-slice_fusion.refs_0_, bf16[1024,256]{1,0:T(8,128)(2,1)S(1)} %collective-permute-done.8.refs_1_, ...), custom_call_target="tpu_custom_call" | custom-call | flops 4294967296 | bytes 4194304 | tf_op jit(solution)/shard_map/add_a/pallas_call | solution.py:241
  37.2 1.5 %collective-permute-done.9 = bf16[512,256]{1,0:T(8,128)(2,1)S(1)} collective-permute-done((bf16[512,256]{1,0:T(8,128)(2,1)S(1)}, bf16[512,256]{1,0:T(8,128)(2,1)S(1)}, u32[]{:S(2)}, u32[]{:S(2)}) %collective-permute-start.9) | collective-permute-done | bytes 262176 | tf_op jit(solution)/shard_map/r3/ppermute | solution.py:70
  38.9 1.2 %add_b.1.refs_3_ = f32[9,128,256]{2,1,0:T(8,128)S(1)} custom-call(s32[274]{0:T(512)S(1)} %copy-done.2, s32[10]{0:T(128)S(1)} %copy-done.5, bf16[274,128,128]{2,1,0:T(8,128)(2,1)S(1)} %gather_tiles.1.tiles, bf16[1024,256]{1,0:T(8,128)(2,1)S(1)} %collective-permute-done.12.refs_0_, ...), custom_call_target="tpu_custom_call", output_to_operand_aliasing={{}: (5, {})} | custom-call | flops 4294967296 | bytes 4194304 | tf_op jit(solution)/shard_map/add_b/pallas_call | solution.py:241
  40.1 1.9 %collective-permute-start.10 = (bf16[512,256]{1,0:T(8,128)(2,1)S(1)}, bf16[512,256]{1,0:T(8,128)(2,1)S(1)}, u32[]{:S(2)}, u32[]{:S(2)}) collective-permute-start(bf16[512,256]{1,0:T(8,128)(2,1)S(1)} %collective-permute-done.9), channel_id=1, source_target_pairs={{0,4},{1,3},{2,6},{3,1},{4,0},{5,7},{6,2},{7,5},{8,12},{9,11},{10,... | collective-permute-start | bytes 786440 | tf_op jit(solution)/shard_map/q3b/ppermute | solution.py:70
  43.3 3.2 %collective-permute-done.10.refs_0_ = bf16[512,256]{1,0:T(8,128)(2,1)S(1)} collective-permute-done((bf16[512,256]{1,0:T(8,128)(2,1)S(1)}, bf16[512,256]{1,0:T(8,128)(2,1)S(1)}, u32[]{:S(2)}, u32[]{:S(2)}) %collective-permute-start.10) | collective-permute-done | bytes 262176 | tf_op jit(solution)/shard_map/q3b/ppermute | solution.py:70
  47.7 1.9 %collective-permute-done.14.theirs = f32[4,128,256]{2,1,0:T(8,128)S(1)} collective-permute-done((f32[4,128,256]{2,1,0:T(8,128)S(1)}, f32[4,128,256]{2,1,0:T(8,128)S(1)}, u32[]{:S(2)}, u32[]{:S(2)}) %collective-permute-start.14) | collective-permute-done | bytes 524320 | tf_op jit(solution)/shard_map/rows/ppermute | solution.py:75
  50.8 1.2 %collective-permute-done.15 = f32[136,256]{1,0:T(8,128)S(1)} collective-permute-done((f32[136,256]{1,0:T(8,128)S(1)}, f32[136,256]{1,0:T(8,128)S(1)}, u32[]{:S(2)}, u32[]{:S(2)}) %collective-permute-start.15) | collective-permute-done | bytes 139296 | tf_op jit(solution)/shard_map/halves/ppermute | solution.py:75
  52.1 3.1 %collective-permute-start.16 = (bf16[136,256]{1,0:T(8,128)(2,1)S(1)}, bf16[136,256]{1,0:T(8,128)(2,1)S(1)}, u32[]{:S(2)}, u32[]{:S(2)}) collective-permute-start(bf16[136,256]{1,0:T(8,128)(2,1)S(1)} %add_convert_fusion), channel_id=1, source_target_pairs={{0,6},{1,7},{2,4},{3,5},{4,2},{5,3},{6,0},{7,1},{8,14},{9,15},{10,... | collective-permute-start | bytes 208904 | tf_op jit(solution)/shard_map/sumd/ppermute | solution.py:70
  55.8 1.9 %collective-permute-done.16 = bf16[136,256]{1,0:T(8,128)(2,1)S(1)} collective-permute-done((bf16[136,256]{1,0:T(8,128)(2,1)S(1)}, bf16[136,256]{1,0:T(8,128)(2,1)S(1)}, u32[]{:S(2)}, u32[]{:S(2)}) %collective-permute-start.16) | collective-permute-done | bytes 69664 | tf_op jit(solution)/shard_map/sumd/ppermute | solution.py:70
  57.7 1.8 %collective-permute-done.17 = bf16[136,256]{1,0:T(8,128)(2,1)S(1)} collective-permute-done((bf16[136,256]{1,0:T(8,128)(2,1)S(1)}, bf16[136,256]{1,0:T(8,128)(2,1)S(1)}, u32[]{:S(2)}, u32[]{:S(2)}) %collective-permute-start.17) | collective-permute-done | bytes 69664 | tf_op jit(solution)/shard_map/sum1/ppermute | solution.py:70
  59.6 1.8 %collective-permute-start.19 = (bf16[136,256]{1,0:T(8,128)(2,1)S(1)}, bf16[136,256]{1,0:T(8,128)(2,1)S(1)}, u32[]{:S(2)}, u32[]{:S(2)}) collective-permute-start(bf16[136,256]{1,0:T(8,128)(2,1)S(1)} %get-tuple-element.49), channel_id=1, source_target_pairs={{0,8},{1,9},{2,10},{3,11},{4,12},{5,13},{6,14},{7,15},{8,0},{9,1},... | collective-permute-start | bytes 208904 | tf_op jit(solution)/shard_map/sum3/ppermute | solution.py:70
  61.4 1.5 %collective-permute-start.20 = (bf16[136,256]{1,0:T(8,128)(2,1)S(1)}, bf16[136,256]{1,0:T(8,128)(2,1)S(1)}, u32[]{:S(2)}, u32[]{:S(2)}) collective-permute-start(bf16[136,256]{1,0:T(8,128)(2,1)S(1)} %get-tuple-element.49), channel_id=1, source_target_pairs={{0,16},{1,17},{2,18},{3,19},{4,20},{5,21},{6,22},{7,23},{8,24},{9,... | collective-permute-start | bytes 208904 | tf_op jit(solution)/shard_map/sum4/ppermute | solution.py:70
  64.0 5.5 %collective-permute-done.20 = bf16[136,256]{1,0:T(8,128)(2,1)S(1)} collective-permute-done((bf16[136,256]{1,0:T(8,128)(2,1)S(1)}, bf16[136,256]{1,0:T(8,128)(2,1)S(1)}, u32[]{:S(2)}, u32[]{:S(2)}) %collective-permute-start.20) | collective-permute-done | bytes 69664 | tf_op jit(solution)/shard_map/sum4/ppermute | solution.py:70
  69.7 1.3 %collective-permute-done.22.rest = f32[136,256]{1,0:T(8,128)S(1)} collective-permute-done((f32[136,256]{1,0:T(8,128)S(1)}, f32[136,256]{1,0:T(8,128)S(1)}, u32[]{:S(2)}, u32[]{:S(2)}) %collective-permute-start.22) | collective-permute-done | bytes 139296 | tf_op jit(solution)/shard_map/back/ppermute | solution.py:75
  (65 shorter events, 13.9 us)
Async XLA Ops:
  0.6 21.4 %collective-permute-start.3 = (bf16[128,128,128]{2,1,0:T(8,128)(2,1)}, bf16[128,128,128]{2,1,0:T(8,128)(2,1)}, u32[]{:S(2)}, u32[]{:S(2)}) collective-permute-start(bf16[128,128,128]{2,1,0:T(8,128)(2,1)} %own.1), channel_id=1, source_target_pairs={{0,1},{1,0},{2,3},{3,2},{4,5},{5,4},{6,7},{7,6},{8,9},{9,8},{10,11... | collective-permute-start | bytes 12582920 | tf_op jit(solution)/shard_map/tiles/ppermute | solution.py:75
  1.1 7.7 %collective-permute-start.1 = (bf16[512,256]{1,0:T(8,128)(2,1)}, bf16[512,256]{1,0:T(8,128)(2,1)S(1)}, u32[]{:S(2)}, u32[]{:S(2)}) collective-permute-start(bf16[512,256]{1,0:T(8,128)(2,1)} %param.6), channel_id=1, source_target_pairs={{0,2},{1,5},{2,0},{3,7},{4,6},{5,1},{6,4},{7,3},{8,10},{9,13},{10,... | collective-permute-start | bytes 786440 | tf_op jit(solution)/shard_map/r0/ppermute | solution.py:70
  3.7 14.1 %collective-permute-start = (bf16[512,256]{1,0:T(8,128)(2,1)}, bf16[512,256]{1,0:T(8,128)(2,1)S(1)}, u32[]{:S(2)}, u32[]{:S(2)}) collective-permute-start(bf16[512,256]{1,0:T(8,128)(2,1)} %param.6), channel_id=1, source_target_pairs={{0,8},{1,9},{2,10},{3,11},{4,12},{5,13},{6,14},{7,15},{8,0},{9,1},... | collective-permute-start | bytes 786440 | tf_op jit(solution)/shard_map/z1/ppermute | solution.py:70
  5.3 16.8 %collective-permute-start.2 = (bf16[512,256]{1,0:T(8,128)(2,1)}, bf16[512,256]{1,0:T(8,128)(2,1)S(1)}, u32[]{:S(2)}, u32[]{:S(2)}) collective-permute-start(bf16[512,256]{1,0:T(8,128)(2,1)} %param.6), channel_id=1, source_target_pairs={{0,16},{1,17},{2,18},{3,19},{4,20},{5,21},{6,22},{7,23},{8,24},{9,... | collective-permute-start | bytes 786440 | tf_op jit(solution)/shard_map/z2/ppermute | solution.py:70
  8.9 16.4 %collective-permute-start.8 = (bf16[1024,256]{1,0:T(8,128)(2,1)S(1)}, bf16[1024,256]{1,0:T(8,128)(2,1)S(1)}, u32[]{:S(2)}, u32[]{:S(2)}) collective-permute-start(bf16[1024,256]{1,0:T(8,128)(2,1)S(1)} %constant_dynamic-update-slice_fusion.refs_0_), channel_id=1, source_target_pairs={{0,4},{1,3},{2,6},{3,1},{4,0},{5,7},{6,2},{7,5},{8,12},{9,11},{10,... | collective-permute-start | bytes 1572872 | tf_op jit(solution)/shard_map/q0/ppermute | solution.py:70
  17.8 7.5 %collective-permute-start.6 = (bf16[512,256]{1,0:T(8,128)(2,1)S(1)}, bf16[512,256]{1,0:T(8,128)(2,1)S(1)}, u32[]{:S(2)}, u32[]{:S(2)}) collective-permute-start(bf16[512,256]{1,0:T(8,128)(2,1)S(1)} %collective-permute-done), channel_id=1, source_target_pairs={{0,2},{1,5},{2,0},{3,7},{4,6},{5,1},{6,4},{7,3},{8,10},{9,13},{10,... | collective-permute-start | bytes 786440 | tf_op jit(solution)/shard_map/r1/ppermute | solution.py:70
  18.0 11.8 %collective-permute-start.5 = (bf16[512,256]{1,0:T(8,128)(2,1)}, bf16[512,256]{1,0:T(8,128)(2,1)S(1)}, u32[]{:S(2)}, u32[]{:S(2)}) collective-permute-start(bf16[512,256]{1,0:T(8,128)(2,1)} %param.6), channel_id=1, source_target_pairs={{0,24},{1,25},{2,26},{3,27},{4,28},{5,29},{6,30},{7,31},{8,16},{9,... | collective-permute-start | bytes 786440 | tf_op jit(solution)/shard_map/z3/ppermute | solution.py:70
  21.6 10.6 %copy-start.3 = (s32[10]{0:T(128)}, s32[10]{0:T(128)S(1)}, u32[]{:S(2)}) copy-start(s32[10]{0:T(128)S(1)} %select_reduce_fusion.2.starts) | copy-start | bytes 124
  22.1 10.2 %collective-permute-start.4 = (bf16[512,256]{1,0:T(8,128)(2,1)S(1)}, bf16[512,256]{1,0:T(8,128)(2,1)S(1)}, u32[]{:S(2)}, u32[]{:S(2)}) collective-permute-start(bf16[512,256]{1,0:T(8,128)(2,1)S(1)} %collective-permute-done.2), channel_id=1, source_target_pairs={{0,4},{1,3},{2,6},{3,1},{4,0},{5,7},{6,2},{7,5},{8,12},{9,11},{10,... | collective-permute-start | bytes 786440 | tf_op jit(solution)/shard_map/q2a/ppermute | solution.py:70
  23.1 6.7 %collective-permute-start.7 = (bf16[512,256]{1,0:T(8,128)(2,1)S(1)}, bf16[512,256]{1,0:T(8,128)(2,1)S(1)}, u32[]{:S(2)}, u32[]{:S(2)}) collective-permute-start(bf16[512,256]{1,0:T(8,128)(2,1)S(1)} %collective-permute-done.2), channel_id=1, source_target_pairs={{0,2},{1,5},{2,0},{3,7},{4,6},{5,1},{6,4},{7,3},{8,10},{9,13},{10,... | collective-permute-start | bytes 786440 | tf_op jit(solution)/shard_map/r2/ppermute | solution.py:70
  25.3 13.5 %collective-permute-start.12 = (bf16[1024,256]{1,0:T(8,128)(2,1)S(1)}, bf16[1024,256]{1,0:T(8,128)(2,1)S(1)}, u32[]{:S(2)}, u32[]{:S(2)}) collective-permute-start(bf16[1024,256]{1,0:T(8,128)(2,1)S(1)} %collective-permute-done.8.refs_1_), channel_id=1, source_target_pairs={{0,8},{1,9},{2,10},{3,11},{4,12},{5,13},{6,14},{7,15},{8,0},{9,1},... | collective-permute-start | bytes 1572872 | tf_op jit(solution)/shard_map/q1/ppermute | solution.py:70
  29.9 8.9 %collective-permute-start.9 = (bf16[512,256]{1,0:T(8,128)(2,1)S(1)}, bf16[512,256]{1,0:T(8,128)(2,1)S(1)}, u32[]{:S(2)}, u32[]{:S(2)}) collective-permute-start(bf16[512,256]{1,0:T(8,128)(2,1)S(1)} %collective-permute-done.5), channel_id=1, source_target_pairs={{0,2},{1,5},{2,0},{3,7},{4,6},{5,1},{6,4},{7,3},{8,10},{9,13},{10,... | collective-permute-start | bytes 786440 | tf_op jit(solution)/shard_map/r3/ppermute | solution.py:70
  30.5 11.6 %collective-permute-start.13 = (bf16[512,256]{1,0:T(8,128)(2,1)S(1)}, bf16[512,256]{1,0:T(8,128)(2,1)S(1)}, u32[]{:S(2)}, u32[]{:S(2)}) collective-permute-start(bf16[512,256]{1,0:T(8,128)(2,1)S(1)} %collective-permute-done.5), channel_id=1, source_target_pairs={{0,4},{1,3},{2,6},{3,1},{4,0},{5,7},{6,2},{7,5},{8,12},{9,11},{10,... | collective-permute-start | bytes 786440 | tf_op jit(solution)/shard_map/q3a/ppermute | solution.py:70
  34.4 7.7 %collective-permute-start.11 = (bf16[512,256]{1,0:T(8,128)(2,1)S(1)}, bf16[512,256]{1,0:T(8,128)(2,1)S(1)}, u32[]{:S(2)}, u32[]{:S(2)}) collective-permute-start(bf16[512,256]{1,0:T(8,128)(2,1)S(1)} %collective-permute-done.7), channel_id=1, source_target_pairs={{0,4},{1,3},{2,6},{3,1},{4,0},{5,7},{6,2},{7,5},{8,12},{9,11},{10,... | collective-permute-start | bytes 786440 | tf_op jit(solution)/shard_map/q2b/ppermute | solution.py:70
  40.1 6.4 %collective-permute-start.10 = (bf16[512,256]{1,0:T(8,128)(2,1)S(1)}, bf16[512,256]{1,0:T(8,128)(2,1)S(1)}, u32[]{:S(2)}, u32[]{:S(2)}) collective-permute-start(bf16[512,256]{1,0:T(8,128)(2,1)S(1)} %collective-permute-done.9), channel_id=1, source_target_pairs={{0,4},{1,3},{2,6},{3,1},{4,0},{5,7},{6,2},{7,5},{8,12},{9,11},{10,... | collective-permute-start | bytes 786440 | tf_op jit(solution)/shard_map/q3b/ppermute | solution.py:70
  47.6 2.0 %collective-permute-start.14 = (f32[4,128,256]{2,1,0:T(8,128)S(1)}, f32[4,128,256]{2,1,0:T(8,128)S(1)}, u32[]{:S(2)}, u32[]{:S(2)}) collective-permute-start(f32[4,128,256]{2,1,0:T(8,128)S(1)} %get-tuple-element.43), channel_id=1, source_target_pairs={{0,1},{1,0},{2,3},{3,2},{4,5},{5,4},{6,7},{7,6},{8,9},{9,8},{10,11... | collective-permute-start | bytes 1572872 | tf_op jit(solution)/shard_map/rows/ppermute | solution.py:75
  50.7 1.4 %collective-permute-start.15 = (f32[136,256]{1,0:T(8,128)S(1)}, f32[136,256]{1,0:T(8,128)S(1)}, u32[]{:S(2)}, u32[]{:S(2)}) collective-permute-start(f32[136,256]{1,0:T(8,128)S(1)} %get-tuple-element.46), channel_id=1, source_target_pairs={{0,1},{1,0},{2,3},{3,2},{4,5},{5,4},{6,7},{7,6},{8,9},{9,8},{10,11... | collective-permute-start | bytes 417800 | tf_op jit(solution)/shard_map/halves/ppermute | solution.py:75
  52.1 5.6 %collective-permute-start.16 = (bf16[136,256]{1,0:T(8,128)(2,1)S(1)}, bf16[136,256]{1,0:T(8,128)(2,1)S(1)}, u32[]{:S(2)}, u32[]{:S(2)}) collective-permute-start(bf16[136,256]{1,0:T(8,128)(2,1)S(1)} %add_convert_fusion), channel_id=1, source_target_pairs={{0,6},{1,7},{2,4},{3,5},{4,2},{5,3},{6,0},{7,1},{8,14},{9,15},{10,... | collective-permute-start | bytes 208904 | tf_op jit(solution)/shard_map/sumd/ppermute | solution.py:70
  55.2 4.3 %collective-permute-start.17 = (bf16[136,256]{1,0:T(8,128)(2,1)S(1)}, bf16[136,256]{1,0:T(8,128)(2,1)S(1)}, u32[]{:S(2)}, u32[]{:S(2)}) collective-permute-start(bf16[136,256]{1,0:T(8,128)(2,1)S(1)} %add_convert_fusion), channel_id=1, source_target_pairs={{0,2},{1,5},{2,0},{3,7},{4,6},{5,1},{6,4},{7,3},{8,10},{9,13},{10,... | collective-permute-start | bytes 208904 | tf_op jit(solution)/shard_map/sum1/ppermute | solution.py:70
  55.2 4.3 %collective-permute-start.18 = (bf16[136,256]{1,0:T(8,128)(2,1)S(1)}, bf16[136,256]{1,0:T(8,128)(2,1)S(1)}, u32[]{:S(2)}, u32[]{:S(2)}) collective-permute-start(bf16[136,256]{1,0:T(8,128)(2,1)S(1)} %add_convert_fusion), channel_id=1, source_target_pairs={{0,4},{1,3},{2,6},{3,1},{4,0},{5,7},{6,2},{7,5},{8,12},{9,11},{10,... | collective-permute-start | bytes 208904 | tf_op jit(solution)/shard_map/sum2/ppermute | solution.py:70
  59.6 4.5 %collective-permute-start.19 = (bf16[136,256]{1,0:T(8,128)(2,1)S(1)}, bf16[136,256]{1,0:T(8,128)(2,1)S(1)}, u32[]{:S(2)}, u32[]{:S(2)}) collective-permute-start(bf16[136,256]{1,0:T(8,128)(2,1)S(1)} %get-tuple-element.49), channel_id=1, source_target_pairs={{0,8},{1,9},{2,10},{3,11},{4,12},{5,13},{6,14},{7,15},{8,0},{9,1},... | collective-permute-start | bytes 208904 | tf_op jit(solution)/shard_map/sum3/ppermute | solution.py:70
  61.4 8.2 %collective-permute-start.20 = (bf16[136,256]{1,0:T(8,128)(2,1)S(1)}, bf16[136,256]{1,0:T(8,128)(2,1)S(1)}, u32[]{:S(2)}, u32[]{:S(2)}) collective-permute-start(bf16[136,256]{1,0:T(8,128)(2,1)S(1)} %get-tuple-element.49), channel_id=1, source_target_pairs={{0,16},{1,17},{2,18},{3,19},{4,20},{5,21},{6,22},{7,23},{8,24},{9,... | collective-permute-start | bytes 208904 | tf_op jit(solution)/shard_map/sum4/ppermute | solution.py:70
  62.9 6.7 %collective-permute-start.21 = (bf16[136,256]{1,0:T(8,128)(2,1)S(1)}, bf16[136,256]{1,0:T(8,128)(2,1)S(1)}, u32[]{:S(2)}, u32[]{:S(2)}) collective-permute-start(bf16[136,256]{1,0:T(8,128)(2,1)S(1)} %get-tuple-element.49), channel_id=1, source_target_pairs={{0,24},{1,25},{2,26},{3,27},{4,28},{5,29},{6,30},{7,31},{8,16},{9,... | collective-permute-start | bytes 208904 | tf_op jit(solution)/shard_map/sum5/ppermute | solution.py:70
  69.6 1.4 %collective-permute-start.22 = (f32[136,256]{1,0:T(8,128)S(1)}, f32[136,256]{1,0:T(8,128)S(1)}, u32[]{:S(2)}, u32[]{:S(2)}) collective-permute-start(f32[136,256]{1,0:T(8,128)S(1)} %add_add_fusion.part), channel_id=1, source_target_pairs={{0,1},{1,0},{2,3},{3,2},{4,5},{5,4},{6,7},{7,6},{8,9},{9,8},{10,11... | collective-permute-start | bytes 417800 | tf_op jit(solution)/shard_map/back/ppermute | solution.py:75
  (6 other events, 27.8 us)
